TPU v7x, 512 devices: a whole 4x8x8 slice. The times are simulated.
512 devices in a mesh: ctx: 32 (over x, z_hi, core), tp: 16 (over y, z_lo).
Axes of the slice: x: 4, y: 8, z: 8 (z_hi: 4, z_lo: 2; z = z_hi * 2 + z_lo), core: 2. Of those that a mesh axis runs over, the one named last changes fastest.
Arguments:
- queries: bfloat16 [8192, 2048], P('ctx', 'tp'), may hold values from -24 to 24
- key_heads: bfloat16 [8192, 4, 128], P('ctx'), may hold values from -6 to 6
- head_values: bfloat16 [8192, 4, 128], P('ctx'), may hold values from -6 to 6
- hidden: bfloat16 [8192, 4096], P('ctx'), may hold values from -0.59765625 to 0.59765625
- out_proj: bfloat16 [2048, 4096], P('tp'), may hold values from -0.125 to 0.125
- norm_gain: float32 [4096], replicated, may hold values from 0.25 to 1.75
- x_proj: bfloat16 [4096, 4096], P('ctx', 'tp'), may hold values from -0.046875 to 0.046875
- bc_proj: bfloat16 [4096, 4, 256], P('ctx'), may hold values from -0.09375 to 0.09375
- dt_proj: bfloat16 [4096, 64], P('ctx', 'tp'), may hold values from -0.09375 to 0.09375
- dt_bias: float32 [64], P('tp'), may hold values from -12 to 0
- decay_log: float32 [64], P('tp'), may hold values from -10 to 3
- skip_gain: float32 [64], P('tp'), may hold values from 0.5 to 1.5
Outputs:
- residual_out: bfloat16 [8192, 4096], P('ctx', 'tp')
- mamba_out: bfloat16 [8192, 4096], P('ctx', 'tp')
All inputs are finite; a program needn't handle non-finite values.
Results may differ from a plain program's by a relative error of at most 0.034.
Values may be sent and summed in bfloat16 or wider, within the bound.
No kernel may reach another device: no remote copies, remote signals or barrier semaphores. Data moves between devices by JAX's collectives and lax.ppermute only.
A program may use at most 64 MiB of HBM per device.

v0:
```python
import math

import jax
import jax.numpy as jnp
from jax import lax
from jax.sharding import PartitionSpec as P


def prefix(value, axis, join, neutral, backward):
    count, mine = (lax.axis_size(axis), lax.axis_index(axis))
    pieces = jax.tree.map(lambda part: lax.all_gather(part, axis), value)
    if backward:
        pieces = jax.tree.map(lambda part: part[::-1], pieces)
        mine = count - 1 - mine
    so_far = jax.tree.map(
        lambda part, zero: jnp.full_like(part, 0) + jnp.asarray(zero, part.dtype), value, neutral
    )

    def lap(position, so_far):
        longer = join(so_far, jax.tree.map(lambda part: part[position], pieces))
        return jax.tree.map(lambda new, old: jnp.where(position < mine, new, old), longer, so_far)

    return lax.fori_loop(0, count - 1, lap, so_far)


def chain(earlier, later):
    return (earlier[0] * later[0], later[0][..., None, None] * earlier[1] + later[1])


def block_positions(rows, tok_dev, n_ctx):
    half = tok_dev // 2
    device = rows // tok_dev
    within = rows % tok_dev
    block = jnp.where(within < half, device, 2 * n_ctx - 1 - device)
    return block * half + within % half


def split_product(form, wide, narrow):
    upper = wide.astype(jnp.bfloat16)
    lower = (wide - upper.astype(jnp.float32)).astype(jnp.bfloat16)
    first_term = jnp.einsum(form, upper, narrow, preferred_element_type=jnp.float32)
    return first_term + jnp.einsum(form, lower, narrow, preferred_element_type=jnp.float32)


def body(
    queries,
    key_heads,
    head_values,
    hidden,
    out_proj,
    norm_gain,
    x_proj,
    bc_proj,
    dt_proj,
    dt_bias,
    decay_log,
    skip_gain,
):
    tok_dev = queries.shape[0]
    half = tok_dev // 2
    n_ctx = lax.axis_size("ctx")
    n_tp = lax.axis_size("tp")
    ctx_index = lax.axis_index("ctx")
    tp_index = lax.axis_index("tp")
    head_dim = key_heads.shape[2]
    kv_total = key_heads.shape[1]
    q_local = queries.shape[1] // head_dim
    group = q_local * n_tp // kv_total
    kv_local = max(1, q_local // group)
    per_kv = q_local // kv_local
    kv_start = tp_index * q_local // group
    keys_mine = lax.dynamic_slice_in_dim(key_heads, kv_start, kv_local, 1)
    values_mine = lax.dynamic_slice_in_dim(head_values, kv_start, kv_local, 1)
    query_pos = block_positions(
        ctx_index * tok_dev + jnp.arange(tok_dev, dtype=jnp.int32), tok_dev, n_ctx
    )
    shaped_q = queries.reshape(tok_dev, kv_local, per_kv, head_dim)
    root_dim = math.sqrt(head_dim)
    start_max = jnp.full((kv_local, per_kv, tok_dev), -1e30, jnp.float32)
    run_max = start_max
    key_piece = lax.all_gather(keys_mine, "ctx", axis=0, tiled=True)
    value_piece = lax.all_gather(values_mine, "ctx", axis=0, tiled=True)
    count = key_piece.shape[0]
    key_pos = block_positions(jnp.arange(count, dtype=jnp.int32), tok_dev, n_ctx)
    scores = (
        jnp.einsum("qgjd,kgd->gjqk", shaped_q, key_piece, preferred_element_type=jnp.float32)
        / root_dim
    )
    allowed = key_pos[None, :] <= query_pos[:, None]
    piece_max = jnp.max(jnp.where(allowed, scores, -1e30), axis=-1)
    new_max = jnp.maximum(run_max, piece_max)
    weights = jnp.where(allowed, jnp.exp(scores - new_max[..., None]), 0.0)
    run_sum = jnp.sum(weights, axis=-1)
    update = jnp.einsum(
        "gjqk,kgd->gjqd",
        weights.astype(jnp.bfloat16),
        value_piece,
        preferred_element_type=jnp.float32,
    )
    accum = update
    run_max, run_sum, accum = (new_max, run_sum, accum)
    attended = (
        jnp.transpose(accum / run_sum[..., None], (2, 0, 1, 3))
        .reshape(tok_dev, q_local * head_dim)
        .astype(jnp.bfloat16)
    )
    head_part = jnp.dot(attended, out_proj, preferred_element_type=jnp.float32)
    slice_width = hidden.shape[1] // n_tp
    attention_sum = lax.psum(head_part.astype(jnp.bfloat16), "tp").astype(jnp.float32)
    residual = (hidden.astype(jnp.float32) + attention_sum).astype(jnp.bfloat16)
    residual_out = lax.dynamic_slice_in_dim(residual, tp_index * slice_width, slice_width, 1)
    as_float = residual.astype(jnp.float32)
    mean_square = jnp.mean(as_float * as_float, axis=-1, keepdims=True)
    normed = (as_float * lax.rsqrt(mean_square + 1e-05) * norm_gain).astype(jnp.bfloat16)
    m_local = skip_gain.shape[0]
    state_size = bc_proj.shape[2] // 2
    groups_all = bc_proj.shape[1]
    per_group = m_local * n_tp // groups_all
    g_local = max(1, m_local // per_group)
    heads_each = m_local // g_local
    g_start = tp_index * m_local // per_group
    head_width = x_proj.shape[1] // m_local
    bc_mine = lax.dynamic_slice_in_dim(bc_proj, g_start, g_local, 1).reshape(
        bc_proj.shape[0], g_local * 2 * state_size
    )
    sum_x = jnp.dot(
        normed,
        lax.all_gather(x_proj, "ctx", axis=0, tiled=True),
        preferred_element_type=jnp.float32,
    )
    sum_bc = jnp.dot(
        normed,
        lax.all_gather(bc_mine, "ctx", axis=0, tiled=True),
        preferred_element_type=jnp.float32,
    )
    sum_dt = jnp.dot(
        normed,
        lax.all_gather(dt_proj, "ctx", axis=0, tiled=True),
        preferred_element_type=jnp.float32,
    )
    inputs_low = sum_x.astype(jnp.bfloat16).reshape(2, half, g_local, heads_each, head_width)
    inputs = inputs_low.astype(jnp.float32)
    bc_round = sum_bc.astype(jnp.bfloat16).reshape(2, half, g_local, 2 * state_size)
    b_low = bc_round[..., :state_size]
    c_low = bc_round[..., state_size:]
    steps = jax.nn.softplus(sum_dt + dt_bias).reshape(2, half, g_local, heads_each)
    rates = -jnp.exp(decay_log).reshape(g_local, heads_each)
    cumul = jnp.transpose(jnp.cumsum(steps * rates, axis=1), (0, 2, 3, 1))
    step_rows = jnp.transpose(steps, (0, 2, 3, 1))
    gram = jnp.einsum("ckgn,csgn->cgks", c_low, b_low, preferred_element_type=jnp.float32)
    places = jnp.arange(half, dtype=jnp.int32)
    causal = places[None, :] <= places[:, None]
    gaps = cumul[..., :, None] - cumul[..., None, :]
    decay = jnp.where(causal, jnp.exp(jnp.where(causal, gaps, 0.0)), 0.0)
    mixing = gram[:, :, None] * decay * step_rows[..., None, :]
    inner = split_product("cgjks,csgjp->ckgjp", mixing, inputs_low)
    last = cumul[..., -1]
    tail = jnp.exp(last[..., None] - cumul) * step_rows
    weighted = jnp.transpose(tail, (0, 3, 1, 2))[..., None] * inputs
    block_state = split_product("csgjp,csgn->cgjpn", weighted, b_low)
    block_decay = jnp.exp(last)
    first = (block_decay[0], block_state[0])
    second = (block_decay[1], block_state[1])
    unit = (jnp.ones_like(first[0]), jnp.zeros_like(first[1]))
    before = prefix(first, "ctx", chain, unit, False)
    last_device = ctx_index == n_ctx - 1
    through = chain(before, first)
    joined = chain(through, second)
    sent = (
        jnp.where(last_device, joined[0], second[0]),
        jnp.where(last_device, joined[1], second[1]),
    )
    after = prefix(sent, "ctx", chain, unit, True)
    second_in = jnp.where(last_device, through[1], after[1])
    entering = jnp.stack([before[1], second_in])
    carried = jnp.transpose(jnp.exp(cumul), (0, 3, 1, 2))[..., None] * split_product(
        "cgjpn,ckgn->ckgjp", entering, c_low
    )
    output = inner + carried + skip_gain.reshape(g_local, heads_each)[:, :, None] * inputs
    mamba_out = output.reshape(tok_dev, m_local * head_width).astype(jnp.bfloat16)
    return (residual_out, mamba_out)


def solution(mesh):
    placed = (
        P("ctx", "tp"),
        P("ctx", None, None),
        P("ctx", None, None),
        P("ctx", None),
        P("tp", None),
        P(),
        P("ctx", "tp"),
        P("ctx", None, None),
        P("ctx", "tp"),
        P("tp"),
        P("tp"),
        P("tp"),
    )
    return jax.shard_map(
        body,
        mesh=mesh,
        in_specs=placed,
        out_specs=(P("ctx", "tp"), P("ctx", "tp")),
        check_vma=False,
    )
```

profile of v0, /device:TPU:1, one launch (start us, length us, event | category | flops | bytes accessed | tf_op | source)
XLA Modules:
  0.0 671.6 jit_solution(12906673132283992635)
XLA Ops:
  7.2 1.2 constant_dynamic-slice_fusion.4
  9.1 1.1 constant_dynamic-slice_fusion.3
  11.0 66.9 %all-gather.13.cloned.1.call-done = bf16[8192,1,128]{2,0,1:T(8,128)(2,1)} async-done(((bf16[256,1,128]{2,0,1:T(8,128)(2,1)}), bf16[8192,1,128]{2,0,1:T(8,128)(2,1)}) %all-gather.13.cloned.1.call-update) | async-done | bytes 2097168 | tf_op jit(solution)/shard_map/all_gather | solution.py:81
  77.9 5.7 fusion.4
  83.6 3.3 copy-done.1
  86.9 3.7 fusion.5
  90.7 48.6 %all-gather.15.cloned.1.call-done = bf16[8192,1,128]{2,0,1:T(8,128)(2,1)} async-done(((bf16[256,1,128]{2,0,1:T(8,128)(2,1)}), bf16[8192,1,128]{2,0,1:T(8,128)(2,1)}) %all-gather.15.cloned.1.call-update) | async-done | bytes 2097168 | tf_op jit(solution)/shard_map/all_gather | solution.py:82
  139.3 8.7 %convolution_convert_fusion = bf16[256,4096]{1,0:T(8,128)(2,1)} fusion(bf16[128,4096]{1,0:T(8,128)(2,1)S(1)} %copy-done, bf16[8192,1,128]{2,0,1:T(8,128)(2,1)} %all-gather.15.cloned.1.call-done, f32[1,1,256,8192]{2,3,1,0:T(8,128)} %copy-done.1, f32[256]{0:T(256)S(1)} %broadcast_maximum_fusion, s32[256]{0:T(256)S(1)} %fusion.88, s32[8192]{0:T(1024)S(1)} %fusion.83, ...), kind=kOutput, calls=%fused_computation.18 | convolution fusion | flops 814809088 | bytes 13667328 | tf_op jit(solution)/shard_map/dot_general | solution.py:107
  149.5 43.0 %all_gather.37 = bf16[4096,4]{0,1:T(4,128)(2,1)S(1)} all-gather(bf16[128,4]{0,1:T(4,128)(2,1)S(1)} %copy-done.14), channel_id=1, replica_groups=mesh['ctx'=32,'tp'=16] {'ctx'}, dimensions={0}, use_global_device_ids=true | all-gather | bytes 33792 | tf_op jit(solution)/shard_map/all_gather | solution.py:138
  192.5 94.5 %all-reduce.2.cloned.1.call-done = bf16[256,4096]{1,0:T(8,128)(2,1)} async-done(((bf16[256,4096]{1,0:T(8,128)(2,1)}), bf16[256,4096]{1,0:T(8,128)(2,1)}) %all-reduce.2.cloned.1.call-update) | async-done | bytes 2097168 | tf_op jit(solution)/shard_map/psum | solution.py:109
  287.0 3.2 fusion.7
  290.2 68.7 %all-gather.17.cloned.1.call-done = bf16[4096,256]{1,0:T(8,128)(2,1)} async-done(((bf16[128,256]{1,0:T(8,128)(2,1)}), bf16[4096,256]{1,0:T(8,128)(2,1)}) %all-gather.17.cloned.1.call-update) | async-done | bytes 2097168 | tf_op jit(solution)/shard_map/all_gather | solution.py:128
  358.9 2.4 convolution_convert_fusion.1
  362.1 1.1 copy.90
  365.1 55.0 %all-gather.19.cloned.1.call-done = bf16[4096,1,256]{2,0,1:T(8,128)(2,1)} async-done(((bf16[128,1,256]{2,0,1:T(8,128)(2,1)}), bf16[4096,1,256]{2,0,1:T(8,128)(2,1)}) %all-gather.19.cloned.1.call-update) | async-done | bytes 2097168 | tf_op jit(solution)/shard_map/all_gather | solution.py:133
  420.1 2.4 fusion.24
  423.1 1.1 convolution_add_fusion.1
  425.6 43.8 %all-gather.1 = f32[32,1,4,1]{2,3,1,0:T(1,128)} all-gather(f32[1,1,4,1]{2,3,1,0:T(1,128)S(1)} %get-tuple-element.328), channel_id=3, replica_groups=mesh['ctx'=32,'tp'=16] {'ctx'}, dimensions={0}, use_global_device_ids=true | all-gather | bytes 528 | tf_op jit(solution)/shard_map/all_gather | solution.py:11
  469.4 19.7 %all-gather.21.cloned.1.call-done = f32[32,4,64,128]{3,2,1,0:T(8,128)} async-done(((f32[1,4,64,128]{3,2,1,0:T(8,128)}), f32[32,4,64,128]{3,2,1,0:T(8,128)}) %all-gather.21.cloned.1.call-update) | async-done | bytes 4194320 | tf_op jit(solution)/shard_map/all_gather | solution.py:11
  489.1 70.9 %while.30 = (s32[]{:T(128)}, f32[1,4]{1,0:T(1,128)S(1)}, f32[1,4,64,128]{3,2,1,0:T(8,128)S(1)}, s32[]{:T(128)}, f32[32,1,4]{2,1,0:T(1,128)}, /*index=5*/f32[32,1,4,64,128]{4,3,2,1,0:T(8,128)}, s32[]{:T(128)}, s32[]{:T(128)}) while((s32[]{:T(128)}, f32[1,4]{1,0:T(1,128)S(1)}, f32[1,4,64,128]{3,2,1,0:T(8,128)S(1)}, s32[]{:T(128)}, ...), condition=%wide.region_6.7_spmd.clone, body=%wide.region_5.6_spmd.clone.sunk | while | flops 131088 | bytes 393431 | solution.py:23
  560.0 1.3 add_select_fusion
  561.4 2.0 reshape.405
  564.3 2.0 copy.102
  567.0 1.0 fusion.65
  568.0 1.3 fusion.50
  570.0 42.2 %all-gather.5 = f32[32,1,4]{2,1,0:T(1,128)S(1)} all-gather(f32[1,1,4]{2,1,0:T(1,128)S(1)} %fusion.91), channel_id=5, replica_groups=mesh['ctx'=32,'tp'=16] {'ctx'}, dimensions={0}, use_global_device_ids=true | all-gather | bytes 528 | tf_op jit(solution)/shard_map/all_gather | solution.py:11
  612.5 13.4 %all-gather.23.cloned.1.call-done = f32[32,4,64,128]{3,2,1,0:T(8,128)} async-done(((f32[1,4,64,128]{3,2,1,0:T(8,128)}), f32[32,4,64,128]{3,2,1,0:T(8,128)}) %all-gather.23.cloned.1.call-update) | async-done | bytes 4194320 | tf_op jit(solution)/shard_map/all_gather | solution.py:11
  625.9 4.8 reverse_bitcast_fusion
  630.7 32.0 %while.31 = (s32[]{:T(128)}, f32[1,4,64,128]{3,2,1,0:T(8,128)S(1)}, s32[]{:T(128)}, f32[32,1,4]{2,1,0:T(1,128)S(1)}, f32[32,1,4,64,128]{4,3,2,1,0:T(8,128)}, /*index=5*/s32[]{:T(128)}, s32[]{:T(128)}) while((s32[]{:T(128)}, f32[1,4,64,128]{3,2,1,0:T(8,128)S(1)}, s32[]{:T(128)}, f32[32,1,4]{2,1,0:T(1,128)S(1)}, ...), condition=%wide.region_8.9_spmd.clone, body=%wide.region_7.8_spmd.clone.sunk | while | flops 131076 | bytes 393369 | solution.py:23
  631.8 1.0 fusion.113
  632.8 1.0 fusion.113
  633.8 1.0 fusion.113
  (242 shorter events, 110.9 us)
Async XLA Ops:
  7.2 132.1 %copy-start = (bf16[128,4096]{1,0:T(8,128)(2,1)S(1)}, bf16[128,4096]{1,0:T(8,128)(2,1)}, u32[]{:S(2)}) copy-start(bf16[128,4096]{1,0:T(8,128)(2,1)} %param.20) | copy-start | bytes 3145732
  7.2 70.7 %all-gather.13.cloned.1.call-start = ((), (), s32[]{:S(2)}) async-start(), calls=%async_computation | async-start | bytes 2162688 | tf_op jit(solution)/shard_map/all_gather | solution.py:81
  9.1 130.2 %all-gather.15.cloned.1.call-start = ((), (), s32[]{:S(2)}) async-start(), calls=%async_computation.1 | async-start | bytes 2162688 | tf_op jit(solution)/shard_map/all_gather | solution.py:82
  10.9 276.1 %all-reduce.2.cloned.1.call-start = ((), (), s32[]{:S(2)}) async-start(), calls=%async_computation.2 | async-start | bytes 4194304 | tf_op jit(solution)/shard_map/psum | solution.py:109
  83.6 3.3 copy-start.1
  90.6 58.0 %copy-start.11 = (bf16[128,4,256]{2,1,0:T(4,128)(2,1)S(1)}, bf16[128,4,256]{2,1,0:T(4,128)(2,1)}, u32[]{:S(2)}) copy-start(bf16[128,4,256]{2,1,0:T(4,128)(2,1)} %param.23) | copy-start | bytes 786436
  90.6 58.9 %copy-start.14 = (bf16[128,4]{0,1:T(4,128)(2,1)S(1)}, bf16[128,4]{0,1:T(4,128)(2,1)}, u32[]{:S(2)}) copy-start(bf16[128,4]{0,1:T(4,128)(2,1)} %param.24) | copy-start | bytes 3076
  90.6 101.8 %copy-start.17 = (f32[4]{0:T(128)S(1)}, f32[4]{0:T(128)}, u32[]{:S(2)}) copy-start(f32[4]{0:T(128)} %param.26) | copy-start | bytes 52
  148.0 210.9 %copy-start.16 = (f32[4096]{0:T(1024)S(1)}, f32[4096]{0:T(1024)}, u32[]{:S(2)}) copy-start(f32[4096]{0:T(1024)} %param.21) | copy-start | bytes 49156
  148.0 210.9 %all-gather.17.cloned.1.call-start = ((), (), s32[]{:S(2)}) async-start(), calls=%async_computation.3 | async-start | bytes 2162688 | tf_op jit(solution)/shard_map/all_gather | solution.py:128
  148.6 271.5 %all-gather.19.cloned.1.call-start = ((), (), s32[]{:S(2)}) async-start(), calls=%async_computation.4 | async-start | bytes 2162688 | tf_op jit(solution)/shard_map/all_gather | solution.py:133
  149.4 339.7 %all-gather.21.cloned.1.call-start = ((), (), s32[]{:S(2)}) async-start(), calls=%async_computation.5 | async-start | bytes 4325376 | tf_op jit(solution)/shard_map/all_gather | solution.py:11
  290.2 73.0 %copy-start.18 = (f32[4]{0:T(128)S(1)}, f32[4]{0:T(128)}, u32[]{:S(2)}) copy-start(f32[4]{0:T(128)} %param.25) | copy-start | bytes 52
  290.2 73.8 %copy-start.15 = (f32[256]{0:T(256)}, f32[256]{0:T(256)S(1)}, u32[]{:S(2)}) copy-start(f32[256]{0:T(256)S(1)} %add_rsqrt_fusion) | copy-start | bytes 3076
  361.3 2.8 copy-start.9
  363.2 59.3 %copy-start.5 = (bf16[2,128,4,64]{1,3,2,0:T(8,128)(2,1)}, bf16[2,128,4,64]{1,3,2,0:T(8,128)(2,1)S(1)}, u32[]{:S(2)}) copy-start(bf16[2,128,4,64]{1,3,2,0:T(8,128)(2,1)S(1)} %copy.90) | copy-start | bytes 393220
  364.3 60.6 %copy-start.4 = (f32[2,128,1,4]{3,2,1,0:T(1,128)}, f32[2,128,1,4]{3,2,1,0:T(1,128)S(1)}, u32[]{:S(2)}) copy-start(f32[2,128,1,4]{3,2,1,0:T(1,128)S(1)} %fusion.59) | copy-start | bytes 12292
  365.1 60.0 %copy-start.12 = (f32[2,1,4,1]{2,1,3,0:T(1,128)S(1)}, f32[2,1,4,1]{2,1,3,0:T(1,128)}, u32[]{:S(2)}) copy-start(f32[2,1,4,1]{2,1,3,0:T(1,128)} %get-tuple-element.323) | copy-start | bytes 100
  422.5 0.7 copy-start.7
  424.2 137.1 %copy-start.2 = (f32[2,4,64,128]{3,2,1,0:T(8,128)}, f32[2,4,64,128]{3,2,1,0:T(8,128)S(1)}, u32[]{:S(2)}) copy-start(f32[2,4,64,128]{3,2,1,0:T(8,128)S(1)} %convolution_add_fusion.1) | copy-start | bytes 786436
  425.0 201.0 %all-gather.23.cloned.1.call-start = ((), (), s32[]{:S(2)}) async-start(), calls=%async_computation.6 | async-start | bytes 4325376 | tf_op jit(solution)/shard_map/all_gather | solution.py:11
  612.5 50.3 %copy-start.3 = (f32[2,4,64,128]{3,2,1,0:T(8,128)S(1)}, f32[2,4,64,128]{3,2,1,0:T(8,128)}, u32[]{:S(2)}) copy-start(f32[2,4,64,128]{3,2,1,0:T(8,128)} %copy-done.2) | copy-start | bytes 786436
  612.5 50.3 %copy-start.13 = (f32[4]{0:T(128)S(1)}, f32[4]{0:T(128)}, u32[]{:S(2)}) copy-start(f32[4]{0:T(128)} %get-tuple-element.326) | copy-start | bytes 52
  612.5 50.4 %copy-start.8 = (bf16[256,256]{1,0:T(8,128)(2,1)S(1)}, bf16[256,256]{1,0:T(8,128)(2,1)}, u32[]{:S(2)}) copy-start(bf16[256,256]{1,0:T(8,128)(2,1)} %copy-done.7) | copy-start | bytes 393220
  612.5 50.8 %copy-start.6 = (bf16[2,128,4,64]{1,3,2,0:T(8,128)(2,1)S(1)}, bf16[2,128,4,64]{1,3,2,0:T(8,128)(2,1)}, u32[]{:S(2)}) copy-start(bf16[2,128,4,64]{1,3,2,0:T(8,128)(2,1)} %copy-done.5) | copy-start | bytes 393220
  612.5 50.8 %copy-start.10 = (f32[2,128,1,4,64]{1,4,3,0,2:T(8,128)S(1)}, f32[2,128,1,4,64]{1,4,3,0,2:T(8,128)}, u32[]{:S(2)}) copy-start(f32[2,128,1,4,64]{1,4,3,0,2:T(8,128)} %copy.102) | copy-start | bytes 786436
  612.5 50.8 %copy-start.19 = (f32[4]{0:T(128)S(1)}, f32[4]{0:T(128)}, u32[]{:S(2)}) copy-start(f32[4]{0:T(128)} %param.27) | copy-start | bytes 52
Sparse Core Ops, SparseCore 0:
  11.7 66.1 all-gather.12
  81.6 57.6 all-gather.14
  148.1 138.8 all-reduce.1
  290.0 68.8 all-gather.16
  362.4 57.6 all-gather.18
  425.1 63.9 all-gather.20
  561.5 64.4 all-gather.22
where the time goes:
time: 674 us; the launch traced here: 672 us
  waiting for transfers between devices  368 us (55%)
  blocking collectives  129 us (19%)
  other arithmetic  91 us (14%)
  local copies, waits for them, and re-layouts  43.9 us (7%)
  matrix products  24.1 us (4%)
  between operations  14.6 us (2%)
    psum x1, waiting for transfers between devices, body(): lax.psum(head_part.astype(jnp.bfloat16), 'tp').astype(jnp.float32)  94.5 us
    all_gather x2, blocking collectives, prefix(): pieces = jax.tree.map(lambda part: lax.all_gather(part, axis), value)  86.1 us
    select_n x93, other arithmetic, lap(): jnp.where(position < mine, new, old)  81.7 us
    all_gather x1, waiting for transfers between devices, body(): lax.all_gather(x_proj, 'ctx', axis=0, tiled=True)  68.7 us
    all_gather x1, waiting for transfers between devices, body(): key_piece = lax.all_gather(keys_mine, 'ctx', axis=0, tiled=True)  66.9 us
    all_gather x1, waiting for transfers between devices, body(): lax.all_gather(bc_mine, 'ctx', axis=0, tiled=True)  55 us
    all_gather x1, waiting for transfers between devices, body(): value_piece = lax.all_gather(values_mine, 'ctx', axis=0, tiled=True)  48.6 us
    all_gather x1, blocking collectives, body(): lax.all_gather(dt_proj, 'ctx', axis=0, tiled=True)  43 us
  transfers between devices with their start and end apart: 7, of which 7 were waited for; matrix products, arithmetic and copies ran while one was open for 5% of the time, Pallas kernels for 0%

commit v1 on v0

v1 whole, which is shorter than its diff:
```python
import math

import jax
import jax.numpy as jnp
from jax import lax
from jax.sharding import Mesh
from jax.sharding import PartitionSpec as P

AXES = ("x", "zhh", "zhl", "co", "yhi", "ylo", "zl")
SIZES = (4, 2, 2, 2, 4, 2, 2)
ZH = ("zhh", "zhl")
CTX = ("x", "zhh", "zhl", "co")
Y = ("yhi", "ylo")
TP = ("yhi", "ylo", "zl")
BF = jnp.bfloat16
F32 = jnp.float32
LOWEST = -1e30


def split3(value):
    first = value.astype(BF)
    rest = value - first.astype(F32)
    second = rest.astype(BF)
    third = (rest - second.astype(F32)).astype(BF)
    return first, second, third


def swap(value, axis):
    return lax.ppermute(value, axis, [(0, 1), (1, 0)])


def exchange(value, axes):
    return lax.all_to_all(value, axes, split_axis=0, concat_axis=0, tiled=True)


def split_product(form, wide, narrow):
    upper = wide.astype(BF)
    lower = (wide - upper.astype(F32)).astype(BF)
    first_term = jnp.einsum(form, upper, narrow, preferred_element_type=F32)
    return first_term + jnp.einsum(form, lower, narrow, preferred_element_type=F32)


def body(
    queries,
    key_heads,
    head_values,
    hidden,
    out_proj,
    norm_gain,
    x_proj,
    bc_proj,
    dt_proj,
    dt_bias,
    decay_log,
    skip_gain,
):
    ctx = lax.axis_index(CTX)
    group = lax.axis_index("yhi")
    ylo = lax.axis_index("ylo")
    zl = lax.axis_index("zl")
    y = lax.axis_index(Y)
    quarter = 2 * ylo + zl

    bc_half = lax.dynamic_slice(bc_proj, (0, group, 128 * zl), (128, 1, 128))[:, 0]
    packed = jnp.concatenate(
        [x_proj, bc_half, jnp.pad(dt_proj, ((0, 0), (0, 124)))], axis=1
    )
    packed = lax.ppermute(packed, ("zhl", "zl"), [(0, 0), (1, 2), (2, 1), (3, 3)])
    weights = lax.all_gather(packed, ("zhl", "x", "zhh", "co"), axis=0, tiled=True)
    weights = weights.reshape(2, 2048, 512)

    other_q = swap(queries, "zl")
    pair_q = jnp.where(
        zl == 0, jnp.stack([queries, other_q]), jnp.stack([other_q, queries])
    )
    other_q = swap(pair_q, "ylo")
    four_q = jnp.where(
        ylo == 0,
        jnp.concatenate([pair_q, other_q]),
        jnp.concatenate([other_q, pair_q]),
    )

    by_zl = out_proj.reshape(128, 8, 2, 256)
    mine = lax.dynamic_index_in_dim(by_zl, zl, 2, keepdims=False)
    theirs = lax.dynamic_index_in_dim(by_zl, 1 - zl, 2, keepdims=False)
    pair_w = jnp.stack([mine, swap(theirs, "zl")]).reshape(2, 128, 2048)
    four_w = jnp.concatenate([pair_w, swap(pair_w, "ylo")])

    def part(heads):
        return lax.dynamic_slice(
            heads.reshape(2, 128, 4, 128), (0, 32 * quarter, group, 0), (2, 32, 1, 128)
        ).reshape(1, 64, 128)

    both = jnp.concatenate([part(key_heads), part(head_values)])[None]
    both = lax.all_gather(both, ZH, axis=0, tiled=True)
    both = lax.all_gather(both, "x", axis=0, tiled=True)
    keys = lax.all_gather(both[:, 0], "co", axis=0, tiled=True).reshape(2048, 128)
    values = lax.all_gather(both[:, 1], "co", axis=0, tiled=True).reshape(2048, 128)

    spot = jnp.arange(2048, dtype=jnp.int32)
    source = (spot // 64 % 16) * 2 + spot // 1024
    block = jnp.where(spot % 64 < 32, source, 63 - source)
    key_pos = block * 128 + 32 * quarter + spot % 32
    row = jnp.arange(256, dtype=jnp.int32)
    query_pos = jnp.where(row < 128, ctx, 63 - ctx) * 128 + row % 128
    scores = jnp.einsum(
        "hqd,kd->hqk", four_q, keys, preferred_element_type=F32
    ) / math.sqrt(128)
    allowed = key_pos[None, :] <= query_pos[:, None]
    top = jnp.max(jnp.where(allowed, scores, LOWEST), axis=-1)
    raised = jnp.where(allowed, jnp.exp(scores - top[..., None]), 0.0)
    total = jnp.sum(raised, axis=-1)
    summed = jnp.einsum("hqk,kd->hqd", raised.astype(BF), values, preferred_element_type=F32)
    safe = jnp.where(total > 0, total, 1.0)
    share = (summed / safe[..., None]).astype(BF)
    level = jnp.where(total > 0, top + jnp.log(safe), LOWEST)

    share = jnp.transpose(share.reshape(4, 4, 2, 32, 128), (2, 0, 1, 3, 4)).reshape(2, 512, 128)
    level = jnp.transpose(level.reshape(4, 4, 2, 32), (2, 0, 1, 3)).reshape(2, 4, 128)
    sent = jnp.concatenate([share, *split3(level), jnp.zeros((2, 4, 128), BF)], axis=1)
    sent = jnp.broadcast_to(sent[:, None], (2, 2, 528, 128)).reshape(4 * 528, 128)
    came = exchange(sent, ("ylo", "zl")).reshape(4, 528, 128)
    levels = came[:, 512:524].reshape(4, 3, 512).astype(F32)
    levels = (levels[:, 2] + levels[:, 1]) + levels[:, 0]
    scale = jnp.exp(levels - jnp.max(levels, axis=0))
    scale = scale / jnp.sum(scale, axis=0)
    attended = jnp.sum(scale[..., None] * came[:, :512].astype(F32), axis=0).astype(BF)
    attended = attended.reshape(4, 128, 128)
    relative = jnp.stack(
        [lax.dynamic_index_in_dim(attended, quarter ^ r, 0, keepdims=False) for r in range(4)]
    )
    head_part = jnp.einsum("rtd,rdn->tn", relative, four_w, preferred_element_type=F32)

    parts = exchange(head_part.astype(BF), "yhi").reshape(4, 32, 2048)
    attention_sum = jnp.sum(parts.astype(F32), axis=0)
    hidden_mine = lax.dynamic_slice(
        hidden.reshape(256, 8, 2, 256), (32 * y, 0, zl, 0), (32, 8, 1, 256)
    ).reshape(32, 2048)
    residual = (hidden_mine.astype(F32) + attention_sum).astype(BF)
    spread = jnp.broadcast_to(residual[None], (8, 32, 2048)).reshape(256, 2048)
    residual = exchange(spread, Y)
    residual_out = lax.dynamic_slice(residual, (0, 256 * y), (256, 256))

    gain = lax.dynamic_index_in_dim(norm_gain.reshape(8, 2, 256), zl, 1, keepdims=False)
    as_float = residual.astype(F32)
    square = jnp.sum(as_float * as_float, axis=-1, keepdims=True)
    gained = (as_float * gain.reshape(1, 2048)).astype(BF)
    sums = jnp.einsum("tk,zkn->ztn", gained, weights, preferred_element_type=F32)
    own = lax.dynamic_index_in_dim(sums, zl, 0, keepdims=False)
    away = lax.dynamic_index_in_dim(sums, 1 - zl, 0, keepdims=False)
    sum_bc = jnp.concatenate([sums[0, :, 256:384], sums[1, :, 256:384]], axis=1)
    fine = jnp.concatenate(split3(jnp.concatenate([away[:, 384:388], square], axis=1)), axis=1)
    sent = jnp.concatenate(
        [away[:, :256].astype(BF), sum_bc.astype(BF), jnp.pad(fine, ((0, 0), (0, 113)))], axis=1
    )
    came = swap(sent, "zl").astype(F32)
    fine = came[:, 512:527].reshape(256, 3, 5)
    fine = (fine[:, 2] + fine[:, 1]) + fine[:, 0]
    norm = lax.rsqrt((square + fine[:, 4:5]) / 4096.0 + 1e-05)
    sum_x = (own[:, :256] + came[:, :256]) * norm
    sum_bc = (sum_bc + came[:, 256:512]) * norm
    sum_dt = (own[:, 384:388] + fine[:, :4]) * norm

    half = 128
    inputs_low = sum_x.astype(BF).reshape(2, half, 1, 4, 64)
    inputs = inputs_low.astype(F32)
    bc_round = sum_bc.astype(BF).reshape(2, half, 1, 256)
    b_low = bc_round[..., :128]
    c_low = bc_round[..., 128:]
    steps = jax.nn.softplus(sum_dt + dt_bias).reshape(2, half, 1, 4)
    rates = -jnp.exp(decay_log).reshape(1, 4)
    cumul = jnp.transpose(jnp.cumsum(steps * rates, axis=1), (0, 2, 3, 1))
    step_rows = jnp.transpose(steps, (0, 2, 3, 1))
    gram = jnp.einsum("ckgn,csgn->cgks", c_low, b_low, preferred_element_type=F32)
    places = jnp.arange(half, dtype=jnp.int32)
    causal = places[None, :] <= places[:, None]
    gaps = cumul[..., :, None] - cumul[..., None, :]
    decay = jnp.where(causal, jnp.exp(jnp.where(causal, gaps, 0.0)), 0.0)
    mixing = gram[:, :, None] * decay * step_rows[..., None, :]
    inner = split_product("cgjks,csgjp->ckgjp", mixing, inputs_low)
    last = cumul[..., -1]
    tail = jnp.exp(last[..., None] - cumul) * step_rows
    weighted = jnp.transpose(tail, (0, 3, 1, 2))[..., None] * inputs
    block_state = split_product("csgjp,csgn->cgjpn", weighted, b_low)
    block_decay = jnp.exp(last)

    rows = jnp.transpose(block_state.reshape(2, 32, 8, 128), (1, 0, 2, 3)).reshape(32, 16, 128)
    decays = jnp.repeat(block_decay.reshape(2, 4).T, 8, axis=0)
    decays = jnp.broadcast_to(decays[..., None], (32, 2, 128))
    sent = jnp.concatenate([rows, decays, jnp.zeros((32, 6, 128), F32)], axis=1)
    came = exchange(sent, CTX)
    state = jnp.zeros((8, 128), F32)
    first, second = [], []
    for i in range(32):
        first.append(state)
        state = came[i, 16:17] * state + came[i, :8]
    for i in range(31, -1, -1):
        second.append(state)
        state = came[i, 17:18] * state + came[i, 8:16]
    entering = jnp.stack(
        [jnp.concatenate([a, b]) for a, b in zip(first, second[::-1])]
    )
    entering = exchange(entering, CTX)
    entering = jnp.transpose(entering.reshape(32, 2, 8, 128), (1, 0, 2, 3)).reshape(2, 1, 4, 64, 128)

    carried = jnp.transpose(jnp.exp(cumul), (0, 3, 1, 2))[..., None] * split_product(
        "cgjpn,ckgn->ckgjp", entering, c_low
    )
    output = inner + carried + skip_gain.reshape(1, 4)[:, :, None] * inputs
    mamba_out = output.reshape(256, 256).astype(BF)
    return (residual_out, mamba_out)


def solution(mesh):
    fine = Mesh(mesh.devices.reshape(SIZES), AXES)
    placed = (
        P(CTX, TP),
        P(CTX, None, None),
        P(CTX, None, None),
        P(CTX, None),
        P(TP, None),
        P(),
        P(CTX, TP),
        P(CTX, None, None),
        P(CTX, TP),
        P(TP),
        P(TP),
        P(TP),
    )
    return jax.shard_map(
        body,
        mesh=fine,
        in_specs=placed,
        out_specs=(P(CTX, TP), P(CTX, TP)),
        check_vma=False,
    )
```

time: 674 us -> 299 us (0.44)
  waiting for transfers between devices: 368 us -> 120 us
  blocking collectives: 129 us -> 37.6 us
  starting transfers between devices: 0.29 us -> 65 us
  other arithmetic: 91 us -> 27.7 us
  local copies, waits for them, and re-layouts: 43.9 us -> 14.6 us
    all_gather x6 -> x1, waiting for transfers between devices: 272 us -> 0.01 us  [body(): lax.all_gather(packed, ('zhl', 'x', 'zhh', 'co'), axis=0, tiled=True)]
    psum x1 -> x0, waiting for transfers between devices: 94.5 us -> none  [body(): lax.psum(head_part.astype(jnp.bfloat16), 'tp').astype(jnp.float32)]
    all_gather x3 -> x4, blocking collectives: 129 us -> 37.6 us  [the longest x1 16.5 us: body(): both = lax.all_gather(both, ZH, axis=0, tiled=True)]
    select_n x95 -> x3, other arithmetic: 83.1 us -> 0.1 us  [the longest x1 0.08 us: body(): steps = jax.nn.softplus(sum_dt + dt_bias).reshape(2, half, 1, 4)]
    all_to_all x0 -> x5, waiting for transfers between devices: none -> 64.8 us  [exchange(): return lax.all_to_all(value, axes, split_axis=0, concat_axis=0, tiled=True)]
    ppermute x0 -> x6, waiting for transfers between devices: none -> 54.8 us  [the longest x5 54.8 us: swap(): return lax.ppermute(value, axis, [(0, 1), (1, 0)])]
    all_to_all x0 -> x5, starting transfers between devices: none -> 47.6 us  [exchange(): return lax.all_to_all(value, axes, split_axis=0, concat_axis=0, tiled=True)]
    mul x63 -> x3, local copies, waits for them, and re-layouts: 20.6 us -> 0.03 us  [the longest x2 0.02 us: body(): state = came[i, 17:18] * state + came[i, 8:16]]
  transfers between devices with their start and end apart: 7 -> 12, of which waited for: 7 -> 8; matrix products, arithmetic and copies ran while one was open for 5% -> 11% of each run, Pallas kernels for 0% -> 0%
where the time goes in v1:
time: 299 us; the launch traced here: 298 us
  waiting for transfers between devices  120 us (40%)
  starting transfers between devices  65 us (22%)
  blocking collectives  37.6 us (13%)
  other arithmetic  27.7 us (9%)
  matrix products  18.9 us (6%)
  between operations  14.8 us (5%)
  local copies, waits for them, and re-layouts  14.6 us (5%)
    all_to_all x5, waiting for transfers between devices, exchange(): return lax.all_to_all(value, axes, split_axis=0, concat_axis=0, tiled=True)  64.8 us
    ppermute x5, waiting for transfers between devices, swap(): return lax.ppermute(value, axis, [(0, 1), (1, 0)])  54.8 us
    all_to_all x5, starting transfers between devices, exchange(): return lax.all_to_all(value, axes, split_axis=0, concat_axis=0, tiled=True)  47.6 us
    unnamed x30, other arithmetic  17.9 us
    ppermute x5, starting transfers between devices, swap(): return lax.ppermute(value, axis, [(0, 1), (1, 0)])  16.7 us
    all_gather x1, blocking collectives, body(): both = lax.all_gather(both, ZH, axis=0, tiled=True)  16.5 us
    all_gather x1, blocking collectives, body(): both = lax.all_gather(both, 'x', axis=0, tiled=True)  10.2 us
    all_gather x1, blocking collectives, body(): lax.all_gather(both[:, 0], 'co', axis=0, tiled=True).reshape(2048, 128)  8.45 us
  transfers between devices with their start and end apart: 12, of which 8 were waited for; matrix products, arithmetic and copies ran while one was open for 11% of the time, Pallas kernels for 0%

profile of v1, /device:TPU:1, one launch (start us, length us, event | category | flops | bytes accessed | tf_op | source)
XLA Modules:
  0.0 298.3 jit_solution(15356671813256384443)
XLA Ops:
  7.2 5.0 %collective-permute-start = (bf16[256,128]{1,0:T(8,128)(2,1)}, bf16[256,128]{1,0:T(8,128)(2,1)S(1)}, u32[]{:S(2)}, u32[]{:S(2)}) collective-permute-start(bf16[256,128]{1,0:T(8,128)(2,1)} %param.12), channel_id=1, source_target_pairs={{0,1},{1,0},{2,3},{3,2},{4,5},{5,4},{6,7},{7,6},{8,9},{9,8},{10,11... | collective-permute-start | bytes 196616 | tf_op jit(solution)/shard_map/ppermute | solution.py:29
  14.8 1.0 copy.115
  15.8 1.0 copy.116
  16.8 16.5 %all-gather = bf16[8,64,128]{2,1,0:T(8,128)(2,1)S(1)} all-gather(bf16[2,64,128]{2,1,0:T(8,128)(2,1)S(1)} %pad_maximum_fusion.3), channel_id=2, replica_groups=mesh['x'=4,'zhh'=2,'zhl'=2,'co'=2,'yhi'=4,'ylo'=2,'zl'=2] {'zhh','zhl'}, dimensions={0}, use_global_device_ids=true | all-gather | bytes 163840 | tf_op jit(solution)/shard_map/all_gather | solution.py:95
  33.3 10.2 %all_gather.16 = bf16[16,2,64,128]{3,2,1,0:T(8,128)(2,1)S(1)} all-gather(bf16[4,2,64,128]{3,2,1,0:T(8,128)(2,1)S(1)} %bitcast.727), channel_id=1, replica_groups=mesh['x'=4,'zhh'=2,'zhl'=2,'co'=2,'yhi'=4,'ylo'=2,'zl'=2] {'x'}, dimensions={0}, use_global_device_ids=true | all-gather | bytes 655360 | tf_op jit(solution)/shard_map/all_gather | solution.py:96
  43.9 8.4 %all-gather.1 = bf16[32,1,64,128]{3,2,1,0:T(8,128)(2,1)} all-gather(bf16[16,1,64,128]{3,2,1,0:T(8,128)(2,1)S(1)} %get-tuple-element.85), channel_id=3, replica_groups=mesh['x'=4,'zhh'=2,'zhl'=2,'co'=2,'yhi'=4,'ylo'=2,'zl'=2] {'co'}, dimensions={0}, use_global_device_ids=true | all-gather | bytes 786432 | tf_op jit(solution)/shard_map/all_gather | solution.py:97
  53.1 3.2 %collective-permute-start.1 = (bf16[2,256,128]{2,1,0:T(8,128)(2,1)S(1)}, bf16[2,256,128]{2,1,0:T(8,128)(2,1)S(1)}, u32[]{:S(2)}, u32[]{:S(2)}) collective-permute-start(bf16[2,256,128]{2,1,0:T(8,128)(2,1)S(1)} %maximum_select_fusion.2), channel_id=1, source_target_pairs={{0,2},{2,0},{1,3},{3,1},{4,6},{6,4},{5,7},{7,5},{8,10},{10,8},{9,1... | collective-permute-start | bytes 393224 | tf_op jit(solution)/shard_map/ppermute | solution.py:29
  56.3 2.5 all-gather.2
  59.7 6.0 %select_reduce_fusion = (f32[4,256]{1,0:T(4,128)S(1)}, f32[4,256,2048]{2,1,0:T(8,128)}) fusion(pred[256,2048]{1,0:T(8,128)(4,1)S(1)} %broadcast_compare_fusion, bf16[2048,128,1]{1,0,2:T(8,128)(2,1)} %bitcast.728, bf16[2,256,128]{2,1,0:T(8,128)(2,1)S(1)} %collective-permute-done.1, bf16[2,256,128]{2,1,0:T(8,128)(2,1)S(1)} %maximum_select_fusion.2, pred[]{:T(512)S(6)} %eq.12), kind=kOutput, calls=%fused_computation.1 | convolution fusion | flops 543554560 | bytes 9703425 | tf_op jit(solution)/shard_map/hqd,kd->hqk/dot_general | solution.py:106
  65.8 4.6 %fusion = f32[4,256]{1,0:T(4,128)S(1)} fusion(f32[4,256,2048]{2,1,0:T(8,128)} %get-tuple-element.162, f32[4,256]{1,0:T(4,128)S(1)} %get-tuple-element.161, pred[256,2048]{1,0:T(8,128)(4,1)S(1)} %broadcast_compare_fusion), kind=kLoop, calls=%fused_computation.2 | loop fusion | flops 8387584 | bytes 8921088 | tf_op jit(solution)/shard_map/reduce_sum | solution.py:112
  70.6 5.1 %fusion.22 = bf16[4,256,128]{2,1,0:T(8,128)(2,1)S(1)} fusion(bf16[2048,128,1]{1,0,2:T(8,128)(2,1)S(1)} %bitcast.729, f32[4,256,2048]{2,1,0:T(8,128)} %get-tuple-element.162, f32[4,256]{1,0:T(4,128)S(1)} %get-tuple-element.161, pred[256,2048]{1,0:T(8,128)(4,1)S(1)} %broadcast_compare_fusion, f32[4,256]{1,0:T(4,128)S(1)} %compare_select_fusion.3), kind=kOutput, calls=%fused_computation.31 | convolution fusion | flops 545521664 | bytes 9707520 | tf_op jit(solution)/shard_map/hqk,kd->hqd/dot_general | solution.py:113
  76.0 0.9 broadcast_in_dim.105
  76.9 5.7 %all-to-all-start = ((bf16[4,528,128]{2,1,0:T(8,128)(2,1)}), bf16[4,528,128]{2,1,0:T(8,128)(2,1)S(1)}, u32[]{:S(2)}, u32[]{:S(2)}) async-start(bf16[4,528,128]{2,1,0:T(8,128)(2,1)} %bitcast.15), calls=%async_computation | async-start | bytes 1081344 | tf_op jit(solution)/shard_map/all_to_all | solution.py:33
  83.1 3.4 %collective-permute-start.2 = (bf16[128,8,256]{2,1,0:T(8,128)(2,1)S(1)}, bf16[128,8,256]{2,1,0:T(8,128)(2,1)S(1)}, u32[]{:S(2)}, u32[]{:S(2)}) collective-permute-start(bf16[128,8,256]{2,1,0:T(8,128)(2,1)S(1)} %bitcast.730), channel_id=1, source_target_pairs={{0,1},{1,0},{2,3},{3,2},{4,5},{5,4},{6,7},{7,6},{8,9},{9,8},{10,11... | collective-permute-start | bytes 1572872 | tf_op jit(solution)/shard_map/ppermute | solution.py:29
  86.7 23.6 %collective-permute-done.2 = bf16[128,8,256]{2,1,0:T(8,128)(2,1)S(1)} collective-permute-done((bf16[128,8,256]{2,1,0:T(8,128)(2,1)S(1)}, bf16[128,8,256]{2,1,0:T(8,128)(2,1)S(1)}, u32[]{:S(2)}, u32[]{:S(2)}) %collective-permute-start.2) | collective-permute-done | bytes 524320 | tf_op jit(solution)/shard_map/ppermute | solution.py:29
  110.7 3.2 %collective-permute-start.3 = (bf16[2,128,2048]{2,1,0:T(8,128)(2,1)S(1)}, bf16[2,128,2048]{2,1,0:T(8,128)(2,1)}, u32[]{:S(2)}, u32[]{:S(2)}) collective-permute-start(bf16[2,128,2048]{2,1,0:T(8,128)(2,1)S(1)} %pad_maximum_fusion), channel_id=1, source_target_pairs={{0,2},{2,0},{1,3},{3,1},{4,6},{6,4},{5,7},{7,5},{8,10},{10,8},{9,1... | collective-permute-start | bytes 3145736 | tf_op jit(solution)/shard_map/ppermute | solution.py:29
  114.4 22.3 %collective-permute-done.3 = bf16[2,128,2048]{2,1,0:T(8,128)(2,1)} collective-permute-done((bf16[2,128,2048]{2,1,0:T(8,128)(2,1)S(1)}, bf16[2,128,2048]{2,1,0:T(8,128)(2,1)}, u32[]{:S(2)}, u32[]{:S(2)}) %collective-permute-start.3) | collective-permute-done | bytes 1048608 | tf_op jit(solution)/shard_map/ppermute | solution.py:29
  136.8 2.6 fusion.5
  139.3 6.6 %all-to-all-start.1 = ((bf16[4,32,2048]{2,1,0:T(8,128)(2,1)}), bf16[4,32,2048]{2,1,0:T(8,128)(2,1)S(1)}, u32[]{:S(2)}, u32[]{:S(2)}) async-start(bf16[4,32,2048]{2,1,0:T(8,128)(2,1)} %bitcast.21), calls=%async_computation.1 | async-start | bytes 1048576 | tf_op jit(solution)/shard_map/all_to_all | solution.py:33
  146.0 3.3 %reshape.448 = bf16[256,8,2,256]{3,2,1,0:T(2,128)(2,1)S(1)} reshape(bf16[256,4096]{1,0:T(8,128)(2,1)} %param.15) | data formatting | bytes 4194304 | tf_op jit(solution)/shard_map/reshape | solution.py:137
  150.1 9.0 %all-to-all-done.1 = bf16[4,32,2048]{2,1,0:T(8,128)(2,1)S(1)} async-done(((bf16[4,32,2048]{2,1,0:T(8,128)(2,1)}), bf16[4,32,2048]{2,1,0:T(8,128)(2,1)S(1)}, u32[]{:S(2)}, u32[]{:S(2)}) %all-to-all-start.1) | async-done | bytes 524320 | tf_op jit(solution)/shard_map/all_to_all | solution.py:33
  159.3 1.1 broadcast_in_dim.106
  160.4 5.6 %all-to-all-start.2 = ((bf16[8,32,2048]{2,1,0:T(8,128)(2,1)}), bf16[8,32,2048]{2,1,0:T(8,128)(2,1)S(1)}, u32[]{:S(2)}, u32[]{:S(2)}) async-start(bf16[8,32,2048]{2,1,0:T(8,128)(2,1)} %broadcast_in_dim.106), calls=%async_computation.2 | async-start | bytes 2097152 | tf_op jit(solution)/shard_map/all_to_all | solution.py:33
  166.0 29.1 %all-to-all-done.2 = bf16[8,32,2048]{2,1,0:T(8,128)(2,1)S(1)} async-done(((bf16[8,32,2048]{2,1,0:T(8,128)(2,1)}), bf16[8,32,2048]{2,1,0:T(8,128)(2,1)S(1)}, u32[]{:S(2)}, u32[]{:S(2)}) %all-to-all-start.2) | async-done | bytes 1048608 | tf_op jit(solution)/shard_map/all_to_all | solution.py:33
  195.7 3.5 %fusion.259 = f32[2,512,256]{2,1,0:T(8,128)S(1)} fusion(bf16[2,2048,512]{2,1,0:T(8,128)(2,1)} %bitcast.746, bf16[256,2048,1]{1,0,2:T(8,128)(2,1)S(1)} %bitcast.720), kind=kOutput, calls=%fused_computation.465 | convolution fusion | flops 1073741824 | bytes 6291456 | tf_op jit(solution)/shard_map/tk,zkn->ztn/dot_general | solution.py:148
  199.4 1.9 collective-permute-start.5
  201.5 8.7 %collective-permute-done.5 = bf16[256,640]{0,1:T(8,128)(2,1)S(1)} collective-permute-done((bf16[256,640]{0,1:T(8,128)(2,1)S(1)}, bf16[256,640]{0,1:T(8,128)(2,1)S(1)}, u32[]{:S(2)}, u32[]{:S(2)}) %collective-permute-start.5) | collective-permute-done | bytes 327712 | tf_op jit(solution)/shard_map/ppermute | solution.py:29
  212.5 24.8 %all-to-all-start.3 = ((f32[32,24,128]{2,1,0:T(8,128)}), f32[32,24,128]{2,1,0:T(8,128)S(1)}, u32[]{:S(2)}, u32[]{:S(2)}) async-start(f32[32,24,128]{2,1,0:T(8,128)} %maximum_maximum_fusion), calls=%async_computation.3 | async-start | bytes 786432 | tf_op jit(solution)/shard_map/all_to_all | solution.py:33
  237.3 15.4 %all-to-all-done.3 = f32[32,24,128]{2,1,0:T(8,128)S(1)} async-done(((f32[32,24,128]{2,1,0:T(8,128)}), f32[32,24,128]{2,1,0:T(8,128)S(1)}, u32[]{:S(2)}, u32[]{:S(2)}) %all-to-all-start.3) | async-done | bytes 393248 | tf_op jit(solution)/shard_map/all_to_all | solution.py:33
  272.0 4.8 %all-to-all-start.4 = ((f32[32,16,128]{2,1,0:T(8,128)}), f32[32,16,128]{2,1,0:T(8,128)S(1)}, u32[]{:S(2)}, u32[]{:S(2)}) async-start(f32[32,16,128]{2,1,0:T(8,128)} %constant_dynamic-update-slice_fusion), calls=%async_computation.4 | async-start | bytes 524288 | tf_op jit(solution)/shard_map/all_to_all | solution.py:33
  278.3 11.3 %all-to-all-done.4 = f32[32,16,128]{2,1,0:T(8,128)S(1)} async-done(((f32[32,16,128]{2,1,0:T(8,128)}), f32[32,16,128]{2,1,0:T(8,128)S(1)}, u32[]{:S(2)}, u32[]{:S(2)}) %all-to-all-start.4) | async-done | bytes 262176 | tf_op jit(solution)/shard_map/all_to_all | solution.py:33
  290.6 0.9 reshape.486
  (150 shorter events, 32.3 us)
Async XLA Ops:
  7.2 5.1 %copy-start = (bf16[128,4,256]{2,1,0:T(4,128)(2,1)S(1)}, bf16[128,4,256]{2,1,0:T(4,128)(2,1)}, u32[]{:S(2)}) copy-start(bf16[128,4,256]{2,1,0:T(4,128)(2,1)} %param.19) | copy-start | bytes 786436
  7.2 45.9 %copy-start.3 = (bf16[256,128]{1,0:T(8,128)(2,1)S(1)}, bf16[256,128]{1,0:T(8,128)(2,1)}, u32[]{:S(2)}) copy-start(bf16[256,128]{1,0:T(8,128)(2,1)} %param.12) | copy-start | bytes 196612
  7.2 45.2 %copy-start.1 = (bf16[128,4096]{1,0:T(8,128)(2,1)S(1)}, bf16[128,4096]{1,0:T(8,128)(2,1)}, u32[]{:S(2)}) copy-start(bf16[128,4096]{1,0:T(8,128)(2,1)} %param.16) | copy-start | bytes 3145732
  7.2 188.5 %all-gather.5.cloned.1.call-start = ((), (), s32[]{:S(2)}) async-start(), calls=%async_computation.5 | async-start | bytes 4325376 | tf_op jit(solution)/shard_map/all_gather | solution.py:69
  7.2 45.8 %collective-permute-start = (bf16[256,128]{1,0:T(8,128)(2,1)}, bf16[256,128]{1,0:T(8,128)(2,1)S(1)}, u32[]{:S(2)}, u32[]{:S(2)}) collective-permute-start(bf16[256,128]{1,0:T(8,128)(2,1)} %param.12), channel_id=1, source_target_pairs={{0,1},{1,0},{2,3},{3,2},{4,5},{5,4},{6,7},{7,6},{8,9},{9,8},{10,11... | collective-permute-start | bytes 196616 | tf_op jit(solution)/shard_map/ppermute | solution.py:29
  14.1 44.7 %collective-permute-start.4 = (bf16[128,512]{1,0:T(8,128)(2,1)S(1)}, bf16[128,512]{1,0:T(8,128)(2,1)S(1)}, u32[]{:S(2)}, u32[]{:S(2)}) collective-permute-start(bf16[128,512]{1,0:T(8,128)(2,1)S(1)} %fusion.51), channel_id=1, source_target_pairs={{0,0},{1,32},{32,1},{33,33},{2,2},{3,34},{34,3},{35,35},{4,4},{5,3... | collective-permute-start | bytes 393224 | tf_op jit(solution)/shard_map/ppermute | solution.py:68
  53.1 6.6 %collective-permute-start.1 = (bf16[2,256,128]{2,1,0:T(8,128)(2,1)S(1)}, bf16[2,256,128]{2,1,0:T(8,128)(2,1)S(1)}, u32[]{:S(2)}, u32[]{:S(2)}) collective-permute-start(bf16[2,256,128]{2,1,0:T(8,128)(2,1)S(1)} %maximum_select_fusion.2), channel_id=1, source_target_pairs={{0,2},{2,0},{1,3},{3,1},{4,6},{6,4},{5,7},{7,5},{8,10},{10,8},{9,1... | collective-permute-start | bytes 393224 | tf_op jit(solution)/shard_map/ppermute | solution.py:29
  58.8 0.7 copy-start.2
  76.9 37.0 %all-to-all-start = ((bf16[4,528,128]{2,1,0:T(8,128)(2,1)}), bf16[4,528,128]{2,1,0:T(8,128)(2,1)S(1)}, u32[]{:S(2)}, u32[]{:S(2)}) async-start(bf16[4,528,128]{2,1,0:T(8,128)(2,1)} %bitcast.15), calls=%async_computation | async-start | bytes 1081344 | tf_op jit(solution)/shard_map/all_to_all | solution.py:33
  83.1 27.2 %collective-permute-start.2 = (bf16[128,8,256]{2,1,0:T(8,128)(2,1)S(1)}, bf16[128,8,256]{2,1,0:T(8,128)(2,1)S(1)}, u32[]{:S(2)}, u32[]{:S(2)}) collective-permute-start(bf16[128,8,256]{2,1,0:T(8,128)(2,1)S(1)} %bitcast.730), channel_id=1, source_target_pairs={{0,1},{1,0},{2,3},{3,2},{4,5},{5,4},{6,7},{7,6},{8,9},{9,8},{10,11... | collective-permute-start | bytes 1572872 | tf_op jit(solution)/shard_map/ppermute | solution.py:29
  110.7 26.1 %collective-permute-start.3 = (bf16[2,128,2048]{2,1,0:T(8,128)(2,1)S(1)}, bf16[2,128,2048]{2,1,0:T(8,128)(2,1)}, u32[]{:S(2)}, u32[]{:S(2)}) collective-permute-start(bf16[2,128,2048]{2,1,0:T(8,128)(2,1)S(1)} %pad_maximum_fusion), channel_id=1, source_target_pairs={{0,2},{2,0},{1,3},{3,1},{4,6},{6,4},{5,7},{7,5},{8,10},{10,8},{9,1... | collective-permute-start | bytes 3145736 | tf_op jit(solution)/shard_map/ppermute | solution.py:29
  139.3 19.8 %all-to-all-start.1 = ((bf16[4,32,2048]{2,1,0:T(8,128)(2,1)}), bf16[4,32,2048]{2,1,0:T(8,128)(2,1)S(1)}, u32[]{:S(2)}, u32[]{:S(2)}) async-start(bf16[4,32,2048]{2,1,0:T(8,128)(2,1)} %bitcast.21), calls=%async_computation.1 | async-start | bytes 1048576 | tf_op jit(solution)/shard_map/all_to_all | solution.py:33
  146.0 20.0 %copy-start.4 = (f32[4096]{0:T(1024)S(1)}, f32[4096]{0:T(1024)}, u32[]{:S(2)}) copy-start(f32[4096]{0:T(1024)} %param.17) | copy-start | bytes 49156
  160.4 34.8 %all-to-all-start.2 = ((bf16[8,32,2048]{2,1,0:T(8,128)(2,1)}), bf16[8,32,2048]{2,1,0:T(8,128)(2,1)S(1)}, u32[]{:S(2)}, u32[]{:S(2)}) async-start(bf16[8,32,2048]{2,1,0:T(8,128)(2,1)} %broadcast_in_dim.106), calls=%async_computation.2 | async-start | bytes 2097152 | tf_op jit(solution)/shard_map/all_to_all | solution.py:33
  195.7 5.8 %copy-start.6 = (f32[4]{0:T(128)S(1)}, f32[4]{0:T(128)}, u32[]{:S(2)}) copy-start(f32[4]{0:T(128)} %param.22) | copy-start | bytes 52
  199.2 11.3 %copy-start.5 = (f32[4]{0:T(128)S(1)}, f32[4]{0:T(128)}, u32[]{:S(2)}) copy-start(f32[4]{0:T(128)} %param.21) | copy-start | bytes 52
  199.4 10.7 %collective-permute-start.5 = (bf16[256,640]{0,1:T(8,128)(2,1)S(1)}, bf16[256,640]{0,1:T(8,128)(2,1)S(1)}, u32[]{:S(2)}, u32[]{:S(2)}) collective-permute-start(bf16[256,640]{0,1:T(8,128)(2,1)S(1)} %pad_maximum_fusion.1), channel_id=1, source_target_pairs={{0,1},{1,0},{2,3},{3,2},{4,5},{5,4},{6,7},{7,6},{8,9},{9,8},{10,11... | collective-permute-start | bytes 983048 | tf_op jit(solution)/shard_map/ppermute | solution.py:29
  211.4 78.6 %copy-start.7 = (f32[4]{0:T(128)S(1)}, f32[4]{0:T(128)}, u32[]{:S(2)}) copy-start(f32[4]{0:T(128)} %param.23) | copy-start | bytes 52
  212.5 40.2 %all-to-all-start.3 = ((f32[32,24,128]{2,1,0:T(8,128)}), f32[32,24,128]{2,1,0:T(8,128)S(1)}, u32[]{:S(2)}, u32[]{:S(2)}) async-start(f32[32,24,128]{2,1,0:T(8,128)} %maximum_maximum_fusion), calls=%async_computation.3 | async-start | bytes 786432 | tf_op jit(solution)/shard_map/all_to_all | solution.py:33
  272.0 17.6 %all-to-all-start.4 = ((f32[32,16,128]{2,1,0:T(8,128)}), f32[32,16,128]{2,1,0:T(8,128)S(1)}, u32[]{:S(2)}, u32[]{:S(2)}) async-start(f32[32,16,128]{2,1,0:T(8,128)} %constant_dynamic-update-slice_fusion), calls=%async_computation.4 | async-start | bytes 524288 | tf_op jit(solution)/shard_map/all_to_all | solution.py:33
Sparse Core Ops, SparseCore 0:
  59.6 86.1 all-gather.4

commit v2 on v1

--- a/solution.py
+++ b/solution.py
@@ -3,6 +3,8 @@
 import jax
 import jax.numpy as jnp
 from jax import lax
+from jax.experimental import pallas as pl
+from jax.experimental.pallas import tpu as pltpu
 from jax.sharding import Mesh
 from jax.sharding import PartitionSpec as P
 
@@ -25,6 +27,16 @@
     return first, second, third
 
 
+def features(value, zl):
+    return jnp.concatenate(
+        [
+            lax.dynamic_slice_in_dim(value, 512 * i + 256 * zl, 256, 1)
+            for i in range(8)
+        ],
+        axis=1,
+    )
+
+
 def swap(value, axis):
     return lax.ppermute(value, axis, [(0, 1), (1, 0)])
 
@@ -38,6 +50,98 @@
     lower = (wide - upper.astype(F32)).astype(BF)
     first_term = jnp.einsum(form, upper, narrow, preferred_element_type=F32)
     return first_term + jnp.einsum(form, lower, narrow, preferred_element_type=F32)
+
+
+def attend(spots, q_ref, k_ref, v_ref, out_ref):
+    ctx, quarter = spots[0], spots[1]
+    lane = lax.broadcasted_iota(jnp.int32, (32, 256), 1)
+    token = lane % 128 // 32 * 64 + lane // 128 * 32 + lane % 32
+    seat = jnp.where(token < 128, ctx, 63 - ctx) * 128 + token % 128
+    reach = seat - lax.broadcasted_iota(jnp.int32, (32, 256), 0)
+    levels = []
+    for head in range(4):
+        tiles = []
+        for chunk in range(8):
+            scores = lax.dot_general(
+                k_ref[256 * chunk : 256 * (chunk + 1)],
+                q_ref[head],
+                (((1,), (1,)), ((), ())),
+                preferred_element_type=F32,
+            ) * (math.log2(math.e) / math.sqrt(128))
+            for piece in range(8):
+                place = 4 * chunk + piece // 2
+                source = place % 16 * 2 + place // 16
+                block = source if piece % 2 == 0 else 63 - source
+                allowed = reach >= block * 128 + 32 * quarter
+                tiles.append(
+                    jnp.where(allowed, scores[32 * piece : 32 * (piece + 1)], LOWEST)
+                )
+        top = tiles[0]
+        for tile in tiles[1:]:
+            top = jnp.maximum(top, tile)
+        top = jnp.max(top, axis=0, keepdims=True)
+        total = jnp.zeros((32, 256), F32)
+        summed = jnp.zeros((128, 256), F32)
+        for chunk in range(8):
+            raised = [jnp.exp2(tile - top) for tile in tiles[8 * chunk : 8 * chunk + 8]]
+            for part in raised:
+                total = total + part
+            summed = summed + lax.dot_general(
+                v_ref[256 * chunk : 256 * (chunk + 1)],
+                jnp.concatenate(raised).astype(BF),
+                (((0,), (0,)), ((), ())),
+                preferred_element_type=F32,
+            )
+        total = jnp.sum(total, axis=0, keepdims=True)
+        share = (summed / total).astype(BF)
+        for dest in range(4):
+            half = dest // 2
+            out_ref[dest, 128 * head : 128 * (head + 1)] = share[:, 128 * half : 128 * half + 128]
+        levels.append(jnp.where(top > 0.5 * LOWEST, top + jnp.log2(total), LOWEST))
+    level = jnp.concatenate(levels)
+    fine = jnp.concatenate([*split3(level), jnp.zeros((4, 256), BF)])
+    for dest in range(4):
+        half = dest // 2
+        out_ref[dest, 512:528] = fine[:, 128 * half : 128 * half + 128]
+
+
+def project(spots, came_ref, own_ref, far_ref, out_ref, attended):
+    quarter = spots[1]
+    fine = [came_ref[source, 512:528].astype(F32) for source in range(4)]
+    levels = [(part[8:12] + part[4:8]) + part[0:4] for part in fine]
+    top = jnp.maximum(jnp.maximum(levels[0], levels[1]), jnp.maximum(levels[2], levels[3]))
+    scales = [jnp.exp2(level - top) for level in levels]
+    total = (scales[0] + scales[1]) + (scales[2] + scales[3])
+    scales = [scale / total for scale in scales]
+    for head in range(4):
+        joined = jnp.zeros((128, 128), F32)
+        for source in range(4):
+            joined = joined + scales[source][head : head + 1] * came_ref[
+                source, 128 * head : 128 * (head + 1)
+            ].astype(F32)
+        attended[head] = joined.astype(BF)
+    total = None
+    for far, w_ref in ((0, own_ref), (2, far_ref)):
+        pair = jnp.concatenate([attended[quarter ^ far], attended[quarter ^ far ^ 1]])
+        product = lax.dot_general(
+            pair, w_ref[...], (((0,), (0,)), ((), ())), preferred_element_type=F32
+        )
+        total = product if total is None else total + product
+    out_ref[...] = total.astype(BF)
+
+
+def scan(came_ref, out_ref):
+    state = jnp.zeros((8, 128), F32)
+    for i in range(32):
+        out_ref[i, :8] = state
+        state = came_ref[i, 16:17] * state + came_ref[i, :8]
+    for i in range(31, -1, -1):
+        out_ref[i, 8:] = state
+        state = came_ref[i, 17:18] * state + came_ref[i, 8:16]
+
+
+VM = pl.BlockSpec(memory_space=pltpu.VMEM)
+SM = pl.BlockSpec(memory_space=pltpu.SMEM)
 
 
 def body(
@@ -69,22 +173,11 @@
     weights = lax.all_gather(packed, ("zhl", "x", "zhh", "co"), axis=0, tiled=True)
     weights = weights.reshape(2, 2048, 512)
 
-    other_q = swap(queries, "zl")
-    pair_q = jnp.where(
-        zl == 0, jnp.stack([queries, other_q]), jnp.stack([other_q, queries])
-    )
-    other_q = swap(pair_q, "ylo")
-    four_q = jnp.where(
-        ylo == 0,
-        jnp.concatenate([pair_q, other_q]),
-        jnp.concatenate([other_q, pair_q]),
-    )
-
-    by_zl = out_proj.reshape(128, 8, 2, 256)
-    mine = lax.dynamic_index_in_dim(by_zl, zl, 2, keepdims=False)
-    theirs = lax.dynamic_index_in_dim(by_zl, 1 - zl, 2, keepdims=False)
-    pair_w = jnp.stack([mine, swap(theirs, "zl")]).reshape(2, 128, 2048)
-    four_w = jnp.concatenate([pair_w, swap(pair_w, "ylo")])
+    spots = jnp.stack([ctx, quarter]).astype(jnp.int32)
+
+    sorted_q = jnp.swapaxes(queries.reshape(4, 2, 32, 128), 0, 1).reshape(256, 128)
+    mine = features(out_proj, zl)
+    theirs = features(out_proj, 1 - zl)
 
     def part(heads):
         return lax.dynamic_slice(
@@ -92,50 +185,47 @@
         ).reshape(1, 64, 128)
 
     both = jnp.concatenate([part(key_heads), part(head_values)])[None]
+    other_q = swap(sorted_q, "zl")
+    other_w = swap(theirs, "zl")
     both = lax.all_gather(both, ZH, axis=0, tiled=True)
+    both, other_q, other_w = lax.optimization_barrier((both, other_q, other_w))
+    pair_q = jnp.where(
+        zl == 0, jnp.stack([sorted_q, other_q]), jnp.stack([other_q, sorted_q])
+    )
+    pair_w = jnp.concatenate([mine, other_w])
+    far_q = swap(pair_q, "ylo")
+    far_w = swap(pair_w, "ylo")
     both = lax.all_gather(both, "x", axis=0, tiled=True)
     keys = lax.all_gather(both[:, 0], "co", axis=0, tiled=True).reshape(2048, 128)
     values = lax.all_gather(both[:, 1], "co", axis=0, tiled=True).reshape(2048, 128)
-
-    spot = jnp.arange(2048, dtype=jnp.int32)
-    source = (spot // 64 % 16) * 2 + spot // 1024
-    block = jnp.where(spot % 64 < 32, source, 63 - source)
-    key_pos = block * 128 + 32 * quarter + spot % 32
-    row = jnp.arange(256, dtype=jnp.int32)
-    query_pos = jnp.where(row < 128, ctx, 63 - ctx) * 128 + row % 128
-    scores = jnp.einsum(
-        "hqd,kd->hqk", four_q, keys, preferred_element_type=F32
-    ) / math.sqrt(128)
-    allowed = key_pos[None, :] <= query_pos[:, None]
-    top = jnp.max(jnp.where(allowed, scores, LOWEST), axis=-1)
-    raised = jnp.where(allowed, jnp.exp(scores - top[..., None]), 0.0)
-    total = jnp.sum(raised, axis=-1)
-    summed = jnp.einsum("hqk,kd->hqd", raised.astype(BF), values, preferred_element_type=F32)
-    safe = jnp.where(total > 0, total, 1.0)
-    share = (summed / safe[..., None]).astype(BF)
-    level = jnp.where(total > 0, top + jnp.log(safe), LOWEST)
-
-    share = jnp.transpose(share.reshape(4, 4, 2, 32, 128), (2, 0, 1, 3, 4)).reshape(2, 512, 128)
-    level = jnp.transpose(level.reshape(4, 4, 2, 32), (2, 0, 1, 3)).reshape(2, 4, 128)
-    sent = jnp.concatenate([share, *split3(level), jnp.zeros((2, 4, 128), BF)], axis=1)
-    sent = jnp.broadcast_to(sent[:, None], (2, 2, 528, 128)).reshape(4 * 528, 128)
-    came = exchange(sent, ("ylo", "zl")).reshape(4, 528, 128)
-    levels = came[:, 512:524].reshape(4, 3, 512).astype(F32)
-    levels = (levels[:, 2] + levels[:, 1]) + levels[:, 0]
-    scale = jnp.exp(levels - jnp.max(levels, axis=0))
-    scale = scale / jnp.sum(scale, axis=0)
-    attended = jnp.sum(scale[..., None] * came[:, :512].astype(F32), axis=0).astype(BF)
-    attended = attended.reshape(4, 128, 128)
-    relative = jnp.stack(
-        [lax.dynamic_index_in_dim(attended, quarter ^ r, 0, keepdims=False) for r in range(4)]
-    )
-    head_part = jnp.einsum("rtd,rdn->tn", relative, four_w, preferred_element_type=F32)
-
-    parts = exchange(head_part.astype(BF), "yhi").reshape(4, 32, 2048)
+    four_q = jnp.where(
+        ylo == 0,
+        jnp.concatenate([pair_q, far_q]),
+        jnp.concatenate([far_q, pair_q]),
+    )
+
+    sent = pl.pallas_call(
+        attend,
+        out_shape=jax.ShapeDtypeStruct((4, 528, 128), BF),
+        in_specs=[SM, VM, VM, VM],
+        out_specs=VM,
+        compiler_params=pltpu.CompilerParams(vmem_limit_bytes=32 << 20),
+        name="attend",
+    )(spots, four_q, keys, values)
+    came = exchange(sent.reshape(4 * 528, 128), ("ylo", "zl")).reshape(4, 528, 128)
+    head_part = pl.pallas_call(
+        project,
+        out_shape=jax.ShapeDtypeStruct((128, 2048), BF),
+        in_specs=[SM, VM, VM, VM],
+        out_specs=VM,
+        scratch_shapes=[pltpu.VMEM((4, 128, 128), BF)],
+        compiler_params=pltpu.CompilerParams(vmem_limit_bytes=32 << 20),
+        name="project",
+    )(spots, came, pair_w, far_w)
+
+    parts = exchange(head_part, "yhi").reshape(4, 32, 2048)
     attention_sum = jnp.sum(parts.astype(F32), axis=0)
-    hidden_mine = lax.dynamic_slice(
-        hidden.reshape(256, 8, 2, 256), (32 * y, 0, zl, 0), (32, 8, 1, 256)
-    ).reshape(32, 2048)
+    hidden_mine = features(lax.dynamic_slice(hidden, (32 * y, 0), (32, 4096)), zl)
     residual = (hidden_mine.astype(F32) + attention_sum).astype(BF)
     spread = jnp.broadcast_to(residual[None], (8, 32, 2048)).reshape(256, 2048)
     residual = exchange(spread, Y)
@@ -189,17 +279,13 @@
     decays = jnp.broadcast_to(decays[..., None], (32, 2, 128))
     sent = jnp.concatenate([rows, decays, jnp.zeros((32, 6, 128), F32)], axis=1)
     came = exchange(sent, CTX)
-    state = jnp.zeros((8, 128), F32)
-    first, second = [], []
-    for i in range(32):
-        first.append(state)
-        state = came[i, 16:17] * state + came[i, :8]
-    for i in range(31, -1, -1):
-        second.append(state)
-        state = came[i, 17:18] * state + came[i, 8:16]
-    entering = jnp.stack(
-        [jnp.concatenate([a, b]) for a, b in zip(first, second[::-1])]
-    )
+    entering = pl.pallas_call(
+        scan,
+        out_shape=jax.ShapeDtypeStruct((32, 16, 128), F32),
+        in_specs=[VM],
+        out_specs=VM,
+        name="scan",
+    )(came)
     entering = exchange(entering, CTX)
     entering = jnp.transpose(entering.reshape(32, 2, 8, 128), (1, 0, 2, 3)).reshape(2, 1, 4, 64, 128)
 

time: 299 us -> 240 us (0.80)
  waiting for transfers between devices: 120 us -> 76.7 us
  other arithmetic: 27.7 us -> 3.04 us
  blocking collectives: 37.6 us -> 55.7 us
  matrix products: 18.9 us -> 5.17 us
  starting transfers between devices: 65 us -> 54.3 us
  Pallas kernels: 0 us -> 8.7 us
  local copies, waits for them, and re-layouts: 14.6 us -> 20.4 us
    ppermute x5, waiting for transfers between devices: 54.8 us -> 8.35 us  [swap(): return lax.ppermute(value, axis, [(0, 1), (1, 0)])]
    unnamed x30 -> x0, other arithmetic: 17.9 us -> none
    all_to_all x5, starting transfers between devices: 47.6 us -> 32.7 us  [exchange(): return lax.all_to_all(value, axes, split_axis=0, concat_axis=0, tiled=True)]
    dot_general x3 -> x0, matrix products: 13.7 us -> none  [the longest x1 6.03 us: body(): jnp.einsum('hqd,kd->hqk', four_q, keys, preferred_element_type=F32)]
    all_gather x1, blocking collectives: 16.5 us -> 27.3 us  [body(): both = lax.all_gather(both, ZH, axis=0, tiled=True)]
    unnamed x26 -> x41, local copies, waits for them, and re-layouts: 5.98 us -> 15.6 us
    pallas_call x0 -> x3, Pallas kernels: none -> 8.7 us  [the longest x1 4.91 us: body(): pl.pallas_call(attend, out_shape=jax.ShapeDtypeStruct((4, 528, 128), BF),...]
    all_gather x1, blocking collectives: 8.45 us -> 15.2 us  [body(): lax.all_gather(both[:, 0], 'co', axis=0, tiled=True).reshape(2048, 128)]
  transfers between devices with their start and end apart: 12 -> 12, of which waited for: 8 -> 6; matrix products, arithmetic and copies ran while one was open for 11% -> 7% of each run, Pallas kernels for 0% -> 3%
where the time goes in v2:
time: 240 us; the launch traced here: 239 us
  waiting for transfers between devices  76.7 us (32%)
  blocking collectives  55.7 us (23%)
  starting transfers between devices  54.3 us (23%)
  local copies, waits for them, and re-layouts  20.4 us (8%)
  between operations  14.7 us (6%)
  Pallas kernels  8.7 us (4%)
  matrix products  5.17 us (2%)
  other arithmetic  3.04 us (1%)
    all_to_all x5, waiting for transfers between devices, exchange(): return lax.all_to_all(value, axes, split_axis=0, concat_axis=0, tiled=True)  68.3 us
    all_to_all x5, starting transfers between devices, exchange(): return lax.all_to_all(value, axes, split_axis=0, concat_axis=0, tiled=True)  32.7 us
    all_gather x1, blocking collectives, body(): both = lax.all_gather(both, ZH, axis=0, tiled=True)  27.3 us
    ppermute x5, starting transfers between devices, swap(): return lax.ppermute(value, axis, [(0, 1), (1, 0)])  20.8 us
    unnamed x41, local copies, waits for them, and re-layouts  15.6 us
    all_gather x1, blocking collectives, body(): lax.all_gather(both[:, 0], 'co', axis=0, tiled=True).reshape(2048, 128)  15.2 us
    all_gather x1, blocking collectives, body(): both = lax.all_gather(both, 'x', axis=0, tiled=True)  11 us
    ppermute x5, waiting for transfers between devices, swap(): return lax.ppermute(value, axis, [(0, 1), (1, 0)])  8.35 us
  transfers between devices with their start and end apart: 12, of which 6 were waited for; matrix products, arithmetic and copies ran while one was open for 7% of the time, Pallas kernels for 3%

profile of v2, /device:TPU:1, one launch (start us, length us, event | category | flops | bytes accessed | tf_op | source)
XLA Modules:
  0.0 238.6 jit_solution(15464143465809932212)
XLA Ops:
  11.4 0.9 dynamic-slice_dynamic-update-slice_fusion.6
  12.3 0.9 dynamic-slice_dynamic-update-slice_fusion.5
  13.2 0.9 dynamic-slice_dynamic-update-slice_fusion.4
  14.1 0.9 dynamic-slice_dynamic-update-slice_fusion.3
  15.0 0.9 dynamic-slice_dynamic-update-slice_fusion.2
  15.9 0.9 dynamic-slice_dynamic-update-slice_fusion.1
  16.8 0.9 dynamic-slice_dynamic-update-slice_fusion
  17.7 11.4 %collective-permute-start.1 = (bf16[128,2048]{1,0:T(8,128)(2,1)S(1)}, bf16[128,2048]{1,0:T(8,128)(2,1)S(1)}, u32[]{:S(2)}, u32[]{:S(2)}) collective-permute-start(bf16[128,2048]{1,0:T(8,128)(2,1)S(1)} %get-tuple-element.23), channel_id=1, source_target_pairs={{0,1},{1,0},{2,3},{3,2},{4,5},{5,4},{6,7},{7,6},{8,9},{9,8},{10,11... | collective-permute-start | bytes 1572872 | tf_op jit(solution)/shard_map/ppermute | solution.py:41
  29.1 1.9 collective-permute-start
  31.3 27.3 %all-gather = bf16[8,64,128]{2,1,0:T(8,128)(2,1)S(1)} all-gather(bf16[2,64,128]{2,1,0:T(8,128)(2,1)S(1)} %pad_maximum_fusion.3), channel_id=2, replica_groups=mesh['x'=4,'zhh'=2,'zhl'=2,'co'=2,'yhi'=4,'ylo'=2,'zl'=2] {'zhh','zhl'}, dimensions={0}, use_global_device_ids=true | all-gather | bytes 163840 | tf_op jit(solution)/shard_map/all_gather | solution.py:190
  58.6 3.2 %collective-permute-start.2 = (bf16[2,256,128]{2,1,0:T(8,128)(2,1)S(1)}, bf16[2,256,128]{2,1,0:T(8,128)(2,1)S(1)}, u32[]{:S(2)}, u32[]{:S(2)}) collective-permute-start(bf16[2,256,128]{2,1,0:T(8,128)(2,1)S(1)} %maximum_select_fusion.1), channel_id=1, source_target_pairs={{0,2},{2,0},{1,3},{3,1},{4,6},{6,4},{5,7},{7,5},{8,10},{10,8},{9,1... | collective-permute-start | bytes 393224 | tf_op jit(solution)/shard_map/ppermute | solution.py:41
  61.9 2.1 collective-permute-start.3
  64.0 11.0 %all_gather.16 = bf16[16,2,64,128]{3,2,1,0:T(8,128)(2,1)S(1)} all-gather(bf16[4,2,64,128]{3,2,1,0:T(8,128)(2,1)S(1)} %bitcast.141), channel_id=1, replica_groups=mesh['x'=4,'zhh'=2,'zhl'=2,'co'=2,'yhi'=4,'ylo'=2,'zl'=2] {'x'}, dimensions={0}, use_global_device_ids=true | all-gather | bytes 655360 | tf_op jit(solution)/shard_map/all_gather | solution.py:198
  75.1 15.2 %all-gather.1 = bf16[32,1,64,128]{3,2,1,0:T(8,128)(2,1)S(1)} all-gather(bf16[16,1,64,128]{3,2,1,0:T(8,128)(2,1)S(1)} %get-tuple-element.41), channel_id=3, replica_groups=mesh['x'=4,'zhh'=2,'zhl'=2,'co'=2,'yhi'=4,'ylo'=2,'zl'=2] {'co'}, dimensions={0}, use_global_device_ids=true | all-gather | bytes 786432 | tf_op jit(solution)/shard_map/all_gather | solution.py:199
  90.3 2.2 all-gather.2
  92.5 4.9 %attend.1 = bf16[4,528,128]{2,1,0:T(8,128)(2,1)} custom-call(s32[2]{0:T(128)S(1)} %pad_add_fusion.spots, bf16[4,256,128]{2,1,0:T(8,128)(2,1)S(1)} %maximum_select_fusion.q_ref, bf16[2048,128]{1,0:T(8,128)(2,1)S(1)} %bitcast.125, bf16[2048,128]{1,0:T(8,128)(2,1)S(1)} %bitcast.126), custom_call_target="tpu_custom_call" | custom-call | tf_op jit(solution)/shard_map/attend/pallas_call | solution.py:207
  97.4 3.5 %all-to-all-start = ((bf16[4,528,128]{2,1,0:T(8,128)(2,1)}), bf16[4,528,128]{2,1,0:T(8,128)(2,1)S(1)}, u32[]{:S(2)}, u32[]{:S(2)}) async-start(bf16[4,528,128]{2,1,0:T(8,128)(2,1)} %attend.1), calls=%async_computation | async-start | bytes 1081344 | tf_op jit(solution)/shard_map/all_to_all | solution.py:45
  101.7 7.4 %all-to-all-done.came_ref = bf16[4,528,128]{2,1,0:T(8,128)(2,1)S(1)} async-done(((bf16[4,528,128]{2,1,0:T(8,128)(2,1)}), bf16[4,528,128]{2,1,0:T(8,128)(2,1)S(1)}, u32[]{:S(2)}, u32[]{:S(2)}) %all-to-all-start) | async-done | bytes 540704 | tf_op jit(solution)/shard_map/all_to_all | solution.py:45
  109.1 1.9 project.1
  111.0 6.6 %all-to-all-start.1 = ((bf16[4,32,2048]{2,1,0:T(8,128)(2,1)}), bf16[4,32,2048]{2,1,0:T(8,128)(2,1)S(1)}, u32[]{:S(2)}, u32[]{:S(2)}) async-start(bf16[4,32,2048]{2,1,0:T(8,128)(2,1)} %bitcast.15), calls=%async_computation.1 | async-start | bytes 1048576 | tf_op jit(solution)/shard_map/all_to_all | solution.py:45
  123.5 5.1 %all-to-all-done.1 = bf16[4,32,2048]{2,1,0:T(8,128)(2,1)S(1)} async-done(((bf16[4,32,2048]{2,1,0:T(8,128)(2,1)}), bf16[4,32,2048]{2,1,0:T(8,128)(2,1)S(1)}, u32[]{:S(2)}, u32[]{:S(2)}) %all-to-all-start.1) | async-done | bytes 524320 | tf_op jit(solution)/shard_map/all_to_all | solution.py:45
  128.8 1.1 broadcast_in_dim.48
  129.9 8.3 %all-to-all-start.2 = ((bf16[8,32,2048]{2,1,0:T(8,128)(2,1)}), bf16[8,32,2048]{2,1,0:T(8,128)(2,1)S(1)}, u32[]{:S(2)}, u32[]{:S(2)}) async-start(bf16[8,32,2048]{2,1,0:T(8,128)(2,1)} %broadcast_in_dim.48), calls=%async_computation.2 | async-start | bytes 2097152 | tf_op jit(solution)/shard_map/all_to_all | solution.py:45
  138.3 29.1 %all-to-all-done.2 = bf16[8,32,2048]{2,1,0:T(8,128)(2,1)S(1)} async-done(((bf16[8,32,2048]{2,1,0:T(8,128)(2,1)}), bf16[8,32,2048]{2,1,0:T(8,128)(2,1)S(1)}, u32[]{:S(2)}, u32[]{:S(2)}) %all-to-all-start.2) | async-done | bytes 1048608 | tf_op jit(solution)/shard_map/all_to_all | solution.py:45
  167.9 3.5 %fusion.68 = f32[2,512,256]{2,1,0:T(8,128)S(1)} fusion(bf16[2,2048,512]{2,1,0:T(8,128)(2,1)} %bitcast.157, bf16[256,2048,1]{1,0,2:T(8,128)(2,1)S(1)} %bitcast.136), kind=kOutput, calls=%fused_computation.142 | convolution fusion | flops 1073741824 | bytes 6291456 | tf_op jit(solution)/shard_map/tk,zkn->ztn/dot_general | solution.py:238
  171.7 2.2 collective-permute-start.5
  174.0 8.3 %collective-permute-done.5 = bf16[256,640]{0,1:T(8,128)(2,1)S(1)} collective-permute-done((bf16[256,640]{0,1:T(8,128)(2,1)S(1)}, bf16[256,640]{0,1:T(8,128)(2,1)S(1)}, u32[]{:S(2)}, u32[]{:S(2)}) %collective-permute-start.5) | collective-permute-done | bytes 327712 | tf_op jit(solution)/shard_map/ppermute | solution.py:41
  184.7 9.5 %all-to-all-start.3 = ((f32[32,24,128]{2,1,0:T(8,128)}), f32[32,24,128]{2,1,0:T(8,128)S(1)}, u32[]{:S(2)}, u32[]{:S(2)}) async-start(f32[32,24,128]{2,1,0:T(8,128)} %maximum_maximum_fusion), calls=%async_computation.3 | async-start | bytes 786432 | tf_op jit(solution)/shard_map/all_to_all | solution.py:45
  194.3 15.4 %all-to-all-done.3.came_ref = f32[32,24,128]{2,1,0:T(8,128)S(1)} async-done(((f32[32,24,128]{2,1,0:T(8,128)}), f32[32,24,128]{2,1,0:T(8,128)S(1)}, u32[]{:S(2)}, u32[]{:S(2)}) %all-to-all-start.3) | async-done | bytes 393248 | tf_op jit(solution)/shard_map/all_to_all | solution.py:45
  210.4 1.8 scan.1
  212.3 4.8 %all-to-all-start.4 = ((f32[32,16,128]{2,1,0:T(8,128)}), f32[32,16,128]{2,1,0:T(8,128)S(1)}, u32[]{:S(2)}, u32[]{:S(2)}) async-start(f32[32,16,128]{2,1,0:T(8,128)} %scan.1), calls=%async_computation.4 | async-start | bytes 524288 | tf_op jit(solution)/shard_map/all_to_all | solution.py:45
  218.6 11.3 %all-to-all-done.4 = f32[32,16,128]{2,1,0:T(8,128)S(1)} async-done(((f32[32,16,128]{2,1,0:T(8,128)}), f32[32,16,128]{2,1,0:T(8,128)S(1)}, u32[]{:S(2)}, u32[]{:S(2)}) %all-to-all-start.4) | async-done | bytes 262176 | tf_op jit(solution)/shard_map/all_to_all | solution.py:45
  (107 shorter events, 18.5 us)
Async XLA Ops:
  7.2 1.0 copy-start
  7.2 21.9 %copy-start.5 = (bf16[256,128]{1,0:T(8,128)(2,1)S(1)}, bf16[256,128]{1,0:T(8,128)(2,1)}, u32[]{:S(2)}) copy-start(bf16[256,128]{1,0:T(8,128)(2,1)} %param.12) | copy-start | bytes 196612
  7.2 23.9 %copy-start.2 = (bf16[256,4,128]{2,1,0:T(4,128)(2,1)S(1)}, bf16[256,4,128]{2,1,0:T(4,128)(2,1)}, u32[]{:S(2)}) copy-start(bf16[256,4,128]{2,1,0:T(4,128)(2,1)} %param.14) | copy-start | bytes 786436
  7.2 23.9 %copy-start.3 = (bf16[256,4,128]{2,1,0:T(4,128)(2,1)S(1)}, bf16[256,4,128]{2,1,0:T(4,128)(2,1)}, u32[]{:S(2)}) copy-start(bf16[256,4,128]{2,1,0:T(4,128)(2,1)} %param.13) | copy-start | bytes 786436
  7.2 160.7 %all-gather.5.cloned.1.call-start = ((), (), s32[]{:S(2)}) async-start(), calls=%async_computation.5 | async-start | bytes 4325376 | tf_op jit(solution)/shard_map/all_gather | solution.py:173
  9.2 0.7 collective-permute-start.4
  9.9 0.7 copy-start.4
  17.7 40.9 %collective-permute-start.1 = (bf16[128,2048]{1,0:T(8,128)(2,1)S(1)}, bf16[128,2048]{1,0:T(8,128)(2,1)S(1)}, u32[]{:S(2)}, u32[]{:S(2)}) collective-permute-start(bf16[128,2048]{1,0:T(8,128)(2,1)S(1)} %get-tuple-element.23), channel_id=1, source_target_pairs={{0,1},{1,0},{2,3},{3,2},{4,5},{5,4},{6,7},{7,6},{8,9},{9,8},{10,11... | collective-permute-start | bytes 1572872 | tf_op jit(solution)/shard_map/ppermute | solution.py:41
  29.1 29.5 %collective-permute-start = (bf16[256,128]{1,0:T(8,128)(2,1)S(1)}, bf16[256,128]{1,0:T(8,128)(2,1)S(1)}, u32[]{:S(2)}, u32[]{:S(2)}) collective-permute-start(bf16[256,128]{1,0:T(8,128)(2,1)S(1)} %bitcast.144), channel_id=1, source_target_pairs={{0,1},{1,0},{2,3},{3,2},{4,5},{5,4},{6,7},{7,6},{8,9},{9,8},{10,11... | collective-permute-start | bytes 196616 | tf_op jit(solution)/shard_map/ppermute | solution.py:41
  58.6 33.8 %collective-permute-start.2 = (bf16[2,256,128]{2,1,0:T(8,128)(2,1)S(1)}, bf16[2,256,128]{2,1,0:T(8,128)(2,1)S(1)}, u32[]{:S(2)}, u32[]{:S(2)}) collective-permute-start(bf16[2,256,128]{2,1,0:T(8,128)(2,1)S(1)} %maximum_select_fusion.1), channel_id=1, source_target_pairs={{0,2},{2,0},{1,3},{3,1},{4,6},{6,4},{5,7},{7,5},{8,10},{10,8},{9,1... | collective-permute-start | bytes 393224 | tf_op jit(solution)/shard_map/ppermute | solution.py:41
  61.9 47.2 %collective-permute-start.3 = (bf16[256,2048]{1,0:T(8,128)(2,1)S(1)}, bf16[256,2048]{1,0:T(8,128)(2,1)S(1)}, u32[]{:S(2)}, u32[]{:S(2)}) collective-permute-start(bf16[256,2048]{1,0:T(8,128)(2,1)S(1)} %pad_maximum_fusion.own_ref), channel_id=1, source_target_pairs={{0,2},{2,0},{1,3},{3,1},{4,6},{6,4},{5,7},{7,5},{8,10},{10,8},{9,1... | collective-permute-start | bytes 3145736 | tf_op jit(solution)/shard_map/ppermute | solution.py:41
  97.4 11.7 %all-to-all-start = ((bf16[4,528,128]{2,1,0:T(8,128)(2,1)}), bf16[4,528,128]{2,1,0:T(8,128)(2,1)S(1)}, u32[]{:S(2)}, u32[]{:S(2)}) async-start(bf16[4,528,128]{2,1,0:T(8,128)(2,1)} %attend.1), calls=%async_computation | async-start | bytes 1081344 | tf_op jit(solution)/shard_map/all_to_all | solution.py:45
  111.0 17.6 %all-to-all-start.1 = ((bf16[4,32,2048]{2,1,0:T(8,128)(2,1)}), bf16[4,32,2048]{2,1,0:T(8,128)(2,1)S(1)}, u32[]{:S(2)}, u32[]{:S(2)}) async-start(bf16[4,32,2048]{2,1,0:T(8,128)(2,1)} %bitcast.15), calls=%async_computation.1 | async-start | bytes 1048576 | tf_op jit(solution)/shard_map/all_to_all | solution.py:45
  128.7 9.5 %copy-start.6 = (f32[4096]{0:T(1024)S(1)}, f32[4096]{0:T(1024)}, u32[]{:S(2)}) copy-start(f32[4096]{0:T(1024)} %param.17) | copy-start | bytes 49156
  129.9 37.5 %all-to-all-start.2 = ((bf16[8,32,2048]{2,1,0:T(8,128)(2,1)}), bf16[8,32,2048]{2,1,0:T(8,128)(2,1)S(1)}, u32[]{:S(2)}, u32[]{:S(2)}) async-start(bf16[8,32,2048]{2,1,0:T(8,128)(2,1)} %broadcast_in_dim.48), calls=%async_computation.2 | async-start | bytes 2097152 | tf_op jit(solution)/shard_map/all_to_all | solution.py:45
  171.4 2.6 %copy-start.8 = (f32[4]{0:T(128)S(1)}, f32[4]{0:T(128)}, u32[]{:S(2)}) copy-start(f32[4]{0:T(128)} %param.22) | copy-start | bytes 52
  171.4 11.0 %copy-start.7 = (f32[4]{0:T(128)S(1)}, f32[4]{0:T(128)}, u32[]{:S(2)}) copy-start(f32[4]{0:T(128)} %param.21) | copy-start | bytes 52
  171.7 10.7 %collective-permute-start.5 = (bf16[256,640]{0,1:T(8,128)(2,1)S(1)}, bf16[256,640]{0,1:T(8,128)(2,1)S(1)}, u32[]{:S(2)}, u32[]{:S(2)}) collective-permute-start(bf16[256,640]{0,1:T(8,128)(2,1)S(1)} %pad_maximum_fusion.1), channel_id=1, source_target_pairs={{0,1},{1,0},{2,3},{3,2},{4,5},{5,4},{6,7},{7,6},{8,9},{9,8},{10,11... | collective-permute-start | bytes 983048 | tf_op jit(solution)/shard_map/ppermute | solution.py:41
  184.7 25.0 %all-to-all-start.3 = ((f32[32,24,128]{2,1,0:T(8,128)}), f32[32,24,128]{2,1,0:T(8,128)S(1)}, u32[]{:S(2)}, u32[]{:S(2)}) async-start(f32[32,24,128]{2,1,0:T(8,128)} %maximum_maximum_fusion), calls=%async_computation.3 | async-start | bytes 786432 | tf_op jit(solution)/shard_map/all_to_all | solution.py:45
  209.7 0.7 copy-start.1
  212.3 17.6 %all-to-all-start.4 = ((f32[32,16,128]{2,1,0:T(8,128)}), f32[32,16,128]{2,1,0:T(8,128)S(1)}, u32[]{:S(2)}, u32[]{:S(2)}) async-start(f32[32,16,128]{2,1,0:T(8,128)} %scan.1), calls=%async_computation.4 | async-start | bytes 524288 | tf_op jit(solution)/shard_map/all_to_all | solution.py:45
  217.8 12.5 %copy-start.9 = (f32[4]{0:T(128)S(1)}, f32[4]{0:T(128)}, u32[]{:S(2)}) copy-start(f32[4]{0:T(128)} %param.23) | copy-start | bytes 52
Sparse Core Ops, SparseCore 0:
  10.8 94.8 all-gather.4

commit v3 on v2

--- a/solution.py
+++ b/solution.py
@@ -52,27 +52,64 @@
     return first_term + jnp.einsum(form, lower, narrow, preferred_element_type=F32)
 
 
-def attend(spots, q_ref, k_ref, v_ref, out_ref):
-    ctx, quarter = spots[0], spots[1]
+def pick(spots, q_ref, w_hbm, home_ref, away_ref, rest_ref, sems):
+    zl, co = spots[2], spots[3]
+    copies = []
+    for at, (out_ref, side, half) in enumerate(
+        ((home_ref, zl, co), (away_ref, 1 - zl, co), (rest_ref, zl, 1 - co))
+    ):
+        for i in range(4):
+            start = pl.multiple_of(2048 * half + 512 * i + 256 * side, 256)
+            copies.append(
+                pltpu.make_async_copy(
+                    w_hbm.at[:, pl.ds(start, 256)],
+                    out_ref.at[:128, 256 * i : 256 * (i + 1)],
+                    sems.at[4 * at + i],
+                )
+            )
+    for copy in copies:
+        copy.start()
+    for i in range(8):
+        block = q_ref[32 * i : 32 * (i + 1)]
+        home_ref[128:, 128 * i : 128 * (i + 1)] = block
+        away_ref[128:, 128 * i : 128 * (i + 1)] = block
+    for copy in copies:
+        copy.wait()
+
+
+def attend(spots, home_ref, zl_ref, ylo_ref, both_ref, kv_ref, kv_co_ref, out_ref):
+    ctx, quarter, co = spots[0], spots[1], spots[3]
     lane = lax.broadcasted_iota(jnp.int32, (32, 256), 1)
     token = lane % 128 // 32 * 64 + lane // 128 * 32 + lane % 32
     seat = jnp.where(token < 128, ctx, 63 - ctx) * 128 + token % 128
-    reach = seat - lax.broadcasted_iota(jnp.int32, (32, 256), 0)
+    reach = seat - lax.broadcasted_iota(jnp.int32, (32, 256), 0) - 32 * quarter
+
+    def rows(chunk, start):
+        ref = kv_ref if chunk < 4 else kv_co_ref
+        first = chunk % 4 * 4
+        return jnp.concatenate([ref[first + i, start : start + 64] for i in range(4)])
+
     levels = []
     for head in range(4):
         tiles = []
+        query = jnp.concatenate(
+            [
+                (home_ref, zl_ref, ylo_ref, both_ref)[head][128:, 128 * i : 128 * (i + 1)]
+                for i in (0, 2, 4, 6, 1, 3, 5, 7)
+            ]
+        )
         for chunk in range(8):
             scores = lax.dot_general(
-                k_ref[256 * chunk : 256 * (chunk + 1)],
-                q_ref[head],
+                rows(chunk, 0),
+                query,
                 (((1,), (1,)), ((), ())),
                 preferred_element_type=F32,
             ) * (math.log2(math.e) / math.sqrt(128))
             for piece in range(8):
-                place = 4 * chunk + piece // 2
-                source = place % 16 * 2 + place // 16
+                core = co if chunk < 4 else 1 - co
+                source = (chunk % 4 * 4 + piece // 2) * 2 + core
                 block = source if piece % 2 == 0 else 63 - source
-                allowed = reach >= block * 128 + 32 * quarter
+                allowed = reach >= block * 128
                 tiles.append(
                     jnp.where(allowed, scores[32 * piece : 32 * (piece + 1)], LOWEST)
                 )
@@ -87,7 +124,7 @@
             for part in raised:
                 total = total + part
             summed = summed + lax.dot_general(
-                v_ref[256 * chunk : 256 * (chunk + 1)],
+                rows(chunk, 64),
                 jnp.concatenate(raised).astype(BF),
                 (((0,), (0,)), ((), ())),
                 preferred_element_type=F32,
@@ -105,29 +142,33 @@
         out_ref[dest, 512:528] = fine[:, 128 * half : 128 * half + 128]
 
 
-def project(spots, came_ref, own_ref, far_ref, out_ref, attended):
-    quarter = spots[1]
+def project(spots, came_ref, *refs):
+    quarter, co = spots[1], spots[3]
+    own_refs, rest_refs, out_ref, attended = refs[:4], refs[4:8], refs[8], refs[9]
     fine = [came_ref[source, 512:528].astype(F32) for source in range(4)]
     levels = [(part[8:12] + part[4:8]) + part[0:4] for part in fine]
-    top = jnp.maximum(jnp.maximum(levels[0], levels[1]), jnp.maximum(levels[2], levels[3]))
-    scales = [jnp.exp2(level - top) for level in levels]
-    total = (scales[0] + scales[1]) + (scales[2] + scales[3])
-    scales = [scale / total for scale in scales]
     for head in range(4):
+        level = [levels[s][head ^ s : (head ^ s) + 1] for s in range(4)]
+        top = jnp.maximum(jnp.maximum(level[0], level[1]), jnp.maximum(level[2], level[3]))
+        scales = [jnp.exp2(one - top) for one in level]
+        total = (scales[0] + scales[1]) + (scales[2] + scales[3])
         joined = jnp.zeros((128, 128), F32)
         for source in range(4):
-            joined = joined + scales[source][head : head + 1] * came_ref[
-                source, 128 * head : 128 * (head + 1)
+            slot = 128 * (head ^ source)
+            joined = joined + (scales[source] / total) * came_ref[
+                source, slot : slot + 128
             ].astype(F32)
         attended[head] = joined.astype(BF)
-    total = None
-    for far, w_ref in ((0, own_ref), (2, far_ref)):
-        pair = jnp.concatenate([attended[quarter ^ far], attended[quarter ^ far ^ 1]])
-        product = lax.dot_general(
-            pair, w_ref[...], (((0,), (0,)), ((), ())), preferred_element_type=F32
-        )
-        total = product if total is None else total + product
-    out_ref[...] = total.astype(BF)
+    four = jnp.concatenate([attended[quarter ^ r] for r in range(4)])
+
+    def times(w_refs):
+        rows = jnp.concatenate([w_ref[:128] for w_ref in w_refs])
+        return lax.dot_general(
+            four, rows, (((0,), (0,)), ((), ())), preferred_element_type=F32
+        ).astype(BF)
+
+    out_ref[:, pl.ds(pl.multiple_of(1024 * co, 1024), 1024)] = times(own_refs)
+    out_ref[:, pl.ds(pl.multiple_of(1024 * (1 - co), 1024), 1024)] = times(rest_refs)
 
 
 def scan(came_ref, out_ref):
@@ -142,6 +183,7 @@
 
 VM = pl.BlockSpec(memory_space=pltpu.VMEM)
 SM = pl.BlockSpec(memory_space=pltpu.SMEM)
+HB = pl.BlockSpec(memory_space=pl.ANY)
 
 
 def body(
@@ -170,58 +212,58 @@
         [x_proj, bc_half, jnp.pad(dt_proj, ((0, 0), (0, 124)))], axis=1
     )
     packed = lax.ppermute(packed, ("zhl", "zl"), [(0, 0), (1, 2), (2, 1), (3, 3)])
-    weights = lax.all_gather(packed, ("zhl", "x", "zhh", "co"), axis=0, tiled=True)
-    weights = weights.reshape(2, 2048, 512)
-
-    spots = jnp.stack([ctx, quarter]).astype(jnp.int32)
-
-    sorted_q = jnp.swapaxes(queries.reshape(4, 2, 32, 128), 0, 1).reshape(256, 128)
-    mine = features(out_proj, zl)
-    theirs = features(out_proj, 1 - zl)
+    spots = jnp.stack([ctx, quarter, zl, lax.axis_index("co")]).astype(jnp.int32)
+
+    home, away, rest = pl.pallas_call(
+        pick,
+        out_shape=(
+            jax.ShapeDtypeStruct((160, 1024), BF),
+            jax.ShapeDtypeStruct((160, 1024), BF),
+            jax.ShapeDtypeStruct((128, 1024), BF),
+        ),
+        in_specs=[SM, VM, HB],
+        out_specs=(VM, VM, VM),
+        scratch_shapes=[pltpu.SemaphoreType.DMA((12,))],
+        name="pick",
+    )(spots, queries, out_proj)
 
     def part(heads):
         return lax.dynamic_slice(
             heads.reshape(2, 128, 4, 128), (0, 32 * quarter, group, 0), (2, 32, 1, 128)
-        ).reshape(1, 64, 128)
-
-    both = jnp.concatenate([part(key_heads), part(head_values)])[None]
-    other_q = swap(sorted_q, "zl")
-    other_w = swap(theirs, "zl")
-    both = lax.all_gather(both, ZH, axis=0, tiled=True)
-    both, other_q, other_w = lax.optimization_barrier((both, other_q, other_w))
-    pair_q = jnp.where(
-        zl == 0, jnp.stack([sorted_q, other_q]), jnp.stack([other_q, sorted_q])
-    )
-    pair_w = jnp.concatenate([mine, other_w])
-    far_q = swap(pair_q, "ylo")
-    far_w = swap(pair_w, "ylo")
-    both = lax.all_gather(both, "x", axis=0, tiled=True)
-    keys = lax.all_gather(both[:, 0], "co", axis=0, tiled=True).reshape(2048, 128)
-    values = lax.all_gather(both[:, 1], "co", axis=0, tiled=True).reshape(2048, 128)
-    four_q = jnp.where(
-        ylo == 0,
-        jnp.concatenate([pair_q, far_q]),
-        jnp.concatenate([far_q, pair_q]),
-    )
+        ).reshape(64, 128)
+
+    both = jnp.concatenate([part(key_heads), part(head_values)])
+    both = jnp.broadcast_to(both, (16, 128, 128)).reshape(2048, 128)
+    both = exchange(both, ("x", "zhh", "zhl")).reshape(16, 128, 128)
+    near = [
+        swap(away, "zl"),
+        swap(home, "ylo"),
+        lax.ppermute(away, ("ylo", "zl"), [(0, 3), (1, 2), (2, 1), (3, 0)]),
+    ]
+    both, near, packed = lax.optimization_barrier((both, near, packed))
+    both_co = swap(both, "co")
+    weights = lax.all_gather(packed, ("zhl", "x", "zhh", "co"), axis=0, tiled=True)
+    weights = weights.reshape(2, 2048, 512)
+    near_co = [swap(part, "co") for part in near]
 
     sent = pl.pallas_call(
         attend,
         out_shape=jax.ShapeDtypeStruct((4, 528, 128), BF),
-        in_specs=[SM, VM, VM, VM],
+        in_specs=[SM] + [VM] * 6,
         out_specs=VM,
         compiler_params=pltpu.CompilerParams(vmem_limit_bytes=32 << 20),
         name="attend",
-    )(spots, four_q, keys, values)
+    )(spots, home, *near, both, both_co)
     came = exchange(sent.reshape(4 * 528, 128), ("ylo", "zl")).reshape(4, 528, 128)
     head_part = pl.pallas_call(
         project,
         out_shape=jax.ShapeDtypeStruct((128, 2048), BF),
-        in_specs=[SM, VM, VM, VM],
+        in_specs=[SM] + [VM] * 9,
         out_specs=VM,
         scratch_shapes=[pltpu.VMEM((4, 128, 128), BF)],
         compiler_params=pltpu.CompilerParams(vmem_limit_bytes=32 << 20),
         name="project",
-    )(spots, came, pair_w, far_w)
+    )(spots, came, home, *near, rest, *near_co)
 
     parts = exchange(head_part, "yhi").reshape(4, 32, 2048)
     attention_sum = jnp.sum(parts.astype(F32), axis=0)

time: 240 us -> 209 us (0.87)
  blocking collectives: 55.7 us -> 0 us
  waiting for transfers between devices: 76.7 us -> 90 us
  starting transfers between devices: 54.3 us -> 67 us
  local copies, waits for them, and re-layouts: 20.4 us -> 16.4 us
  Pallas kernels: 8.7 us -> 11.9 us
    all_gather x4 -> x0, blocking collectives: 55.7 us -> none  [the longest x1 27.3 us: body(): both = lax.all_gather(both, ZH, axis=0, tiled=True)]
    ppermute x5 -> x7, waiting for transfers between devices: 8.35 us -> 23.3 us  [swap(): return lax.ppermute(value, axis, [(0, 1), (1, 0)])]
    all_to_all x5 -> x6, starting transfers between devices: 32.7 us -> 44.3 us  [exchange(): return lax.all_to_all(value, axes, split_axis=0, concat_axis=0, tiled=True)]
    unnamed x41 -> x42, local copies, waits for them, and re-layouts: 15.6 us -> 11.6 us
    ppermute x0 -> x1, starting transfers between devices: none -> 3.19 us  [body(): lax.ppermute(away, ('ylo', 'zl'), [(0, 3), (1, 2), (2, 1), (3, 0)])]
    pallas_call x0 -> x1, Pallas kernels: none -> 3.07 us  [body(): pl.pallas_call(pick, out_shape=(jax.ShapeDtypeStruct((160, 1024), BF), ja...]
    ppermute x5 -> x7, starting transfers between devices: 20.8 us -> 18.6 us  [swap(): return lax.ppermute(value, axis, [(0, 1), (1, 0)])]
    all_to_all x5 -> x6, waiting for transfers between devices: 68.3 us -> 66.7 us  [exchange(): return lax.all_to_all(value, axes, split_axis=0, concat_axis=0, tiled=True)]
  transfers between devices with their start and end apart: 12 -> 16, of which waited for: 6 -> 10; matrix products, arithmetic and copies ran while one was open for 7% -> 5% of each run, Pallas kernels for 3% -> 5%
where the time goes in v3:
time: 209 us; the launch traced here: 208 us
  waiting for transfers between devices  90 us (43%)
  starting transfers between devices  67 us (32%)
  local copies, waits for them, and re-layouts  16.4 us (8%)
  between operations  14.6 us (7%)
  Pallas kernels  11.9 us (6%)
  matrix products  5.16 us (2%)
  other arithmetic  2.66 us (1%)
    all_to_all x6, waiting for transfers between devices, exchange(): return lax.all_to_all(value, axes, split_axis=0, concat_axis=0, tiled=True)  66.7 us
    all_to_all x6, starting transfers between devices, exchange(): return lax.all_to_all(value, axes, split_axis=0, concat_axis=0, tiled=True)  44.3 us
    ppermute x7, waiting for transfers between devices, swap(): return lax.ppermute(value, axis, [(0, 1), (1, 0)])  23.3 us
    ppermute x7, starting transfers between devices, swap(): return lax.ppermute(value, axis, [(0, 1), (1, 0)])  18.6 us
    unnamed x42, local copies, waits for them, and re-layouts  11.6 us
    pallas_call x1, Pallas kernels, body(): pl.pallas_call(attend, out_shape=jax.ShapeDtypeStruct((4, 528, 128), BF),...  4.97 us
  transfers between devices with their start and end apart: 16, of which 10 were waited for; matrix products, arithmetic and copies ran while one was open for 5% of the time, Pallas kernels for 5%

profile of v3, /device:TPU:1, one launch (start us, length us, event | category | flops | bytes accessed | tf_op | source)
XLA Modules:
  0.0 207.7 jit_solution(16420028375291614679)
XLA Ops:
  7.2 1.0 copy.55
  8.3 1.0 copy.54
  9.3 0.9 broadcast_in_dim.47
  10.2 13.4 %all-to-all-start = ((bf16[16,128,128]{2,1,0:T(8,128)(2,1)}), bf16[16,128,128]{2,1,0:T(8,128)(2,1)S(1)}, u32[]{:S(2)}, u32[]{:S(2)}) async-start(bf16[16,128,128]{2,1,0:T(8,128)(2,1)} %broadcast_in_dim.47), calls=%async_computation | async-start | bytes 1048576 | tf_op jit(solution)/shard_map/all_to_all | solution.py:45
  24.3 3.1 %pick.1 = (bf16[160,1024]{1,0:T(8,128)(2,1)}, bf16[160,1024]{1,0:T(8,128)(2,1)}, bf16[128,1024]{1,0:T(8,128)(2,1)}) custom-call(s32[4]{0:T(128)} %pad_add_fusion.spots, bf16[256,128]{1,0:T(8,128)(2,1)} %q_ref.1, bf16[128,4096]{1,0:T(8,128)(2,1)} %w_hbm.1), custom_call_target="tpu_custom_call" | custom-call | tf_op jit(solution)/shard_map/pick/pallas_call | solution.py:217
  27.4 3.1 %collective-permute-start = (bf16[160,1024]{1,0:T(8,128)(2,1)}, bf16[160,1024]{1,0:T(8,128)(2,1)S(1)}, u32[]{:S(2)}, u32[]{:S(2)}) collective-permute-start(bf16[160,1024]{1,0:T(8,128)(2,1)} %get-tuple-element.11), channel_id=1, source_target_pairs={{0,1},{1,0},{2,3},{3,2},{4,5},{5,4},{6,7},{7,6},{8,9},{9,8},{10,11... | collective-permute-start | bytes 983048 | tf_op jit(solution)/shard_map/ppermute | solution.py:41
  30.5 3.2 %collective-permute-start.2 = (bf16[160,1024]{1,0:T(8,128)(2,1)}, bf16[160,1024]{1,0:T(8,128)(2,1)S(1)}, u32[]{:S(2)}, u32[]{:S(2)}) collective-permute-start(bf16[160,1024]{1,0:T(8,128)(2,1)} %get-tuple-element.11), channel_id=1, source_target_pairs={{0,3},{1,2},{2,1},{3,0},{4,7},{5,6},{6,5},{7,4},{8,11},{9,10},{10,... | collective-permute-start | bytes 983048 | tf_op jit(solution)/shard_map/ppermute | solution.py:241
  33.7 2.1 %collective-permute-start.1 = (bf16[160,1024]{1,0:T(8,128)(2,1)}, bf16[160,1024]{1,0:T(8,128)(2,1)S(1)}, u32[]{:S(2)}, u32[]{:S(2)}) collective-permute-start(bf16[160,1024]{1,0:T(8,128)(2,1)} %get-tuple-element.10.home_ref.refs_0_), channel_id=1, source_target_pairs={{0,2},{2,0},{1,3},{3,1},{4,6},{6,4},{5,7},{7,5},{8,10},{10,8},{9,1... | collective-permute-start | bytes 983048 | tf_op jit(solution)/shard_map/ppermute | solution.py:41
  37.0 13.3 %collective-permute-done.zl_ref.refs_1_ = bf16[160,1024]{1,0:T(8,128)(2,1)S(1)} collective-permute-done((bf16[160,1024]{1,0:T(8,128)(2,1)}, bf16[160,1024]{1,0:T(8,128)(2,1)S(1)}, u32[]{:S(2)}, u32[]{:S(2)}) %collective-permute-start) | collective-permute-done | bytes 327712 | tf_op jit(solution)/shard_map/ppermute | solution.py:41
  50.9 3.9 %collective-permute-start.4 = (bf16[16,128,128]{2,1,0:T(8,128)(2,1)S(1)}, bf16[16,128,128]{2,1,0:T(8,128)(2,1)S(1)}, u32[]{:S(2)}, u32[]{:S(2)}) collective-permute-start(bf16[16,128,128]{2,1,0:T(8,128)(2,1)S(1)} %all-to-all-done.kv_ref), channel_id=1, source_target_pairs={{0,16},{16,0},{1,17},{17,1},{2,18},{18,2},{3,19},{19,3},{4,20},{20... | collective-permute-start | bytes 1572872 | tf_op jit(solution)/shard_map/ppermute | solution.py:41
  54.8 1.5 collective-permute-done.4.kv_co_ref
  56.3 1.0 copy-done.1
  57.9 5.0 %attend.1 = bf16[4,528,128]{2,1,0:T(8,128)(2,1)} custom-call(s32[4]{0:T(128)S(1)} %copy-done.4, bf16[160,1024]{1,0:T(8,128)(2,1)S(1)} %copy-done.1, bf16[160,1024]{1,0:T(8,128)(2,1)S(1)} %collective-permute-done.zl_ref.refs_1_, bf16[160,1024]{1,0:T(8,128)(2,1)S(1)} %collective-permute-done.1.ylo_ref.refs_2_, ...), custom_call_target="tpu_custom_call" | custom-call | tf_op jit(solution)/shard_map/attend/pallas_call | solution.py:249
  62.9 3.5 %all-to-all-start.1 = ((bf16[4,528,128]{2,1,0:T(8,128)(2,1)}), bf16[4,528,128]{2,1,0:T(8,128)(2,1)S(1)}, u32[]{:S(2)}, u32[]{:S(2)}) async-start(bf16[4,528,128]{2,1,0:T(8,128)(2,1)} %attend.1), calls=%async_computation.1 | async-start | bytes 1081344 | tf_op jit(solution)/shard_map/all_to_all | solution.py:45
  66.4 2.3 %collective-permute-start.5 = (bf16[160,1024]{1,0:T(8,128)(2,1)S(1)}, bf16[160,1024]{1,0:T(8,128)(2,1)S(1)}, u32[]{:S(2)}, u32[]{:S(2)}) collective-permute-start(bf16[160,1024]{1,0:T(8,128)(2,1)S(1)} %collective-permute-done.zl_ref.refs_1_), channel_id=1, source_target_pairs={{0,16},{16,0},{1,17},{17,1},{2,18},{18,2},{3,19},{19,3},{4,20},{20... | collective-permute-start | bytes 983048 | tf_op jit(solution)/shard_map/ppermute | solution.py:41
  68.7 2.0 collective-permute-start.6
  70.7 2.3 %collective-permute-start.7 = (bf16[160,1024]{1,0:T(8,128)(2,1)S(1)}, bf16[160,1024]{1,0:T(8,128)(2,1)S(1)}, u32[]{:S(2)}, u32[]{:S(2)}) collective-permute-start(bf16[160,1024]{1,0:T(8,128)(2,1)S(1)} %collective-permute-done.2.both_ref.refs_3_), channel_id=1, source_target_pairs={{0,16},{16,0},{1,17},{17,1},{2,18},{18,2},{3,19},{19,3},{4,20},{20... | collective-permute-start | bytes 983048 | tf_op jit(solution)/shard_map/ppermute | solution.py:41
  74.2 2.3 %all-to-all-done.1.came_ref = bf16[4,528,128]{2,1,0:T(8,128)(2,1)S(1)} async-done(((bf16[4,528,128]{2,1,0:T(8,128)(2,1)}), bf16[4,528,128]{2,1,0:T(8,128)(2,1)S(1)}, u32[]{:S(2)}, u32[]{:S(2)}) %all-to-all-start.1) | async-done | bytes 540704 | tf_op jit(solution)/shard_map/all_to_all | solution.py:45
  76.5 2.0 project.1
  78.5 7.8 %all-to-all-start.2 = ((bf16[4,32,2048]{2,1,0:T(8,128)(2,1)}), bf16[4,32,2048]{2,1,0:T(8,128)(2,1)S(1)}, u32[]{:S(2)}, u32[]{:S(2)}) async-start(bf16[4,32,2048]{2,1,0:T(8,128)(2,1)} %bitcast.9), calls=%async_computation.2 | async-start | bytes 1048576 | tf_op jit(solution)/shard_map/all_to_all | solution.py:45
  92.1 8.6 %all-to-all-done.2 = bf16[4,32,2048]{2,1,0:T(8,128)(2,1)S(1)} async-done(((bf16[4,32,2048]{2,1,0:T(8,128)(2,1)}), bf16[4,32,2048]{2,1,0:T(8,128)(2,1)S(1)}, u32[]{:S(2)}, u32[]{:S(2)}) %all-to-all-start.2) | async-done | bytes 524320 | tf_op jit(solution)/shard_map/all_to_all | solution.py:45
  100.9 1.1 broadcast_in_dim.48
  102.0 4.8 %all-to-all-start.3 = ((bf16[8,32,2048]{2,1,0:T(8,128)(2,1)}), bf16[8,32,2048]{2,1,0:T(8,128)(2,1)S(1)}, u32[]{:S(2)}, u32[]{:S(2)}) async-start(bf16[8,32,2048]{2,1,0:T(8,128)(2,1)} %broadcast_in_dim.48), calls=%async_computation.3 | async-start | bytes 2097152 | tf_op jit(solution)/shard_map/all_to_all | solution.py:45
  106.9 29.1 %all-to-all-done.3 = bf16[8,32,2048]{2,1,0:T(8,128)(2,1)S(1)} async-done(((bf16[8,32,2048]{2,1,0:T(8,128)(2,1)}), bf16[8,32,2048]{2,1,0:T(8,128)(2,1)S(1)}, u32[]{:S(2)}, u32[]{:S(2)}) %all-to-all-start.3) | async-done | bytes 1048608 | tf_op jit(solution)/shard_map/all_to_all | solution.py:45
  136.5 3.5 %fusion.67 = f32[2,512,256]{2,1,0:T(8,128)S(1)} fusion(bf16[2,2048,512]{2,1,0:T(8,128)(2,1)} %bitcast.142, bf16[256,2048,1]{1,0,2:T(8,128)(2,1)S(1)} %bitcast.126), kind=kOutput, calls=%fused_computation.122 | convolution fusion | flops 1073741824 | bytes 6291456 | tf_op jit(solution)/shard_map/tk,zkn->ztn/dot_general | solution.py:280
  140.3 3.0 %collective-permute-start.8 = (bf16[256,640]{0,1:T(8,128)(2,1)S(1)}, bf16[256,640]{0,1:T(8,128)(2,1)S(1)}, u32[]{:S(2)}, u32[]{:S(2)}) collective-permute-start(bf16[256,640]{0,1:T(8,128)(2,1)S(1)} %pad_maximum_fusion), channel_id=1, source_target_pairs={{0,1},{1,0},{2,3},{3,2},{4,5},{5,4},{6,7},{7,6},{8,9},{9,8},{10,11... | collective-permute-start | bytes 983048 | tf_op jit(solution)/shard_map/ppermute | solution.py:41
  143.3 7.6 %collective-permute-done.8 = bf16[256,640]{0,1:T(8,128)(2,1)S(1)} collective-permute-done((bf16[256,640]{0,1:T(8,128)(2,1)S(1)}, bf16[256,640]{0,1:T(8,128)(2,1)S(1)}, u32[]{:S(2)}, u32[]{:S(2)}) %collective-permute-start.8) | collective-permute-done | bytes 327712 | tf_op jit(solution)/shard_map/ppermute | solution.py:41
  153.3 10.0 %all-to-all-start.4 = ((f32[32,24,128]{2,1,0:T(8,128)}), f32[32,24,128]{2,1,0:T(8,128)S(1)}, u32[]{:S(2)}, u32[]{:S(2)}) async-start(f32[32,24,128]{2,1,0:T(8,128)} %maximum_maximum_fusion), calls=%async_computation.4 | async-start | bytes 786432 | tf_op jit(solution)/shard_map/all_to_all | solution.py:45
  163.3 15.4 %all-to-all-done.4.came_ref = f32[32,24,128]{2,1,0:T(8,128)S(1)} async-done(((f32[32,24,128]{2,1,0:T(8,128)}), f32[32,24,128]{2,1,0:T(8,128)S(1)}, u32[]{:S(2)}, u32[]{:S(2)}) %all-to-all-start.4) | async-done | bytes 393248 | tf_op jit(solution)/shard_map/all_to_all | solution.py:45
  179.5 1.8 scan.1
  181.3 4.8 %all-to-all-start.5 = ((f32[32,16,128]{2,1,0:T(8,128)}), f32[32,16,128]{2,1,0:T(8,128)S(1)}, u32[]{:S(2)}, u32[]{:S(2)}) async-start(f32[32,16,128]{2,1,0:T(8,128)} %scan.1), calls=%async_computation.5 | async-start | bytes 524288 | tf_op jit(solution)/shard_map/all_to_all | solution.py:45
  187.6 11.3 %all-to-all-done.5 = f32[32,16,128]{2,1,0:T(8,128)S(1)} async-done(((f32[32,16,128]{2,1,0:T(8,128)}), f32[32,16,128]{2,1,0:T(8,128)S(1)}, u32[]{:S(2)}, u32[]{:S(2)}) %all-to-all-start.5) | async-done | bytes 262176 | tf_op jit(solution)/shard_map/all_to_all | solution.py:45
  (108 shorter events, 17.3 us)
Async XLA Ops:
  7.2 28.8 %copy-start = (bf16[128,4,256]{2,1,0:T(4,128)(2,1)S(1)}, bf16[128,4,256]{2,1,0:T(4,128)(2,1)}, u32[]{:S(2)}) copy-start(bf16[128,4,256]{2,1,0:T(4,128)(2,1)} %param.19) | copy-start | bytes 786436
  7.2 28.6 %copy-start.10 = (bf16[128,4]{0,1:T(4,128)(2,1)S(1)}, bf16[128,4]{0,1:T(4,128)(2,1)}, u32[]{:S(2)}) copy-start(bf16[128,4]{0,1:T(4,128)(2,1)} %param.20) | copy-start | bytes 3076
  7.2 28.9 %copy-start.8 = (bf16[128,256]{1,0:T(8,128)(2,1)S(1)}, bf16[128,256]{1,0:T(8,128)(2,1)}, u32[]{:S(2)}) copy-start(bf16[128,256]{1,0:T(8,128)(2,1)} %param.18) | copy-start | bytes 196612
  10.2 40.6 %all-to-all-start = ((bf16[16,128,128]{2,1,0:T(8,128)(2,1)}), bf16[16,128,128]{2,1,0:T(8,128)(2,1)S(1)}, u32[]{:S(2)}, u32[]{:S(2)}) async-start(bf16[16,128,128]{2,1,0:T(8,128)(2,1)} %broadcast_in_dim.47), calls=%async_computation | async-start | bytes 1048576 | tf_op jit(solution)/shard_map/all_to_all | solution.py:45
  23.6 112.9 %all-gather.2.cloned.1.call-start = ((), (), s32[]{:S(2)}) async-start(), calls=%async_computation.6 | async-start | bytes 4325376 | tf_op jit(solution)/shard_map/all_gather | solution.py:245
  27.4 23.0 %collective-permute-start = (bf16[160,1024]{1,0:T(8,128)(2,1)}, bf16[160,1024]{1,0:T(8,128)(2,1)S(1)}, u32[]{:S(2)}, u32[]{:S(2)}) collective-permute-start(bf16[160,1024]{1,0:T(8,128)(2,1)} %get-tuple-element.11), channel_id=1, source_target_pairs={{0,1},{1,0},{2,3},{3,2},{4,5},{5,4},{6,7},{7,6},{8,9},{9,8},{10,11... | collective-permute-start | bytes 983048 | tf_op jit(solution)/shard_map/ppermute | solution.py:41
  30.5 20.3 %collective-permute-start.2 = (bf16[160,1024]{1,0:T(8,128)(2,1)}, bf16[160,1024]{1,0:T(8,128)(2,1)S(1)}, u32[]{:S(2)}, u32[]{:S(2)}) collective-permute-start(bf16[160,1024]{1,0:T(8,128)(2,1)} %get-tuple-element.11), channel_id=1, source_target_pairs={{0,3},{1,2},{2,1},{3,0},{4,7},{5,6},{6,5},{7,4},{8,11},{9,10},{10,... | collective-permute-start | bytes 983048 | tf_op jit(solution)/shard_map/ppermute | solution.py:241
  33.7 17.1 %collective-permute-start.1 = (bf16[160,1024]{1,0:T(8,128)(2,1)}, bf16[160,1024]{1,0:T(8,128)(2,1)S(1)}, u32[]{:S(2)}, u32[]{:S(2)}) collective-permute-start(bf16[160,1024]{1,0:T(8,128)(2,1)} %get-tuple-element.10.home_ref.refs_0_), channel_id=1, source_target_pairs={{0,2},{2,0},{1,3},{3,1},{4,6},{6,4},{5,7},{7,5},{8,10},{10,8},{9,1... | collective-permute-start | bytes 983048 | tf_op jit(solution)/shard_map/ppermute | solution.py:41
  36.1 40.4 %copy-start.2 = (bf16[160,1024]{1,0:T(8,128)(2,1)S(1)}, bf16[160,1024]{1,0:T(8,128)(2,1)}, u32[]{:S(2)}) copy-start(bf16[160,1024]{1,0:T(8,128)(2,1)} %get-tuple-element.10.home_ref.refs_0_) | copy-start | bytes 983044
  36.2 0.8 collective-permute-start.3
  37.0 13.8 %copy-start.7 = (bf16[128,512]{1,0:T(8,128)(2,1)}, bf16[128,512]{1,0:T(8,128)(2,1)S(1)}, u32[]{:S(2)}) copy-start(bf16[128,512]{1,0:T(8,128)(2,1)S(1)} %collective-permute-done.3) | copy-start | bytes 393220
  37.0 39.5 %copy-start.5 = (s32[4]{0:T(128)S(1)}, s32[4]{0:T(128)}, u32[]{:S(2)}) copy-start(s32[4]{0:T(128)} %pad_add_fusion.spots) | copy-start | bytes 52
  50.9 5.4 %collective-permute-start.4 = (bf16[16,128,128]{2,1,0:T(8,128)(2,1)S(1)}, bf16[16,128,128]{2,1,0:T(8,128)(2,1)S(1)}, u32[]{:S(2)}, u32[]{:S(2)}) collective-permute-start(bf16[16,128,128]{2,1,0:T(8,128)(2,1)S(1)} %all-to-all-done.kv_ref), channel_id=1, source_target_pairs={{0,16},{16,0},{1,17},{17,1},{2,18},{18,2},{3,19},{19,3},{4,20},{20... | collective-permute-start | bytes 1572872 | tf_op jit(solution)/shard_map/ppermute | solution.py:41
  56.3 1.0 copy-start.1
  57.2 0.7 copy-start.4
  57.9 18.6 %copy-start.3 = (bf16[128,1024]{1,0:T(8,128)(2,1)S(1)}, bf16[128,1024]{1,0:T(8,128)(2,1)}, u32[]{:S(2)}) copy-start(bf16[128,1024]{1,0:T(8,128)(2,1)} %get-tuple-element.16.refs_4_) | copy-start | bytes 786436
  62.9 13.6 %all-to-all-start.1 = ((bf16[4,528,128]{2,1,0:T(8,128)(2,1)}), bf16[4,528,128]{2,1,0:T(8,128)(2,1)S(1)}, u32[]{:S(2)}, u32[]{:S(2)}) async-start(bf16[4,528,128]{2,1,0:T(8,128)(2,1)} %attend.1), calls=%async_computation.1 | async-start | bytes 1081344 | tf_op jit(solution)/shard_map/all_to_all | solution.py:45
  66.4 7.5 %collective-permute-start.5 = (bf16[160,1024]{1,0:T(8,128)(2,1)S(1)}, bf16[160,1024]{1,0:T(8,128)(2,1)S(1)}, u32[]{:S(2)}, u32[]{:S(2)}) collective-permute-start(bf16[160,1024]{1,0:T(8,128)(2,1)S(1)} %collective-permute-done.zl_ref.refs_1_), channel_id=1, source_target_pairs={{0,16},{16,0},{1,17},{17,1},{2,18},{18,2},{3,19},{19,3},{4,20},{20... | collective-permute-start | bytes 983048 | tf_op jit(solution)/shard_map/ppermute | solution.py:41
  68.7 5.2 %collective-permute-start.6 = (bf16[160,1024]{1,0:T(8,128)(2,1)S(1)}, bf16[160,1024]{1,0:T(8,128)(2,1)S(1)}, u32[]{:S(2)}, u32[]{:S(2)}) collective-permute-start(bf16[160,1024]{1,0:T(8,128)(2,1)S(1)} %collective-permute-done.1.ylo_ref.refs_2_), channel_id=1, source_target_pairs={{0,16},{16,0},{1,17},{17,1},{2,18},{18,2},{3,19},{19,3},{4,20},{20... | collective-permute-start | bytes 983048 | tf_op jit(solution)/shard_map/ppermute | solution.py:41
  70.7 3.5 %collective-permute-start.7 = (bf16[160,1024]{1,0:T(8,128)(2,1)S(1)}, bf16[160,1024]{1,0:T(8,128)(2,1)S(1)}, u32[]{:S(2)}, u32[]{:S(2)}) collective-permute-start(bf16[160,1024]{1,0:T(8,128)(2,1)S(1)} %collective-permute-done.2.both_ref.refs_3_), channel_id=1, source_target_pairs={{0,16},{16,0},{1,17},{17,1},{2,18},{18,2},{3,19},{19,3},{4,20},{20... | collective-permute-start | bytes 983048 | tf_op jit(solution)/shard_map/ppermute | solution.py:41
  78.5 22.2 %all-to-all-start.2 = ((bf16[4,32,2048]{2,1,0:T(8,128)(2,1)}), bf16[4,32,2048]{2,1,0:T(8,128)(2,1)S(1)}, u32[]{:S(2)}, u32[]{:S(2)}) async-start(bf16[4,32,2048]{2,1,0:T(8,128)(2,1)} %bitcast.9), calls=%async_computation.2 | async-start | bytes 1048576 | tf_op jit(solution)/shard_map/all_to_all | solution.py:45
  100.8 6.0 %copy-start.9 = (f32[4096]{0:T(1024)S(1)}, f32[4096]{0:T(1024)}, u32[]{:S(2)}) copy-start(f32[4096]{0:T(1024)} %param.17) | copy-start | bytes 49156
  102.0 34.0 %all-to-all-start.3 = ((bf16[8,32,2048]{2,1,0:T(8,128)(2,1)}), bf16[8,32,2048]{2,1,0:T(8,128)(2,1)S(1)}, u32[]{:S(2)}, u32[]{:S(2)}) async-start(bf16[8,32,2048]{2,1,0:T(8,128)(2,1)} %broadcast_in_dim.48), calls=%async_computation.3 | async-start | bytes 2097152 | tf_op jit(solution)/shard_map/all_to_all | solution.py:45
  140.0 3.3 %copy-start.12 = (f32[4]{0:T(128)S(1)}, f32[4]{0:T(128)}, u32[]{:S(2)}) copy-start(f32[4]{0:T(128)} %param.22) | copy-start | bytes 52
  140.0 11.0 %copy-start.11 = (f32[4]{0:T(128)S(1)}, f32[4]{0:T(128)}, u32[]{:S(2)}) copy-start(f32[4]{0:T(128)} %param.21) | copy-start | bytes 52
  140.3 10.7 %collective-permute-start.8 = (bf16[256,640]{0,1:T(8,128)(2,1)S(1)}, bf16[256,640]{0,1:T(8,128)(2,1)S(1)}, u32[]{:S(2)}, u32[]{:S(2)}) collective-permute-start(bf16[256,640]{0,1:T(8,128)(2,1)S(1)} %pad_maximum_fusion), channel_id=1, source_target_pairs={{0,1},{1,0},{2,3},{3,2},{4,5},{5,4},{6,7},{7,6},{8,9},{9,8},{10,11... | collective-permute-start | bytes 983048 | tf_op jit(solution)/shard_map/ppermute | solution.py:41
  153.3 25.4 %all-to-all-start.4 = ((f32[32,24,128]{2,1,0:T(8,128)}), f32[32,24,128]{2,1,0:T(8,128)S(1)}, u32[]{:S(2)}, u32[]{:S(2)}) async-start(f32[32,24,128]{2,1,0:T(8,128)} %maximum_maximum_fusion), calls=%async_computation.4 | async-start | bytes 786432 | tf_op jit(solution)/shard_map/all_to_all | solution.py:45
  178.7 0.8 copy-start.6
  181.3 17.6 %all-to-all-start.5 = ((f32[32,16,128]{2,1,0:T(8,128)}), f32[32,16,128]{2,1,0:T(8,128)S(1)}, u32[]{:S(2)}, u32[]{:S(2)}) async-start(f32[32,16,128]{2,1,0:T(8,128)} %scan.1), calls=%async_computation.5 | async-start | bytes 524288 | tf_op jit(solution)/shard_map/all_to_all | solution.py:45
  186.9 12.5 %copy-start.13 = (f32[4]{0:T(128)S(1)}, f32[4]{0:T(128)}, u32[]{:S(2)}) copy-start(f32[4]{0:T(128)} %param.23) | copy-start | bytes 52
Sparse Core Ops, SparseCore 0:
  51.0 84.3 all-gather.1

commit v4 on v3

--- a/solution.py
+++ b/solution.py
@@ -79,67 +79,100 @@
 
 def attend(spots, home_ref, zl_ref, ylo_ref, both_ref, kv_ref, kv_co_ref, out_ref):
     ctx, quarter, co = spots[0], spots[1], spots[3]
-    lane = lax.broadcasted_iota(jnp.int32, (32, 256), 1)
-    token = lane % 128 // 32 * 64 + lane // 128 * 32 + lane % 32
-    seat = jnp.where(token < 128, ctx, 63 - ctx) * 128 + token % 128
-    reach = seat - lax.broadcasted_iota(jnp.int32, (32, 256), 0) - 32 * quarter
+    lane = lax.broadcasted_iota(jnp.int32, (32, 128), 1)
+    token = lane % 64 // 32 * 64 + lane // 64 * 32 + lane % 32
+    reach = token - lax.broadcasted_iota(jnp.int32, (32, 128), 0) - 32 * quarter
+    first_reach = reach + 128 * ctx
+    second_reach = reach + 128 * (63 - ctx)
 
     def rows(chunk, start):
-        ref = kv_ref if chunk < 4 else kv_co_ref
-        first = chunk % 4 * 4
-        return jnp.concatenate([ref[first + i, start : start + 64] for i in range(4)])
-
-    levels = []
-    for head in range(4):
-        tiles = []
-        query = jnp.concatenate(
-            [
-                (home_ref, zl_ref, ylo_ref, both_ref)[head][128:, 128 * i : 128 * (i + 1)]
-                for i in (0, 2, 4, 6, 1, 3, 5, 7)
-            ]
-        )
-        for chunk in range(8):
-            scores = lax.dot_general(
-                rows(chunk, 0),
-                query,
-                (((1,), (1,)), ((), ())),
-                preferred_element_type=F32,
-            ) * (math.log2(math.e) / math.sqrt(128))
-            for piece in range(8):
-                core = co if chunk < 4 else 1 - co
-                source = (chunk % 4 * 4 + piece // 2) * 2 + core
-                block = source if piece % 2 == 0 else 63 - source
-                allowed = reach >= block * 128
-                tiles.append(
-                    jnp.where(allowed, scores[32 * piece : 32 * (piece + 1)], LOWEST)
-                )
+        ref = kv_ref if chunk < 2 else kv_co_ref
+        first = chunk % 2 * 8
+        return jnp.concatenate([ref[first + i, start : start + 32] for i in range(8)])
+
+    def source(chunk, piece):
+        return (chunk % 2 * 8 + piece) * 2 + (co if chunk < 2 else 1 - co)
+
+    def peak(tiles):
         top = tiles[0]
         for tile in tiles[1:]:
             top = jnp.maximum(top, tile)
-        top = jnp.max(top, axis=0, keepdims=True)
-        total = jnp.zeros((32, 256), F32)
+        return jnp.max(top, axis=0, keepdims=True)
+
+    levels = []
+    for head in range(4):
+        q_ref = (home_ref, zl_ref, ylo_ref, both_ref)[head]
+        query = jnp.concatenate(
+            [
+                q_ref[128:, 128 * i : 128 * (i + 1)]
+                for i in (0, 2, 1, 3, 4, 6, 5, 7)
+            ]
+        )
+        early, full, late = [], [], []
+        for chunk in range(4):
+            scores, later = [
+                lax.dot_general(
+                    rows(chunk, start),
+                    some,
+                    (((1,), (1,)), ((), ())),
+                    preferred_element_type=F32,
+                )
+                * (math.log2(math.e) / math.sqrt(128))
+                for start, some in ((0, query), (32, query[128:]))
+            ]
+            for piece in range(8):
+                at = slice(32 * piece, 32 * (piece + 1))
+                block = source(chunk, piece)
+                early.append(
+                    jnp.where(first_reach >= block * 128, scores[at, :128], LOWEST)
+                )
+                full.append(scores[at, 128:])
+                late.append(
+                    jnp.where(second_reach >= (63 - block) * 128, later[at], LOWEST)
+                )
+        tops = [peak(early), jnp.maximum(peak(full), peak(late))]
+        totals = [jnp.zeros((32, 128), F32), jnp.zeros((32, 128), F32)]
         summed = jnp.zeros((128, 256), F32)
-        for chunk in range(8):
-            raised = [jnp.exp2(tile - top) for tile in tiles[8 * chunk : 8 * chunk + 8]]
-            for part in raised:
-                total = total + part
+        added = jnp.zeros((128, 128), F32)
+        for chunk in range(4):
+            raised = [[], [], []]
+            for piece in range(8 * chunk, 8 * chunk + 8):
+                for i, (tiles, half) in enumerate(((early, 0), (full, 1), (late, 1))):
+                    part = jnp.exp2(tiles[piece] - tops[half])
+                    totals[half] = totals[half] + part
+                    raised[i].append(part)
+            raised = [jnp.concatenate(parts).astype(BF) for parts in raised]
             summed = summed + lax.dot_general(
                 rows(chunk, 64),
-                jnp.concatenate(raised).astype(BF),
+                jnp.concatenate(raised[:2], axis=1),
                 (((0,), (0,)), ((), ())),
                 preferred_element_type=F32,
             )
-        total = jnp.sum(total, axis=0, keepdims=True)
-        share = (summed / total).astype(BF)
+            added = added + lax.dot_general(
+                rows(chunk, 96), raised[2], (((0,), (0,)), ((), ())), preferred_element_type=F32
+            )
+        totals = [jnp.sum(total, axis=0, keepdims=True) for total in totals]
+        share = [
+            (summed[:, :128] / totals[0]).astype(BF),
+            ((summed[:, 128:] + added) / totals[1]).astype(BF),
+        ]
         for dest in range(4):
-            half = dest // 2
-            out_ref[dest, 128 * head : 128 * (head + 1)] = share[:, 128 * half : 128 * half + 128]
-        levels.append(jnp.where(top > 0.5 * LOWEST, top + jnp.log2(total), LOWEST))
-    level = jnp.concatenate(levels)
-    fine = jnp.concatenate([*split3(level), jnp.zeros((4, 256), BF)])
+            at = slice(64 * (dest // 2), 64 * (dest // 2) + 64)
+            out_ref[dest, 128 * head : 128 * (head + 1)] = jnp.concatenate(
+                [part[:, at] for part in share], axis=1
+            )
+        levels.append(
+            [
+                jnp.where(top > 0.5 * LOWEST, top + jnp.log2(total), LOWEST)
+                for top, total in zip(tops, totals)
+            ]
+        )
     for dest in range(4):
-        half = dest // 2
-        out_ref[dest, 512:528] = fine[:, 128 * half : 128 * half + 128]
+        at = slice(64 * (dest // 2), 64 * (dest // 2) + 64)
+        level = jnp.concatenate(
+            [jnp.concatenate([part[:, at] for part in pair], axis=1) for pair in levels]
+        )
+        out_ref[dest, 512:528] = jnp.concatenate([*split3(level), jnp.zeros((4, 128), BF)])
 
 
 def project(spots, came_ref, *refs):
@@ -169,6 +202,41 @@
 
     out_ref[:, pl.ds(pl.multiple_of(1024 * co, 1024), 1024)] = times(own_refs)
     out_ref[:, pl.ds(pl.multiple_of(1024 * (1 - co), 1024), 1024)] = times(rest_refs)
+
+
+def mix(spots, r_ref, gain_ref, w_ref, keep_ref, sent_ref):
+    zl = spots[2]
+    value = r_ref[...].astype(F32)
+    square = jnp.sum(value * value, axis=1, keepdims=True)
+    gained = (value * gain_ref[...]).astype(BF)
+
+    def times(side):
+        total = None
+        for p in range(8):
+            product = jnp.dot(
+                gained[:, 256 * p : 256 * (p + 1)],
+                w_ref[p, side],
+                preferred_element_type=F32,
+            )
+            total = product if total is None else total + product
+        return total
+
+    sums = [times(0), times(1)]
+    lane = lax.broadcasted_iota(jnp.int32, (256, 128), 1)
+    for mine in range(2):
+        one = jnp.where(zl == mine, sums[0], sums[1])
+        bc = jnp.concatenate([sums[0][:, 256:384], sums[1][:, 256:384]], axis=1)
+        fine = jnp.where(lane == 4, square, one[:, 384:])
+        if mine == 0:
+            keep_ref[:, :256] = one[:, :256]
+            keep_ref[:, 256:512] = bc
+            keep_ref[:, 512:] = fine
+        else:
+            first, second, third = [part.astype(F32) for part in split3(fine)]
+            fine = first + pltpu.roll(second, 8, 1) + pltpu.roll(third, 16, 1)
+            sent_ref[:, :256] = one[:, :256].astype(BF)
+            sent_ref[:, 256:512] = bc.astype(BF)
+            sent_ref[:, 512:] = fine.astype(BF)
 
 
 def scan(came_ref, out_ref):
@@ -242,8 +310,7 @@
     ]
     both, near, packed = lax.optimization_barrier((both, near, packed))
     both_co = swap(both, "co")
-    weights = lax.all_gather(packed, ("zhl", "x", "zhh", "co"), axis=0, tiled=True)
-    weights = weights.reshape(2, 2048, 512)
+    weights = lax.all_gather(packed, CTX, axis=0, tiled=True).reshape(8, 2, 256, 512)
     near_co = [swap(part, "co") for part in near]
 
     sent = pl.pallas_call(
@@ -273,25 +340,25 @@
     residual = exchange(spread, Y)
     residual_out = lax.dynamic_slice(residual, (0, 256 * y), (256, 256))
 
-    gain = lax.dynamic_index_in_dim(norm_gain.reshape(8, 2, 256), zl, 1, keepdims=False)
-    as_float = residual.astype(F32)
-    square = jnp.sum(as_float * as_float, axis=-1, keepdims=True)
-    gained = (as_float * gain.reshape(1, 2048)).astype(BF)
-    sums = jnp.einsum("tk,zkn->ztn", gained, weights, preferred_element_type=F32)
-    own = lax.dynamic_index_in_dim(sums, zl, 0, keepdims=False)
-    away = lax.dynamic_index_in_dim(sums, 1 - zl, 0, keepdims=False)
-    sum_bc = jnp.concatenate([sums[0, :, 256:384], sums[1, :, 256:384]], axis=1)
-    fine = jnp.concatenate(split3(jnp.concatenate([away[:, 384:388], square], axis=1)), axis=1)
-    sent = jnp.concatenate(
-        [away[:, :256].astype(BF), sum_bc.astype(BF), jnp.pad(fine, ((0, 0), (0, 113)))], axis=1
-    )
+    gain = features(norm_gain[None], zl)
+    keep, sent = pl.pallas_call(
+        mix,
+        out_shape=(
+            jax.ShapeDtypeStruct((256, 640), F32),
+            jax.ShapeDtypeStruct((256, 640), BF),
+        ),
+        in_specs=[SM] + [VM] * 3,
+        out_specs=(VM, VM),
+        compiler_params=pltpu.CompilerParams(vmem_limit_bytes=32 << 20),
+        name="mix",
+    )(spots, residual, gain, weights)
     came = swap(sent, "zl").astype(F32)
-    fine = came[:, 512:527].reshape(256, 3, 5)
-    fine = (fine[:, 2] + fine[:, 1]) + fine[:, 0]
-    norm = lax.rsqrt((square + fine[:, 4:5]) / 4096.0 + 1e-05)
-    sum_x = (own[:, :256] + came[:, :256]) * norm
-    sum_bc = (sum_bc + came[:, 256:512]) * norm
-    sum_dt = (own[:, 384:388] + fine[:, :4]) * norm
+    fine = (came[:, 528:533] + came[:, 520:525]) + came[:, 512:517]
+    fine = keep[:, 512:517] + fine
+    norm = lax.rsqrt(fine[:, 4:5] / 4096.0 + 1e-05)
+    sum_x = (keep[:, :256] + came[:, :256]) * norm
+    sum_bc = (keep[:, 256:512] + came[:, 256:512]) * norm
+    sum_dt = fine[:, :4] * norm
 
     half = 128
     inputs_low = sum_x.astype(BF).reshape(2, half, 1, 4, 64)

time: 209 us -> 208 us (level)
  waiting for transfers between devices: 90 us -> 85.8 us
  matrix products: 5.16 us -> 1.66 us
  starting transfers between devices: 67 us -> 69.8 us
  local copies, waits for them, and re-layouts: 16.4 us -> 18.9 us
    all_to_all x6, waiting for transfers between devices: 66.7 us -> 61.7 us  [exchange(): return lax.all_to_all(value, axes, split_axis=0, concat_axis=0, tiled=True)]
    all_to_all x6, starting transfers between devices: 44.3 us -> 47.9 us  [exchange(): return lax.all_to_all(value, axes, split_axis=0, concat_axis=0, tiled=True)]
    dot_general x1 -> x0, matrix products: 3.52 us -> none  [body(): jnp.einsum('tk,zkn->ztn', gained, weights, preferred_element_type=F32)]
    unnamed x42 -> x51, local copies, waits for them, and re-layouts: 11.6 us -> 13.8 us
  transfers between devices with their start and end apart: 16 -> 16, of which waited for: 10 -> 9; matrix products, arithmetic and copies ran while one was open for 5% -> 5% of each run, Pallas kernels for 5% -> 5%
where the time goes in v4:
time: 208 us; the launch traced here: 206 us
  waiting for transfers between devices  85.8 us (41%)
  starting transfers between devices  69.8 us (34%)
  local copies, waits for them, and re-layouts  18.9 us (9%)
  between operations  14.6 us (7%)
  Pallas kernels  13.1 us (6%)
  other arithmetic  2.49 us (1%)
    all_to_all x6, waiting for transfers between devices, exchange(): return lax.all_to_all(value, axes, split_axis=0, concat_axis=0, tiled=True)  61.7 us
    all_to_all x6, starting transfers between devices, exchange(): return lax.all_to_all(value, axes, split_axis=0, concat_axis=0, tiled=True)  47.9 us
    ppermute x7, waiting for transfers between devices, swap(): return lax.ppermute(value, axis, [(0, 1), (1, 0)])  24.1 us
    ppermute x7, starting transfers between devices, swap(): return lax.ppermute(value, axis, [(0, 1), (1, 0)])  17.9 us
    unnamed x51, local copies, waits for them, and re-layouts  13.8 us
    pallas_call x1, Pallas kernels, body(): pl.pallas_call(attend, out_shape=jax.ShapeDtypeStruct((4, 528, 128), BF),...  4.29 us
  transfers between devices with their start and end apart: 16, of which 9 were waited for; matrix products, arithmetic and copies ran while one was open for 5% of the time, Pallas kernels for 5%

profile of v4, /device:TPU:1, one launch (start us, length us, event | category | flops | bytes accessed | tf_op | source)
XLA Modules:
  0.0 206.4 jit_solution(14702098951479266470)
XLA Ops:
  7.2 1.0 copy.50
  8.2 1.0 copy.51
  10.2 13.4 %all-to-all-start = ((bf16[16,128,128]{2,1,0:T(8,128)(2,1)}), bf16[16,128,128]{2,1,0:T(8,128)(2,1)S(1)}, u32[]{:S(2)}, u32[]{:S(2)}) async-start(bf16[16,128,128]{2,1,0:T(8,128)(2,1)} %broadcast_in_dim.24), calls=%async_computation | async-start | bytes 1048576 | tf_op jit(solution)/shard_map/all_to_all | solution.py:45
  24.3 3.1 %pick.1 = (bf16[160,1024]{1,0:T(8,128)(2,1)}, bf16[160,1024]{1,0:T(8,128)(2,1)}, bf16[128,1024]{1,0:T(8,128)(2,1)}) custom-call(s32[4]{0:T(128)} %pad_add_fusion.spots, bf16[256,128]{1,0:T(8,128)(2,1)} %q_ref.1, bf16[128,4096]{1,0:T(8,128)(2,1)} %w_hbm.1), custom_call_target="tpu_custom_call" | custom-call | tf_op jit(solution)/shard_map/pick/pallas_call | solution.py:285
  27.3 3.1 %collective-permute-start = (bf16[160,1024]{1,0:T(8,128)(2,1)}, bf16[160,1024]{1,0:T(8,128)(2,1)S(1)}, u32[]{:S(2)}, u32[]{:S(2)}) collective-permute-start(bf16[160,1024]{1,0:T(8,128)(2,1)} %get-tuple-element.13), channel_id=1, source_target_pairs={{0,1},{1,0},{2,3},{3,2},{4,5},{5,4},{6,7},{7,6},{8,9},{9,8},{10,11... | collective-permute-start | bytes 983048 | tf_op jit(solution)/shard_map/ppermute | solution.py:41
  30.5 3.2 %collective-permute-start.2 = (bf16[160,1024]{1,0:T(8,128)(2,1)}, bf16[160,1024]{1,0:T(8,128)(2,1)S(1)}, u32[]{:S(2)}, u32[]{:S(2)}) collective-permute-start(bf16[160,1024]{1,0:T(8,128)(2,1)} %get-tuple-element.13), channel_id=1, source_target_pairs={{0,3},{1,2},{2,1},{3,0},{4,7},{5,6},{6,5},{7,4},{8,11},{9,10},{10,... | collective-permute-start | bytes 983048 | tf_op jit(solution)/shard_map/ppermute | solution.py:309
  33.7 2.1 %collective-permute-start.1 = (bf16[160,1024]{1,0:T(8,128)(2,1)}, bf16[160,1024]{1,0:T(8,128)(2,1)S(1)}, u32[]{:S(2)}, u32[]{:S(2)}) collective-permute-start(bf16[160,1024]{1,0:T(8,128)(2,1)} %get-tuple-element.12.home_ref.refs_0_), channel_id=1, source_target_pairs={{0,2},{2,0},{1,3},{3,1},{4,6},{6,4},{5,7},{7,5},{8,10},{10,8},{9,1... | collective-permute-start | bytes 983048 | tf_op jit(solution)/shard_map/ppermute | solution.py:41
  37.0 13.8 %collective-permute-done.1.ylo_ref.refs_2_ = bf16[160,1024]{1,0:T(8,128)(2,1)S(1)} collective-permute-done((bf16[160,1024]{1,0:T(8,128)(2,1)}, bf16[160,1024]{1,0:T(8,128)(2,1)S(1)}, u32[]{:S(2)}, u32[]{:S(2)}) %collective-permute-start.1) | collective-permute-done | bytes 327712 | tf_op jit(solution)/shard_map/ppermute | solution.py:41
  50.8 3.9 %collective-permute-start.4 = (bf16[16,128,128]{2,1,0:T(8,128)(2,1)S(1)}, bf16[16,128,128]{2,1,0:T(8,128)(2,1)S(1)}, u32[]{:S(2)}, u32[]{:S(2)}) collective-permute-start(bf16[16,128,128]{2,1,0:T(8,128)(2,1)S(1)} %all-to-all-done.kv_ref), channel_id=1, source_target_pairs={{0,16},{16,0},{1,17},{17,1},{2,18},{18,2},{3,19},{19,3},{4,20},{20... | collective-permute-start | bytes 1572872 | tf_op jit(solution)/shard_map/ppermute | solution.py:41
  54.7 1.5 collective-permute-done.4.kv_co_ref
  56.2 1.0 copy-done.2
  57.8 4.3 %attend.1 = bf16[4,528,128]{2,1,0:T(8,128)(2,1)} custom-call(s32[4]{0:T(128)S(1)} %copy-done.5, bf16[160,1024]{1,0:T(8,128)(2,1)S(1)} %copy-done.2, bf16[160,1024]{1,0:T(8,128)(2,1)S(1)} %collective-permute-done.zl_ref.refs_1_, bf16[160,1024]{1,0:T(8,128)(2,1)S(1)} %collective-permute-done.1.ylo_ref.refs_2_, ...), custom_call_target="tpu_custom_call" | custom-call | tf_op jit(solution)/shard_map/attend/pallas_call | solution.py:316
  62.1 3.5 %all-to-all-start.1 = ((bf16[4,528,128]{2,1,0:T(8,128)(2,1)}), bf16[4,528,128]{2,1,0:T(8,128)(2,1)S(1)}, u32[]{:S(2)}, u32[]{:S(2)}) async-start(bf16[4,528,128]{2,1,0:T(8,128)(2,1)} %attend.1), calls=%async_computation.1 | async-start | bytes 1081344 | tf_op jit(solution)/shard_map/all_to_all | solution.py:45
  65.6 2.3 %collective-permute-start.5 = (bf16[160,1024]{1,0:T(8,128)(2,1)S(1)}, bf16[160,1024]{1,0:T(8,128)(2,1)S(1)}, u32[]{:S(2)}, u32[]{:S(2)}) collective-permute-start(bf16[160,1024]{1,0:T(8,128)(2,1)S(1)} %collective-permute-done.zl_ref.refs_1_), channel_id=1, source_target_pairs={{0,16},{16,0},{1,17},{17,1},{2,18},{18,2},{3,19},{19,3},{4,20},{20... | collective-permute-start | bytes 983048 | tf_op jit(solution)/shard_map/ppermute | solution.py:41
  67.9 2.0 collective-permute-start.6
  69.9 2.3 %collective-permute-start.7 = (bf16[160,1024]{1,0:T(8,128)(2,1)S(1)}, bf16[160,1024]{1,0:T(8,128)(2,1)S(1)}, u32[]{:S(2)}, u32[]{:S(2)}) collective-permute-start(bf16[160,1024]{1,0:T(8,128)(2,1)S(1)} %collective-permute-done.2.both_ref.refs_3_), channel_id=1, source_target_pairs={{0,16},{16,0},{1,17},{17,1},{2,18},{18,2},{3,19},{19,3},{4,20},{20... | collective-permute-start | bytes 983048 | tf_op jit(solution)/shard_map/ppermute | solution.py:41
  73.5 1.5 all-to-all-done.1.came_ref
  75.0 2.0 project.1
  77.0 6.8 %all-to-all-start.2 = ((bf16[4,32,2048]{2,1,0:T(8,128)(2,1)}), bf16[4,32,2048]{2,1,0:T(8,128)(2,1)S(1)}, u32[]{:S(2)}, u32[]{:S(2)}) async-start(bf16[4,32,2048]{2,1,0:T(8,128)(2,1)} %bitcast.9), calls=%async_computation.2 | async-start | bytes 1048576 | tf_op jit(solution)/shard_map/all_to_all | solution.py:45
  89.6 5.0 %all-to-all-done.2 = bf16[4,32,2048]{2,1,0:T(8,128)(2,1)S(1)} async-done(((bf16[4,32,2048]{2,1,0:T(8,128)(2,1)}), bf16[4,32,2048]{2,1,0:T(8,128)(2,1)S(1)}, u32[]{:S(2)}, u32[]{:S(2)}) %all-to-all-start.2) | async-done | bytes 524320 | tf_op jit(solution)/shard_map/all_to_all | solution.py:45
  94.8 1.1 broadcast_in_dim.46
  95.9 8.4 %all-to-all-start.3 = ((bf16[8,32,2048]{2,1,0:T(8,128)(2,1)}), bf16[8,32,2048]{2,1,0:T(8,128)(2,1)S(1)}, u32[]{:S(2)}, u32[]{:S(2)}) async-start(bf16[8,32,2048]{2,1,0:T(8,128)(2,1)} %broadcast_in_dim.46), calls=%async_computation.3 | async-start | bytes 2097152 | tf_op jit(solution)/shard_map/all_to_all | solution.py:45
  104.5 29.0 %all-to-all-done.3 = bf16[8,32,2048]{2,1,0:T(8,128)(2,1)S(1)} async-done(((bf16[8,32,2048]{2,1,0:T(8,128)(2,1)}), bf16[8,32,2048]{2,1,0:T(8,128)(2,1)S(1)}, u32[]{:S(2)}, u32[]{:S(2)}) %all-to-all-start.3) | async-done | bytes 1048608 | tf_op jit(solution)/shard_map/all_to_all | solution.py:45
  133.5 2.2 %copy-done.1 = bf16[4096,512]{1,0:T(8,128)(2,1)S(1)} copy-done((bf16[4096,512]{1,0:T(8,128)(2,1)S(1)}, bf16[4096,512]{1,0:T(8,128)(2,1)}, u32[]{:S(2)}) %copy-start.1) | copy-done | bytes 4194328
  135.7 1.9 mix.1
  137.6 2.2 %collective-permute-start.8 = (bf16[256,640]{1,0:T(8,128)(2,1)S(1)}, bf16[256,640]{1,0:T(8,128)(2,1)S(1)}, u32[]{:S(2)}, u32[]{:S(2)}) collective-permute-start(bf16[256,640]{1,0:T(8,128)(2,1)S(1)} %get-tuple-element.21), channel_id=1, source_target_pairs={{0,1},{1,0},{2,3},{3,2},{4,5},{5,4},{6,7},{7,6},{8,9},{9,8},{10,11... | collective-permute-start | bytes 983048 | tf_op jit(solution)/shard_map/ppermute | solution.py:41
  139.9 8.4 %collective-permute-done.8 = bf16[256,640]{1,0:T(8,128)(2,1)S(1)} collective-permute-done((bf16[256,640]{1,0:T(8,128)(2,1)S(1)}, bf16[256,640]{1,0:T(8,128)(2,1)S(1)}, u32[]{:S(2)}, u32[]{:S(2)}) %collective-permute-start.8) | collective-permute-done | bytes 327712 | tf_op jit(solution)/shard_map/ppermute | solution.py:41
  151.1 10.9 %all-to-all-start.4 = ((f32[32,24,128]{2,1,0:T(8,128)}), f32[32,24,128]{2,1,0:T(8,128)S(1)}, u32[]{:S(2)}, u32[]{:S(2)}) async-start(f32[32,24,128]{2,1,0:T(8,128)} %maximum_maximum_fusion), calls=%async_computation.4 | async-start | bytes 786432 | tf_op jit(solution)/shard_map/all_to_all | solution.py:45
  162.0 15.4 %all-to-all-done.4.came_ref = f32[32,24,128]{2,1,0:T(8,128)S(1)} async-done(((f32[32,24,128]{2,1,0:T(8,128)}), f32[32,24,128]{2,1,0:T(8,128)S(1)}, u32[]{:S(2)}, u32[]{:S(2)}) %all-to-all-start.4) | async-done | bytes 393248 | tf_op jit(solution)/shard_map/all_to_all | solution.py:45
  178.2 1.8 scan.1
  180.0 4.8 %all-to-all-start.5 = ((f32[32,16,128]{2,1,0:T(8,128)}), f32[32,16,128]{2,1,0:T(8,128)S(1)}, u32[]{:S(2)}, u32[]{:S(2)}) async-start(f32[32,16,128]{2,1,0:T(8,128)} %scan.1), calls=%async_computation.5 | async-start | bytes 524288 | tf_op jit(solution)/shard_map/all_to_all | solution.py:45
  186.8 10.8 %all-to-all-done.5 = f32[32,16,128]{2,1,0:T(8,128)S(1)} async-done(((f32[32,16,128]{2,1,0:T(8,128)}), f32[32,16,128]{2,1,0:T(8,128)S(1)}, u32[]{:S(2)}, u32[]{:S(2)}) %all-to-all-start.5) | async-done | bytes 262176 | tf_op jit(solution)/shard_map/all_to_all | solution.py:45
  (104 shorter events, 18.0 us)
Async XLA Ops:
  7.2 28.6 %copy-start = (bf16[128,4,256]{2,1,0:T(4,128)(2,1)S(1)}, bf16[128,4,256]{2,1,0:T(4,128)(2,1)}, u32[]{:S(2)}) copy-start(bf16[128,4,256]{2,1,0:T(4,128)(2,1)} %param.19) | copy-start | bytes 786436
  7.2 28.8 %copy-start.11 = (bf16[128,4]{0,1:T(4,128)(2,1)S(1)}, bf16[128,4]{0,1:T(4,128)(2,1)}, u32[]{:S(2)}) copy-start(bf16[128,4]{0,1:T(4,128)(2,1)} %param.20) | copy-start | bytes 3076
  7.2 28.9 %copy-start.9 = (bf16[128,256]{1,0:T(8,128)(2,1)S(1)}, bf16[128,256]{1,0:T(8,128)(2,1)}, u32[]{:S(2)}) copy-start(bf16[128,256]{1,0:T(8,128)(2,1)} %param.18) | copy-start | bytes 196612
  10.2 40.6 %all-to-all-start = ((bf16[16,128,128]{2,1,0:T(8,128)(2,1)}), bf16[16,128,128]{2,1,0:T(8,128)(2,1)S(1)}, u32[]{:S(2)}, u32[]{:S(2)}) async-start(bf16[16,128,128]{2,1,0:T(8,128)(2,1)} %broadcast_in_dim.24), calls=%async_computation | async-start | bytes 1048576 | tf_op jit(solution)/shard_map/all_to_all | solution.py:45
  23.6 109.9 %all-gather.2.cloned.1.call-start = ((), (), s32[]{:S(2)}) async-start(), calls=%async_computation.6 | async-start | bytes 4325376 | tf_op jit(solution)/shard_map/all_gather | solution.py:313
  27.3 23.4 %collective-permute-start = (bf16[160,1024]{1,0:T(8,128)(2,1)}, bf16[160,1024]{1,0:T(8,128)(2,1)S(1)}, u32[]{:S(2)}, u32[]{:S(2)}) collective-permute-start(bf16[160,1024]{1,0:T(8,128)(2,1)} %get-tuple-element.13), channel_id=1, source_target_pairs={{0,1},{1,0},{2,3},{3,2},{4,5},{5,4},{6,7},{7,6},{8,9},{9,8},{10,11... | collective-permute-start | bytes 983048 | tf_op jit(solution)/shard_map/ppermute | solution.py:41
  30.5 20.3 %collective-permute-start.2 = (bf16[160,1024]{1,0:T(8,128)(2,1)}, bf16[160,1024]{1,0:T(8,128)(2,1)S(1)}, u32[]{:S(2)}, u32[]{:S(2)}) collective-permute-start(bf16[160,1024]{1,0:T(8,128)(2,1)} %get-tuple-element.13), channel_id=1, source_target_pairs={{0,3},{1,2},{2,1},{3,0},{4,7},{5,6},{6,5},{7,4},{8,11},{9,10},{10,... | collective-permute-start | bytes 983048 | tf_op jit(solution)/shard_map/ppermute | solution.py:309
  33.7 17.1 %collective-permute-start.1 = (bf16[160,1024]{1,0:T(8,128)(2,1)}, bf16[160,1024]{1,0:T(8,128)(2,1)S(1)}, u32[]{:S(2)}, u32[]{:S(2)}) collective-permute-start(bf16[160,1024]{1,0:T(8,128)(2,1)} %get-tuple-element.12.home_ref.refs_0_), channel_id=1, source_target_pairs={{0,2},{2,0},{1,3},{3,1},{4,6},{6,4},{5,7},{7,5},{8,10},{10,8},{9,1... | collective-permute-start | bytes 983048 | tf_op jit(solution)/shard_map/ppermute | solution.py:41
  36.1 38.9 %copy-start.3 = (bf16[160,1024]{1,0:T(8,128)(2,1)S(1)}, bf16[160,1024]{1,0:T(8,128)(2,1)}, u32[]{:S(2)}) copy-start(bf16[160,1024]{1,0:T(8,128)(2,1)} %get-tuple-element.12.home_ref.refs_0_) | copy-start | bytes 983044
  36.1 0.8 collective-permute-start.3
  36.9 13.8 %copy-start.8 = (bf16[128,512]{1,0:T(8,128)(2,1)}, bf16[128,512]{1,0:T(8,128)(2,1)S(1)}, u32[]{:S(2)}) copy-start(bf16[128,512]{1,0:T(8,128)(2,1)S(1)} %collective-permute-done.3) | copy-start | bytes 393220
  37.0 38.0 %copy-start.6 = (s32[4]{0:T(128)S(1)}, s32[4]{0:T(128)}, u32[]{:S(2)}) copy-start(s32[4]{0:T(128)} %pad_add_fusion.spots) | copy-start | bytes 52
  50.8 5.4 %collective-permute-start.4 = (bf16[16,128,128]{2,1,0:T(8,128)(2,1)S(1)}, bf16[16,128,128]{2,1,0:T(8,128)(2,1)S(1)}, u32[]{:S(2)}, u32[]{:S(2)}) collective-permute-start(bf16[16,128,128]{2,1,0:T(8,128)(2,1)S(1)} %all-to-all-done.kv_ref), channel_id=1, source_target_pairs={{0,16},{16,0},{1,17},{17,1},{2,18},{18,2},{3,19},{19,3},{4,20},{20... | collective-permute-start | bytes 1572872 | tf_op jit(solution)/shard_map/ppermute | solution.py:41
  56.2 1.0 copy-start.2
  57.2 0.6 copy-start.5
  57.8 17.2 %copy-start.4 = (bf16[128,1024]{1,0:T(8,128)(2,1)S(1)}, bf16[128,1024]{1,0:T(8,128)(2,1)}, u32[]{:S(2)}) copy-start(bf16[128,1024]{1,0:T(8,128)(2,1)} %get-tuple-element.18.refs_4_) | copy-start | bytes 786436
  62.1 12.9 %all-to-all-start.1 = ((bf16[4,528,128]{2,1,0:T(8,128)(2,1)}), bf16[4,528,128]{2,1,0:T(8,128)(2,1)S(1)}, u32[]{:S(2)}, u32[]{:S(2)}) async-start(bf16[4,528,128]{2,1,0:T(8,128)(2,1)} %attend.1), calls=%async_computation.1 | async-start | bytes 1081344 | tf_op jit(solution)/shard_map/all_to_all | solution.py:45
  65.6 7.5 %collective-permute-start.5 = (bf16[160,1024]{1,0:T(8,128)(2,1)S(1)}, bf16[160,1024]{1,0:T(8,128)(2,1)S(1)}, u32[]{:S(2)}, u32[]{:S(2)}) collective-permute-start(bf16[160,1024]{1,0:T(8,128)(2,1)S(1)} %collective-permute-done.zl_ref.refs_1_), channel_id=1, source_target_pairs={{0,16},{16,0},{1,17},{17,1},{2,18},{18,2},{3,19},{19,3},{4,20},{20... | collective-permute-start | bytes 983048 | tf_op jit(solution)/shard_map/ppermute | solution.py:41
  67.9 5.2 %collective-permute-start.6 = (bf16[160,1024]{1,0:T(8,128)(2,1)S(1)}, bf16[160,1024]{1,0:T(8,128)(2,1)S(1)}, u32[]{:S(2)}, u32[]{:S(2)}) collective-permute-start(bf16[160,1024]{1,0:T(8,128)(2,1)S(1)} %collective-permute-done.1.ylo_ref.refs_2_), channel_id=1, source_target_pairs={{0,16},{16,0},{1,17},{17,1},{2,18},{18,2},{3,19},{19,3},{4,20},{20... | collective-permute-start | bytes 983048 | tf_op jit(solution)/shard_map/ppermute | solution.py:41
  69.9 3.5 %collective-permute-start.7 = (bf16[160,1024]{1,0:T(8,128)(2,1)S(1)}, bf16[160,1024]{1,0:T(8,128)(2,1)S(1)}, u32[]{:S(2)}, u32[]{:S(2)}) collective-permute-start(bf16[160,1024]{1,0:T(8,128)(2,1)S(1)} %collective-permute-done.2.both_ref.refs_3_), channel_id=1, source_target_pairs={{0,16},{16,0},{1,17},{17,1},{2,18},{18,2},{3,19},{19,3},{4,20},{20... | collective-permute-start | bytes 983048 | tf_op jit(solution)/shard_map/ppermute | solution.py:41
  77.0 17.6 %all-to-all-start.2 = ((bf16[4,32,2048]{2,1,0:T(8,128)(2,1)}), bf16[4,32,2048]{2,1,0:T(8,128)(2,1)S(1)}, u32[]{:S(2)}, u32[]{:S(2)}) async-start(bf16[4,32,2048]{2,1,0:T(8,128)(2,1)} %bitcast.9), calls=%async_computation.2 | async-start | bytes 1048576 | tf_op jit(solution)/shard_map/all_to_all | solution.py:45
  94.7 9.6 %copy-start.10 = (f32[4096]{0:T(1024)S(1)}, f32[4096]{0:T(1024)}, u32[]{:S(2)}) copy-start(f32[4096]{0:T(1024)} %param.17) | copy-start | bytes 49156
  95.9 37.6 %all-to-all-start.3 = ((bf16[8,32,2048]{2,1,0:T(8,128)(2,1)}), bf16[8,32,2048]{2,1,0:T(8,128)(2,1)S(1)}, u32[]{:S(2)}, u32[]{:S(2)}) async-start(bf16[8,32,2048]{2,1,0:T(8,128)(2,1)} %broadcast_in_dim.46), calls=%async_computation.3 | async-start | bytes 2097152 | tf_op jit(solution)/shard_map/all_to_all | solution.py:45
  133.5 2.2 %copy-start.1 = (bf16[4096,512]{1,0:T(8,128)(2,1)S(1)}, bf16[4096,512]{1,0:T(8,128)(2,1)}, u32[]{:S(2)}) copy-start(bf16[4096,512]{1,0:T(8,128)(2,1)} %all-gather.2.cloned.1.call-done) | copy-start | bytes 12582916
  135.7 4.2 %copy-start.13 = (f32[4]{0:T(128)S(1)}, f32[4]{0:T(128)}, u32[]{:S(2)}) copy-start(f32[4]{0:T(128)} %param.22) | copy-start | bytes 52
  137.6 11.5 %copy-start.12 = (f32[4]{0:T(128)S(1)}, f32[4]{0:T(128)}, u32[]{:S(2)}) copy-start(f32[4]{0:T(128)} %param.21) | copy-start | bytes 52
  137.6 10.7 %collective-permute-start.8 = (bf16[256,640]{1,0:T(8,128)(2,1)S(1)}, bf16[256,640]{1,0:T(8,128)(2,1)S(1)}, u32[]{:S(2)}, u32[]{:S(2)}) collective-permute-start(bf16[256,640]{1,0:T(8,128)(2,1)S(1)} %get-tuple-element.21), channel_id=1, source_target_pairs={{0,1},{1,0},{2,3},{3,2},{4,5},{5,4},{6,7},{7,6},{8,9},{9,8},{10,11... | collective-permute-start | bytes 983048 | tf_op jit(solution)/shard_map/ppermute | solution.py:41
  151.1 26.4 %all-to-all-start.4 = ((f32[32,24,128]{2,1,0:T(8,128)}), f32[32,24,128]{2,1,0:T(8,128)S(1)}, u32[]{:S(2)}, u32[]{:S(2)}) async-start(f32[32,24,128]{2,1,0:T(8,128)} %maximum_maximum_fusion), calls=%async_computation.4 | async-start | bytes 786432 | tf_op jit(solution)/shard_map/all_to_all | solution.py:45
  177.4 0.7 copy-start.7
  180.0 17.6 %all-to-all-start.5 = ((f32[32,16,128]{2,1,0:T(8,128)}), f32[32,16,128]{2,1,0:T(8,128)S(1)}, u32[]{:S(2)}, u32[]{:S(2)}) async-start(f32[32,16,128]{2,1,0:T(8,128)} %scan.1), calls=%async_computation.5 | async-start | bytes 524288 | tf_op jit(solution)/shard_map/all_to_all | solution.py:45
  186.0 12.0 %copy-start.14 = (f32[4]{0:T(128)S(1)}, f32[4]{0:T(128)}, u32[]{:S(2)}) copy-start(f32[4]{0:T(128)} %param.23) | copy-start | bytes 52
Sparse Core Ops, SparseCore 0:
  50.9 69.0 all-gather.1

commit v5 on v4

--- a/solution.py
+++ b/solution.py
@@ -241,12 +241,17 @@
 
 def scan(came_ref, out_ref):
     state = jnp.zeros((8, 128), F32)
+    fine = [came_ref[i, 16:32].astype(F32) for i in range(32)]
+    rows = [came_ref[i, :16].astype(F32) for i in range(32)]
+    entering = []
     for i in range(32):
-        out_ref[i, :8] = state
-        state = came_ref[i, 16:17] * state + came_ref[i, :8]
+        entering.append(state)
+        decay = (fine[i][4:5] + fine[i][2:3]) + fine[i][0:1]
+        state = decay * state + rows[i][:8]
     for i in range(31, -1, -1):
-        out_ref[i, 8:] = state
-        state = came_ref[i, 17:18] * state + came_ref[i, 8:16]
+        out_ref[i] = jnp.concatenate([entering[i], state]).astype(BF)
+        decay = (fine[i][5:6] + fine[i][3:4]) + fine[i][1:2]
+        state = decay * state + rows[i][8:]
 
 
 VM = pl.BlockSpec(memory_space=pltpu.VMEM)
@@ -383,14 +388,14 @@
     block_state = split_product("csgjp,csgn->cgjpn", weighted, b_low)
     block_decay = jnp.exp(last)
 
-    rows = jnp.transpose(block_state.reshape(2, 32, 8, 128), (1, 0, 2, 3)).reshape(32, 16, 128)
-    decays = jnp.repeat(block_decay.reshape(2, 4).T, 8, axis=0)
-    decays = jnp.broadcast_to(decays[..., None], (32, 2, 128))
-    sent = jnp.concatenate([rows, decays, jnp.zeros((32, 6, 128), F32)], axis=1)
+    rows = jnp.transpose(block_state.astype(BF).reshape(2, 32, 8, 128), (1, 0, 2, 3)).reshape(32, 16, 128)
+    decays = jnp.repeat(jnp.concatenate(split3(block_decay.reshape(2, 4))).T, 8, axis=0)
+    decays = jnp.broadcast_to(decays[..., None], (32, 6, 128))
+    sent = jnp.concatenate([rows, decays, jnp.zeros((32, 10, 128), BF)], axis=1)
     came = exchange(sent, CTX)
     entering = pl.pallas_call(
         scan,
-        out_shape=jax.ShapeDtypeStruct((32, 16, 128), F32),
+        out_shape=jax.ShapeDtypeStruct((32, 16, 128), BF),
         in_specs=[VM],
         out_specs=VM,
         name="scan",
@@ -398,8 +403,8 @@
     entering = exchange(entering, CTX)
     entering = jnp.transpose(entering.reshape(32, 2, 8, 128), (1, 0, 2, 3)).reshape(2, 1, 4, 64, 128)
 
-    carried = jnp.transpose(jnp.exp(cumul), (0, 3, 1, 2))[..., None] * split_product(
-        "cgjpn,ckgn->ckgjp", entering, c_low
+    carried = jnp.transpose(jnp.exp(cumul), (0, 3, 1, 2))[..., None] * jnp.einsum(
+        "cgjpn,ckgn->ckgjp", entering, c_low, preferred_element_type=F32
     )
     output = inner + carried + skip_gain.reshape(1, 4)[:, :, None] * inputs
     mamba_out = output.reshape(256, 256).astype(BF)

time: 208 us -> 203 us (0.976)
  waiting for transfers between devices: 85.8 us -> 81.3 us
    all_to_all x6, waiting for transfers between devices: 61.7 us -> 57.2 us  [exchange(): return lax.all_to_all(value, axes, split_axis=0, concat_axis=0, tiled=True)]
    unnamed x51 -> x50, local copies, waits for them, and re-layouts: 13.8 us -> 13.6 us
where the time goes in v5:
time: 203 us; the launch traced here: 201 us
  waiting for transfers between devices  81.3 us (40%)
  starting transfers between devices  69.6 us (34%)
  local copies, waits for them, and re-layouts  18.9 us (9%)
  between operations  14.6 us (7%)
  Pallas kernels  13 us (6%)
  other arithmetic  2.42 us (1%)
    all_to_all x6, waiting for transfers between devices, exchange(): return lax.all_to_all(value, axes, split_axis=0, concat_axis=0, tiled=True)  57.2 us
    all_to_all x6, starting transfers between devices, exchange(): return lax.all_to_all(value, axes, split_axis=0, concat_axis=0, tiled=True)  47.7 us
    ppermute x7, waiting for transfers between devices, swap(): return lax.ppermute(value, axis, [(0, 1), (1, 0)])  24.1 us
    ppermute x7, starting transfers between devices, swap(): return lax.ppermute(value, axis, [(0, 1), (1, 0)])  17.9 us
    unnamed x50, local copies, waits for them, and re-layouts  13.6 us
    pallas_call x1, Pallas kernels, body(): pl.pallas_call(attend, out_shape=jax.ShapeDtypeStruct((4, 528, 128), BF),...  4.29 us
  transfers between devices with their start and end apart: 16, of which 9 were waited for; matrix products, arithmetic and copies ran while one was open for 5% of the time, Pallas kernels for 5%

profile of v5, /device:TPU:1, one launch (start us, length us, event | category | flops | bytes accessed | tf_op | source)
XLA Modules:
  0.0 201.2 jit_solution(4479510065729033587)
XLA Ops:
  7.2 1.0 copy.50
  8.2 1.0 copy.51
  10.2 13.4 %all-to-all-start = ((bf16[16,128,128]{2,1,0:T(8,128)(2,1)}), bf16[16,128,128]{2,1,0:T(8,128)(2,1)S(1)}, u32[]{:S(2)}, u32[]{:S(2)}) async-start(bf16[16,128,128]{2,1,0:T(8,128)(2,1)} %broadcast_in_dim.24), calls=%async_computation | async-start | bytes 1048576 | tf_op jit(solution)/shard_map/all_to_all | solution.py:45
  24.3 3.1 %pick.1 = (bf16[160,1024]{1,0:T(8,128)(2,1)}, bf16[160,1024]{1,0:T(8,128)(2,1)}, bf16[128,1024]{1,0:T(8,128)(2,1)}) custom-call(s32[4]{0:T(128)} %pad_add_fusion.spots, bf16[256,128]{1,0:T(8,128)(2,1)} %q_ref.1, bf16[128,4096]{1,0:T(8,128)(2,1)} %w_hbm.1), custom_call_target="tpu_custom_call" | custom-call | tf_op jit(solution)/shard_map/pick/pallas_call | solution.py:290
  27.3 3.1 %collective-permute-start = (bf16[160,1024]{1,0:T(8,128)(2,1)}, bf16[160,1024]{1,0:T(8,128)(2,1)S(1)}, u32[]{:S(2)}, u32[]{:S(2)}) collective-permute-start(bf16[160,1024]{1,0:T(8,128)(2,1)} %get-tuple-element.13), channel_id=1, source_target_pairs={{0,1},{1,0},{2,3},{3,2},{4,5},{5,4},{6,7},{7,6},{8,9},{9,8},{10,11... | collective-permute-start | bytes 983048 | tf_op jit(solution)/shard_map/ppermute | solution.py:41
  30.5 3.2 %collective-permute-start.2 = (bf16[160,1024]{1,0:T(8,128)(2,1)}, bf16[160,1024]{1,0:T(8,128)(2,1)S(1)}, u32[]{:S(2)}, u32[]{:S(2)}) collective-permute-start(bf16[160,1024]{1,0:T(8,128)(2,1)} %get-tuple-element.13), channel_id=1, source_target_pairs={{0,3},{1,2},{2,1},{3,0},{4,7},{5,6},{6,5},{7,4},{8,11},{9,10},{10,... | collective-permute-start | bytes 983048 | tf_op jit(solution)/shard_map/ppermute | solution.py:314
  33.7 2.1 %collective-permute-start.1 = (bf16[160,1024]{1,0:T(8,128)(2,1)}, bf16[160,1024]{1,0:T(8,128)(2,1)S(1)}, u32[]{:S(2)}, u32[]{:S(2)}) collective-permute-start(bf16[160,1024]{1,0:T(8,128)(2,1)} %get-tuple-element.12.home_ref.refs_0_), channel_id=1, source_target_pairs={{0,2},{2,0},{1,3},{3,1},{4,6},{6,4},{5,7},{7,5},{8,10},{10,8},{9,1... | collective-permute-start | bytes 983048 | tf_op jit(solution)/shard_map/ppermute | solution.py:41
  37.0 13.8 %collective-permute-done.1.ylo_ref.refs_2_ = bf16[160,1024]{1,0:T(8,128)(2,1)S(1)} collective-permute-done((bf16[160,1024]{1,0:T(8,128)(2,1)}, bf16[160,1024]{1,0:T(8,128)(2,1)S(1)}, u32[]{:S(2)}, u32[]{:S(2)}) %collective-permute-start.1) | collective-permute-done | bytes 327712 | tf_op jit(solution)/shard_map/ppermute | solution.py:41
  50.8 3.9 %collective-permute-start.4 = (bf16[16,128,128]{2,1,0:T(8,128)(2,1)S(1)}, bf16[16,128,128]{2,1,0:T(8,128)(2,1)S(1)}, u32[]{:S(2)}, u32[]{:S(2)}) collective-permute-start(bf16[16,128,128]{2,1,0:T(8,128)(2,1)S(1)} %all-to-all-done.kv_ref), channel_id=1, source_target_pairs={{0,16},{16,0},{1,17},{17,1},{2,18},{18,2},{3,19},{19,3},{4,20},{20... | collective-permute-start | bytes 1572872 | tf_op jit(solution)/shard_map/ppermute | solution.py:41
  54.7 1.5 collective-permute-done.4.kv_co_ref
  56.2 1.0 copy-done.2
  57.8 4.3 %attend.1 = bf16[4,528,128]{2,1,0:T(8,128)(2,1)} custom-call(s32[4]{0:T(128)S(1)} %copy-done.5, bf16[160,1024]{1,0:T(8,128)(2,1)S(1)} %copy-done.2, bf16[160,1024]{1,0:T(8,128)(2,1)S(1)} %collective-permute-done.zl_ref.refs_1_, bf16[160,1024]{1,0:T(8,128)(2,1)S(1)} %collective-permute-done.1.ylo_ref.refs_2_, ...), custom_call_target="tpu_custom_call" | custom-call | tf_op jit(solution)/shard_map/attend/pallas_call | solution.py:321
  62.1 3.5 %all-to-all-start.1 = ((bf16[4,528,128]{2,1,0:T(8,128)(2,1)}), bf16[4,528,128]{2,1,0:T(8,128)(2,1)S(1)}, u32[]{:S(2)}, u32[]{:S(2)}) async-start(bf16[4,528,128]{2,1,0:T(8,128)(2,1)} %attend.1), calls=%async_computation.1 | async-start | bytes 1081344 | tf_op jit(solution)/shard_map/all_to_all | solution.py:45
  65.6 2.3 %collective-permute-start.5 = (bf16[160,1024]{1,0:T(8,128)(2,1)S(1)}, bf16[160,1024]{1,0:T(8,128)(2,1)S(1)}, u32[]{:S(2)}, u32[]{:S(2)}) collective-permute-start(bf16[160,1024]{1,0:T(8,128)(2,1)S(1)} %collective-permute-done.zl_ref.refs_1_), channel_id=1, source_target_pairs={{0,16},{16,0},{1,17},{17,1},{2,18},{18,2},{3,19},{19,3},{4,20},{20... | collective-permute-start | bytes 983048 | tf_op jit(solution)/shard_map/ppermute | solution.py:41
  67.9 2.0 %collective-permute-start.6 = (bf16[160,1024]{1,0:T(8,128)(2,1)S(1)}, bf16[160,1024]{1,0:T(8,128)(2,1)S(1)}, u32[]{:S(2)}, u32[]{:S(2)}) collective-permute-start(bf16[160,1024]{1,0:T(8,128)(2,1)S(1)} %collective-permute-done.1.ylo_ref.refs_2_), channel_id=1, source_target_pairs={{0,16},{16,0},{1,17},{17,1},{2,18},{18,2},{3,19},{19,3},{4,20},{20... | collective-permute-start | bytes 983048 | tf_op jit(solution)/shard_map/ppermute | solution.py:41
  69.9 2.3 %collective-permute-start.7 = (bf16[160,1024]{1,0:T(8,128)(2,1)S(1)}, bf16[160,1024]{1,0:T(8,128)(2,1)S(1)}, u32[]{:S(2)}, u32[]{:S(2)}) collective-permute-start(bf16[160,1024]{1,0:T(8,128)(2,1)S(1)} %collective-permute-done.2.both_ref.refs_3_), channel_id=1, source_target_pairs={{0,16},{16,0},{1,17},{17,1},{2,18},{18,2},{3,19},{19,3},{4,20},{20... | collective-permute-start | bytes 983048 | tf_op jit(solution)/shard_map/ppermute | solution.py:41
  73.5 1.5 all-to-all-done.1.came_ref
  75.0 2.0 project.1
  77.0 6.8 %all-to-all-start.2 = ((bf16[4,32,2048]{2,1,0:T(8,128)(2,1)}), bf16[4,32,2048]{2,1,0:T(8,128)(2,1)S(1)}, u32[]{:S(2)}, u32[]{:S(2)}) async-start(bf16[4,32,2048]{2,1,0:T(8,128)(2,1)} %bitcast.9), calls=%async_computation.2 | async-start | bytes 1048576 | tf_op jit(solution)/shard_map/all_to_all | solution.py:45
  89.6 5.0 %all-to-all-done.2 = bf16[4,32,2048]{2,1,0:T(8,128)(2,1)S(1)} async-done(((bf16[4,32,2048]{2,1,0:T(8,128)(2,1)}), bf16[4,32,2048]{2,1,0:T(8,128)(2,1)S(1)}, u32[]{:S(2)}, u32[]{:S(2)}) %all-to-all-start.2) | async-done | bytes 524320 | tf_op jit(solution)/shard_map/all_to_all | solution.py:45
  94.8 1.1 broadcast_in_dim.46
  95.9 8.4 %all-to-all-start.3 = ((bf16[8,32,2048]{2,1,0:T(8,128)(2,1)}), bf16[8,32,2048]{2,1,0:T(8,128)(2,1)S(1)}, u32[]{:S(2)}, u32[]{:S(2)}) async-start(bf16[8,32,2048]{2,1,0:T(8,128)(2,1)} %broadcast_in_dim.46), calls=%async_computation.3 | async-start | bytes 2097152 | tf_op jit(solution)/shard_map/all_to_all | solution.py:45
  104.5 29.0 %all-to-all-done.3 = bf16[8,32,2048]{2,1,0:T(8,128)(2,1)S(1)} async-done(((bf16[8,32,2048]{2,1,0:T(8,128)(2,1)}), bf16[8,32,2048]{2,1,0:T(8,128)(2,1)S(1)}, u32[]{:S(2)}, u32[]{:S(2)}) %all-to-all-start.3) | async-done | bytes 1048608 | tf_op jit(solution)/shard_map/all_to_all | solution.py:45
  133.5 2.2 %copy-done.1 = bf16[4096,512]{1,0:T(8,128)(2,1)S(1)} copy-done((bf16[4096,512]{1,0:T(8,128)(2,1)S(1)}, bf16[4096,512]{1,0:T(8,128)(2,1)}, u32[]{:S(2)}) %copy-start.1) | copy-done | bytes 4194328
  135.7 1.9 mix.1
  137.6 2.2 %collective-permute-start.8 = (bf16[256,640]{1,0:T(8,128)(2,1)S(1)}, bf16[256,640]{1,0:T(8,128)(2,1)S(1)}, u32[]{:S(2)}, u32[]{:S(2)}) collective-permute-start(bf16[256,640]{1,0:T(8,128)(2,1)S(1)} %get-tuple-element.21), channel_id=1, source_target_pairs={{0,1},{1,0},{2,3},{3,2},{4,5},{5,4},{6,7},{7,6},{8,9},{9,8},{10,11... | collective-permute-start | bytes 983048 | tf_op jit(solution)/shard_map/ppermute | solution.py:41
  139.9 8.4 %collective-permute-done.8 = bf16[256,640]{1,0:T(8,128)(2,1)S(1)} collective-permute-done((bf16[256,640]{1,0:T(8,128)(2,1)S(1)}, bf16[256,640]{1,0:T(8,128)(2,1)S(1)}, u32[]{:S(2)}, u32[]{:S(2)}) %collective-permute-start.8) | collective-permute-done | bytes 327712 | tf_op jit(solution)/shard_map/ppermute | solution.py:41
  151.1 11.0 %all-to-all-start.4 = ((bf16[32,32,128]{2,1,0:T(8,128)(2,1)}), bf16[32,32,128]{2,1,0:T(8,128)(2,1)S(1)}, u32[]{:S(2)}, u32[]{:S(2)}) async-start(bf16[32,32,128]{2,1,0:T(8,128)(2,1)} %maximum_maximum_fusion), calls=%async_computation.4 | async-start | bytes 524288 | tf_op jit(solution)/shard_map/all_to_all | solution.py:45
  162.7 12.2 %all-to-all-done.4.came_ref = bf16[32,32,128]{2,1,0:T(8,128)(2,1)S(1)} async-done(((bf16[32,32,128]{2,1,0:T(8,128)(2,1)}), bf16[32,32,128]{2,1,0:T(8,128)(2,1)S(1)}, u32[]{:S(2)}, u32[]{:S(2)}) %all-to-all-start.4) | async-done | bytes 262176 | tf_op jit(solution)/shard_map/all_to_all | solution.py:45
  175.6 1.7 scan.1
  177.4 4.6 %all-to-all-start.5 = ((bf16[32,16,128]{2,1,0:T(8,128)(2,1)}), bf16[32,16,128]{2,1,0:T(8,128)(2,1)S(1)}, u32[]{:S(2)}, u32[]{:S(2)}) async-start(bf16[32,16,128]{2,1,0:T(8,128)(2,1)} %scan.1), calls=%async_computation.5 | async-start | bytes 262144 | tf_op jit(solution)/shard_map/all_to_all | solution.py:45
  183.3 9.4 %all-to-all-done.5 = bf16[32,16,128]{2,1,0:T(8,128)(2,1)S(1)} async-done(((bf16[32,16,128]{2,1,0:T(8,128)(2,1)}), bf16[32,16,128]{2,1,0:T(8,128)(2,1)S(1)}, u32[]{:S(2)}, u32[]{:S(2)}) %all-to-all-start.5) | async-done | bytes 131104 | tf_op jit(solution)/shard_map/all_to_all | solution.py:45
  (103 shorter events, 17.7 us)
Async XLA Ops:
  7.2 28.6 %copy-start = (bf16[128,4,256]{2,1,0:T(4,128)(2,1)S(1)}, bf16[128,4,256]{2,1,0:T(4,128)(2,1)}, u32[]{:S(2)}) copy-start(bf16[128,4,256]{2,1,0:T(4,128)(2,1)} %param.19) | copy-start | bytes 786436
  7.2 28.8 %copy-start.11 = (bf16[128,4]{0,1:T(4,128)(2,1)S(1)}, bf16[128,4]{0,1:T(4,128)(2,1)}, u32[]{:S(2)}) copy-start(bf16[128,4]{0,1:T(4,128)(2,1)} %param.20) | copy-start | bytes 3076
  7.2 28.9 %copy-start.9 = (bf16[128,256]{1,0:T(8,128)(2,1)S(1)}, bf16[128,256]{1,0:T(8,128)(2,1)}, u32[]{:S(2)}) copy-start(bf16[128,256]{1,0:T(8,128)(2,1)} %param.18) | copy-start | bytes 196612
  10.2 40.6 %all-to-all-start = ((bf16[16,128,128]{2,1,0:T(8,128)(2,1)}), bf16[16,128,128]{2,1,0:T(8,128)(2,1)S(1)}, u32[]{:S(2)}, u32[]{:S(2)}) async-start(bf16[16,128,128]{2,1,0:T(8,128)(2,1)} %broadcast_in_dim.24), calls=%async_computation | async-start | bytes 1048576 | tf_op jit(solution)/shard_map/all_to_all | solution.py:45
  23.6 109.9 %all-gather.2.cloned.1.call-start = ((), (), s32[]{:S(2)}) async-start(), calls=%async_computation.6 | async-start | bytes 4325376 | tf_op jit(solution)/shard_map/all_gather | solution.py:318
  27.3 23.4 %collective-permute-start = (bf16[160,1024]{1,0:T(8,128)(2,1)}, bf16[160,1024]{1,0:T(8,128)(2,1)S(1)}, u32[]{:S(2)}, u32[]{:S(2)}) collective-permute-start(bf16[160,1024]{1,0:T(8,128)(2,1)} %get-tuple-element.13), channel_id=1, source_target_pairs={{0,1},{1,0},{2,3},{3,2},{4,5},{5,4},{6,7},{7,6},{8,9},{9,8},{10,11... | collective-permute-start | bytes 983048 | tf_op jit(solution)/shard_map/ppermute | solution.py:41
  30.5 20.3 %collective-permute-start.2 = (bf16[160,1024]{1,0:T(8,128)(2,1)}, bf16[160,1024]{1,0:T(8,128)(2,1)S(1)}, u32[]{:S(2)}, u32[]{:S(2)}) collective-permute-start(bf16[160,1024]{1,0:T(8,128)(2,1)} %get-tuple-element.13), channel_id=1, source_target_pairs={{0,3},{1,2},{2,1},{3,0},{4,7},{5,6},{6,5},{7,4},{8,11},{9,10},{10,... | collective-permute-start | bytes 983048 | tf_op jit(solution)/shard_map/ppermute | solution.py:314
  33.7 17.1 %collective-permute-start.1 = (bf16[160,1024]{1,0:T(8,128)(2,1)}, bf16[160,1024]{1,0:T(8,128)(2,1)S(1)}, u32[]{:S(2)}, u32[]{:S(2)}) collective-permute-start(bf16[160,1024]{1,0:T(8,128)(2,1)} %get-tuple-element.12.home_ref.refs_0_), channel_id=1, source_target_pairs={{0,2},{2,0},{1,3},{3,1},{4,6},{6,4},{5,7},{7,5},{8,10},{10,8},{9,1... | collective-permute-start | bytes 983048 | tf_op jit(solution)/shard_map/ppermute | solution.py:41
  36.1 38.9 %copy-start.3 = (bf16[160,1024]{1,0:T(8,128)(2,1)S(1)}, bf16[160,1024]{1,0:T(8,128)(2,1)}, u32[]{:S(2)}) copy-start(bf16[160,1024]{1,0:T(8,128)(2,1)} %get-tuple-element.12.home_ref.refs_0_) | copy-start | bytes 983044
  36.1 0.8 collective-permute-start.3
  36.9 13.8 %copy-start.8 = (bf16[128,512]{1,0:T(8,128)(2,1)}, bf16[128,512]{1,0:T(8,128)(2,1)S(1)}, u32[]{:S(2)}) copy-start(bf16[128,512]{1,0:T(8,128)(2,1)S(1)} %collective-permute-done.3) | copy-start | bytes 393220
  36.9 38.0 %copy-start.6 = (s32[4]{0:T(128)S(1)}, s32[4]{0:T(128)}, u32[]{:S(2)}) copy-start(s32[4]{0:T(128)} %pad_add_fusion.spots) | copy-start | bytes 52
  50.8 5.4 %collective-permute-start.4 = (bf16[16,128,128]{2,1,0:T(8,128)(2,1)S(1)}, bf16[16,128,128]{2,1,0:T(8,128)(2,1)S(1)}, u32[]{:S(2)}, u32[]{:S(2)}) collective-permute-start(bf16[16,128,128]{2,1,0:T(8,128)(2,1)S(1)} %all-to-all-done.kv_ref), channel_id=1, source_target_pairs={{0,16},{16,0},{1,17},{17,1},{2,18},{18,2},{3,19},{19,3},{4,20},{20... | collective-permute-start | bytes 1572872 | tf_op jit(solution)/shard_map/ppermute | solution.py:41
  56.2 1.0 copy-start.2
  57.2 0.6 copy-start.5
  57.8 17.2 %copy-start.4 = (bf16[128,1024]{1,0:T(8,128)(2,1)S(1)}, bf16[128,1024]{1,0:T(8,128)(2,1)}, u32[]{:S(2)}) copy-start(bf16[128,1024]{1,0:T(8,128)(2,1)} %get-tuple-element.18.refs_4_) | copy-start | bytes 786436
  62.1 12.9 %all-to-all-start.1 = ((bf16[4,528,128]{2,1,0:T(8,128)(2,1)}), bf16[4,528,128]{2,1,0:T(8,128)(2,1)S(1)}, u32[]{:S(2)}, u32[]{:S(2)}) async-start(bf16[4,528,128]{2,1,0:T(8,128)(2,1)} %attend.1), calls=%async_computation.1 | async-start | bytes 1081344 | tf_op jit(solution)/shard_map/all_to_all | solution.py:45
  65.6 7.5 %collective-permute-start.5 = (bf16[160,1024]{1,0:T(8,128)(2,1)S(1)}, bf16[160,1024]{1,0:T(8,128)(2,1)S(1)}, u32[]{:S(2)}, u32[]{:S(2)}) collective-permute-start(bf16[160,1024]{1,0:T(8,128)(2,1)S(1)} %collective-permute-done.zl_ref.refs_1_), channel_id=1, source_target_pairs={{0,16},{16,0},{1,17},{17,1},{2,18},{18,2},{3,19},{19,3},{4,20},{20... | collective-permute-start | bytes 983048 | tf_op jit(solution)/shard_map/ppermute | solution.py:41
  67.9 5.2 %collective-permute-start.6 = (bf16[160,1024]{1,0:T(8,128)(2,1)S(1)}, bf16[160,1024]{1,0:T(8,128)(2,1)S(1)}, u32[]{:S(2)}, u32[]{:S(2)}) collective-permute-start(bf16[160,1024]{1,0:T(8,128)(2,1)S(1)} %collective-permute-done.1.ylo_ref.refs_2_), channel_id=1, source_target_pairs={{0,16},{16,0},{1,17},{17,1},{2,18},{18,2},{3,19},{19,3},{4,20},{20... | collective-permute-start | bytes 983048 | tf_op jit(solution)/shard_map/ppermute | solution.py:41
  69.9 3.5 %collective-permute-start.7 = (bf16[160,1024]{1,0:T(8,128)(2,1)S(1)}, bf16[160,1024]{1,0:T(8,128)(2,1)S(1)}, u32[]{:S(2)}, u32[]{:S(2)}) collective-permute-start(bf16[160,1024]{1,0:T(8,128)(2,1)S(1)} %collective-permute-done.2.both_ref.refs_3_), channel_id=1, source_target_pairs={{0,16},{16,0},{1,17},{17,1},{2,18},{18,2},{3,19},{19,3},{4,20},{20... | collective-permute-start | bytes 983048 | tf_op jit(solution)/shard_map/ppermute | solution.py:41
  77.0 17.6 %all-to-all-start.2 = ((bf16[4,32,2048]{2,1,0:T(8,128)(2,1)}), bf16[4,32,2048]{2,1,0:T(8,128)(2,1)S(1)}, u32[]{:S(2)}, u32[]{:S(2)}) async-start(bf16[4,32,2048]{2,1,0:T(8,128)(2,1)} %bitcast.9), calls=%async_computation.2 | async-start | bytes 1048576 | tf_op jit(solution)/shard_map/all_to_all | solution.py:45
  94.7 9.6 %copy-start.10 = (f32[4096]{0:T(1024)S(1)}, f32[4096]{0:T(1024)}, u32[]{:S(2)}) copy-start(f32[4096]{0:T(1024)} %param.17) | copy-start | bytes 49156
  95.9 37.6 %all-to-all-start.3 = ((bf16[8,32,2048]{2,1,0:T(8,128)(2,1)}), bf16[8,32,2048]{2,1,0:T(8,128)(2,1)S(1)}, u32[]{:S(2)}, u32[]{:S(2)}) async-start(bf16[8,32,2048]{2,1,0:T(8,128)(2,1)} %broadcast_in_dim.46), calls=%async_computation.3 | async-start | bytes 2097152 | tf_op jit(solution)/shard_map/all_to_all | solution.py:45
  133.5 2.2 %copy-start.1 = (bf16[4096,512]{1,0:T(8,128)(2,1)S(1)}, bf16[4096,512]{1,0:T(8,128)(2,1)}, u32[]{:S(2)}) copy-start(bf16[4096,512]{1,0:T(8,128)(2,1)} %all-gather.2.cloned.1.call-done) | copy-start | bytes 12582916
  135.7 4.2 %copy-start.13 = (f32[4]{0:T(128)S(1)}, f32[4]{0:T(128)}, u32[]{:S(2)}) copy-start(f32[4]{0:T(128)} %param.22) | copy-start | bytes 52
  137.6 11.5 %copy-start.12 = (f32[4]{0:T(128)S(1)}, f32[4]{0:T(128)}, u32[]{:S(2)}) copy-start(f32[4]{0:T(128)} %param.21) | copy-start | bytes 52
  137.6 10.7 %collective-permute-start.8 = (bf16[256,640]{1,0:T(8,128)(2,1)S(1)}, bf16[256,640]{1,0:T(8,128)(2,1)S(1)}, u32[]{:S(2)}, u32[]{:S(2)}) collective-permute-start(bf16[256,640]{1,0:T(8,128)(2,1)S(1)} %get-tuple-element.21), channel_id=1, source_target_pairs={{0,1},{1,0},{2,3},{3,2},{4,5},{5,4},{6,7},{7,6},{8,9},{9,8},{10,11... | collective-permute-start | bytes 983048 | tf_op jit(solution)/shard_map/ppermute | solution.py:41
  151.1 23.9 %all-to-all-start.4 = ((bf16[32,32,128]{2,1,0:T(8,128)(2,1)}), bf16[32,32,128]{2,1,0:T(8,128)(2,1)S(1)}, u32[]{:S(2)}, u32[]{:S(2)}) async-start(bf16[32,32,128]{2,1,0:T(8,128)(2,1)} %maximum_maximum_fusion), calls=%async_computation.4 | async-start | bytes 524288 | tf_op jit(solution)/shard_map/all_to_all | solution.py:45
  175.0 0.7 copy-start.7
  177.4 15.5 %copy-start.14 = (f32[4]{0:T(128)S(1)}, f32[4]{0:T(128)}, u32[]{:S(2)}) copy-start(f32[4]{0:T(128)} %param.23) | copy-start | bytes 52
  177.4 15.3 %all-to-all-start.5 = ((bf16[32,16,128]{2,1,0:T(8,128)(2,1)}), bf16[32,16,128]{2,1,0:T(8,128)(2,1)S(1)}, u32[]{:S(2)}, u32[]{:S(2)}) async-start(bf16[32,16,128]{2,1,0:T(8,128)(2,1)} %scan.1), calls=%async_computation.5 | async-start | bytes 262144 | tf_op jit(solution)/shard_map/all_to_all | solution.py:45
Sparse Core Ops, SparseCore 0:
  50.9 69.0 all-gather.1

commit v6 on v5

--- a/solution.py
+++ b/solution.py
@@ -1,3 +1,4 @@
+import functools
 import math
 
 import jax
@@ -25,6 +26,14 @@
     second = rest.astype(BF)
     third = (rest - second.astype(F32)).astype(BF)
     return first, second, third
+
+
+def split3_kept(value):
+    first = lax.reduce_precision(value, 8, 7)
+    rest = value - first
+    second = lax.reduce_precision(rest, 8, 7)
+    third = rest - second
+    return first.astype(BF), second.astype(BF), third.astype(BF)
 
 
 def features(value, zl):
@@ -77,8 +86,13 @@
         copy.wait()
 
 
-def attend(spots, home_ref, zl_ref, ylo_ref, both_ref, kv_ref, kv_co_ref, out_ref):
+def attend(first, spots, home_ref, zl_ref, ylo_ref, both_ref, kv_ref, *refs):
     ctx, quarter, co = spots[0], spots[1], spots[3]
+    core = co if first else 1 - co
+    if first:
+        sums_ref, stats_ref = refs
+    else:
+        sums_ref, stats_ref, out_ref = refs
     lane = lax.broadcasted_iota(jnp.int32, (32, 128), 1)
     token = lane % 64 // 32 * 64 + lane // 64 * 32 + lane % 32
     reach = token - lax.broadcasted_iota(jnp.int32, (32, 128), 0) - 32 * quarter
@@ -86,12 +100,9 @@
     second_reach = reach + 128 * (63 - ctx)
 
     def rows(chunk, start):
-        ref = kv_ref if chunk < 2 else kv_co_ref
-        first = chunk % 2 * 8
-        return jnp.concatenate([ref[first + i, start : start + 32] for i in range(8)])
-
-    def source(chunk, piece):
-        return (chunk % 2 * 8 + piece) * 2 + (co if chunk < 2 else 1 - co)
+        return jnp.concatenate(
+            [kv_ref[8 * chunk + i, start : start + 32] for i in range(8)]
+        )
 
     def peak(tiles):
         top = tiles[0]
@@ -109,7 +120,7 @@
             ]
         )
         early, full, late = [], [], []
-        for chunk in range(4):
+        for chunk in range(2):
             scores, later = [
                 lax.dot_general(
                     rows(chunk, start),
@@ -122,7 +133,7 @@
             ]
             for piece in range(8):
                 at = slice(32 * piece, 32 * (piece + 1))
-                block = source(chunk, piece)
+                block = (8 * chunk + piece) * 2 + core
                 early.append(
                     jnp.where(first_reach >= block * 128, scores[at, :128], LOWEST)
                 )
@@ -131,10 +142,14 @@
                     jnp.where(second_reach >= (63 - block) * 128, later[at], LOWEST)
                 )
         tops = [peak(early), jnp.maximum(peak(full), peak(late))]
+        if not first:
+            before = [stats_ref[head, i : i + 1] for i in range(4)]
+            tops = [jnp.maximum(tops[i], before[i]) for i in range(2)]
+            scales = [jnp.exp2(before[i] - tops[i]) for i in range(2)]
         totals = [jnp.zeros((32, 128), F32), jnp.zeros((32, 128), F32)]
         summed = jnp.zeros((128, 256), F32)
         added = jnp.zeros((128, 128), F32)
-        for chunk in range(4):
+        for chunk in range(2):
             raised = [[], [], []]
             for piece in range(8 * chunk, 8 * chunk + 8):
                 for i, (tiles, half) in enumerate(((early, 0), (full, 1), (late, 1))):
@@ -152,9 +167,19 @@
                 rows(chunk, 96), raised[2], (((0,), (0,)), ((), ())), preferred_element_type=F32
             )
         totals = [jnp.sum(total, axis=0, keepdims=True) for total in totals]
+        summed = [summed[:, :128], summed[:, 128:] + added]
+        if first:
+            sums_ref[head, :, :128] = summed[0]
+            sums_ref[head, :, 128:] = summed[1]
+            stats_ref[head] = jnp.concatenate([*tops, *totals, jnp.zeros((4, 128), F32)])
+            continue
+        totals = [totals[i] + scales[i] * before[2 + i] for i in range(2)]
         share = [
-            (summed[:, :128] / totals[0]).astype(BF),
-            ((summed[:, 128:] + added) / totals[1]).astype(BF),
+            (
+                (summed[i] + scales[i] * sums_ref[head, :, 128 * i : 128 * (i + 1)])
+                / totals[i]
+            ).astype(BF)
+            for i in range(2)
         ]
         for dest in range(4):
             at = slice(64 * (dest // 2), 64 * (dest // 2) + 64)
@@ -167,6 +192,8 @@
                 for top, total in zip(tops, totals)
             ]
         )
+    if first:
+        return
     for dest in range(4):
         at = slice(64 * (dest // 2), 64 * (dest // 2) + 64)
         level = jnp.concatenate(
@@ -318,14 +345,25 @@
     weights = lax.all_gather(packed, CTX, axis=0, tiled=True).reshape(8, 2, 256, 512)
     near_co = [swap(part, "co") for part in near]
 
+    so_far = pl.pallas_call(
+        functools.partial(attend, True),
+        out_shape=(
+            jax.ShapeDtypeStruct((4, 128, 256), F32),
+            jax.ShapeDtypeStruct((4, 8, 128), F32),
+        ),
+        in_specs=[SM] + [VM] * 5,
+        out_specs=(VM, VM),
+        compiler_params=pltpu.CompilerParams(vmem_limit_bytes=32 << 20),
+        name="attend_own",
+    )(spots, home, *near, both)
     sent = pl.pallas_call(
-        attend,
+        functools.partial(attend, False),
         out_shape=jax.ShapeDtypeStruct((4, 528, 128), BF),
-        in_specs=[SM] + [VM] * 6,
+        in_specs=[SM] + [VM] * 7,
         out_specs=VM,
         compiler_params=pltpu.CompilerParams(vmem_limit_bytes=32 << 20),
-        name="attend",
-    )(spots, home, *near, both, both_co)
+        name="attend_other",
+    )(spots, home, *near, both_co, *so_far)
     came = exchange(sent.reshape(4 * 528, 128), ("ylo", "zl")).reshape(4, 528, 128)
     head_part = pl.pallas_call(
         project,
@@ -389,7 +427,7 @@
     block_decay = jnp.exp(last)
 
     rows = jnp.transpose(block_state.astype(BF).reshape(2, 32, 8, 128), (1, 0, 2, 3)).reshape(32, 16, 128)
-    decays = jnp.repeat(jnp.concatenate(split3(block_decay.reshape(2, 4))).T, 8, axis=0)
+    decays = jnp.repeat(jnp.concatenate(split3_kept(block_decay.reshape(2, 4))).T, 8, axis=0)
     decays = jnp.broadcast_to(decays[..., None], (32, 6, 128))
     sent = jnp.concatenate([rows, decays, jnp.zeros((32, 10, 128), BF)], axis=1)
     came = exchange(sent, CTX)

time: 203 us -> 201 us (level)
  starting transfers between devices: 69.6 us -> 65.7 us
    all_to_all x6, starting transfers between devices: 47.7 us -> 44.6 us  [exchange(): return lax.all_to_all(value, axes, split_axis=0, concat_axis=0, tiled=True)]
    pallas_call x1 -> x2, Pallas kernels: 4.29 us -> 5.79 us  [the longest x1 3.36 us: body(): pl.pallas_call(functools.partial(attend, False), out_shape=jax.ShapeDtype...]
  transfers between devices with their start and end apart: 16 -> 16, of which waited for: 9 -> 8; matrix products, arithmetic and copies ran while one was open for 5% -> 6% of each run, Pallas kernels for 5% -> 5%
where the time goes in v6:
time: 201 us; the launch traced here: 200 us
  waiting for transfers between devices  82 us (41%)
  starting transfers between devices  65.7 us (33%)
  local copies, waits for them, and re-layouts  19 us (9%)
  between operations  14.6 us (7%)
  Pallas kernels  14.5 us (7%)
  other arithmetic  2.49 us (1%)
    all_to_all x6, waiting for transfers between devices, exchange(): return lax.all_to_all(value, axes, split_axis=0, concat_axis=0, tiled=True)  58.7 us
    all_to_all x6, starting transfers between devices, exchange(): return lax.all_to_all(value, axes, split_axis=0, concat_axis=0, tiled=True)  44.6 us
    ppermute x7, waiting for transfers between devices, swap(): return lax.ppermute(value, axis, [(0, 1), (1, 0)])  23.3 us
    ppermute x7, starting transfers between devices, swap(): return lax.ppermute(value, axis, [(0, 1), (1, 0)])  17.2 us
    unnamed x50, local copies, waits for them, and re-layouts  13.7 us
  transfers between devices with their start and end apart: 16, of which 8 were waited for; matrix products, arithmetic and copies ran while one was open for 6% of the time, Pallas kernels for 5%

profile of v6, /device:TPU:1, one launch (start us, length us, event | category | flops | bytes accessed | tf_op | source)
XLA Modules:
  0.0 199.8 jit_solution(17233893332730220393)
XLA Ops:
  7.2 1.0 copy.50
  8.2 1.0 copy.51
  10.2 13.4 %all-to-all-start = ((bf16[16,128,128]{2,1,0:T(8,128)(2,1)}), bf16[16,128,128]{2,1,0:T(8,128)(2,1)S(1)}, u32[]{:S(2)}, u32[]{:S(2)}) async-start(bf16[16,128,128]{2,1,0:T(8,128)(2,1)} %broadcast_in_dim.24), calls=%async_computation | async-start | bytes 1048576 | tf_op jit(solution)/shard_map/all_to_all | solution.py:54
  24.3 3.1 %pick.1 = (bf16[160,1024]{1,0:T(8,128)(2,1)}, bf16[160,1024]{1,0:T(8,128)(2,1)}, bf16[128,1024]{1,0:T(8,128)(2,1)}) custom-call(s32[4]{0:T(128)} %pad_add_fusion.spots, bf16[256,128]{1,0:T(8,128)(2,1)} %q_ref.1, bf16[128,4096]{1,0:T(8,128)(2,1)} %w_hbm.1), custom_call_target="tpu_custom_call" | custom-call | tf_op jit(solution)/shard_map/pick/pallas_call | solution.py:317
  27.4 3.1 %collective-permute-start = (bf16[160,1024]{1,0:T(8,128)(2,1)}, bf16[160,1024]{1,0:T(8,128)(2,1)S(1)}, u32[]{:S(2)}, u32[]{:S(2)}) collective-permute-start(bf16[160,1024]{1,0:T(8,128)(2,1)} %get-tuple-element.15), channel_id=1, source_target_pairs={{0,1},{1,0},{2,3},{3,2},{4,5},{5,4},{6,7},{7,6},{8,9},{9,8},{10,11... | collective-permute-start | bytes 983048 | tf_op jit(solution)/shard_map/ppermute | solution.py:50
  30.5 3.2 %collective-permute-start.2 = (bf16[160,1024]{1,0:T(8,128)(2,1)}, bf16[160,1024]{1,0:T(8,128)(2,1)S(1)}, u32[]{:S(2)}, u32[]{:S(2)}) collective-permute-start(bf16[160,1024]{1,0:T(8,128)(2,1)} %get-tuple-element.15), channel_id=1, source_target_pairs={{0,3},{1,2},{2,1},{3,0},{4,7},{5,6},{6,5},{7,4},{8,11},{9,10},{10,... | collective-permute-start | bytes 983048 | tf_op jit(solution)/shard_map/ppermute | solution.py:341
  33.7 2.1 %collective-permute-start.1 = (bf16[160,1024]{1,0:T(8,128)(2,1)}, bf16[160,1024]{1,0:T(8,128)(2,1)S(1)}, u32[]{:S(2)}, u32[]{:S(2)}) collective-permute-start(bf16[160,1024]{1,0:T(8,128)(2,1)} %get-tuple-element.14.home_ref.refs_0_), channel_id=1, source_target_pairs={{0,2},{2,0},{1,3},{3,1},{4,6},{6,4},{5,7},{7,5},{8,10},{10,8},{9,1... | collective-permute-start | bytes 983048 | tf_op jit(solution)/shard_map/ppermute | solution.py:50
  36.9 13.9 %collective-permute-done.1.ylo_ref.refs_2_ = bf16[160,1024]{1,0:T(8,128)(2,1)S(1)} collective-permute-done((bf16[160,1024]{1,0:T(8,128)(2,1)}, bf16[160,1024]{1,0:T(8,128)(2,1)S(1)}, u32[]{:S(2)}, u32[]{:S(2)}) %collective-permute-start.1) | collective-permute-done | bytes 327712 | tf_op jit(solution)/shard_map/ppermute | solution.py:50
  50.9 3.9 %collective-permute-start.4 = (bf16[16,128,128]{2,1,0:T(8,128)(2,1)S(1)}, bf16[16,128,128]{2,1,0:T(8,128)(2,1)S(1)}, u32[]{:S(2)}, u32[]{:S(2)}) collective-permute-start(bf16[16,128,128]{2,1,0:T(8,128)(2,1)S(1)} %all-to-all-done.kv_ref), channel_id=1, source_target_pairs={{0,16},{16,0},{1,17},{17,1},{2,18},{18,2},{3,19},{19,3},{4,20},{20... | collective-permute-start | bytes 1572872 | tf_op jit(solution)/shard_map/ppermute | solution.py:50
  54.8 1.0 copy-done.2
  56.4 2.4 %attend_own.1 = (f32[4,128,256]{2,1,0:T(8,128)S(1)}, f32[4,8,128]{2,1,0:T(8,128)S(1)}) custom-call(s32[4]{0:T(128)S(1)} %copy-done.5, bf16[160,1024]{1,0:T(8,128)(2,1)S(1)} %copy-done.2, bf16[160,1024]{1,0:T(8,128)(2,1)S(1)} %collective-permute-done.zl_ref.refs_1_, bf16[160,1024]{1,0:T(8,128)(2,1)S(1)} %collective-permute-done.1.ylo_ref.refs_2_, ...), custom_call_target="tpu_custom_call" | custom-call | tf_op jit(solution)/shard_map/attend_own/pallas_call | solution.py:348
  58.9 3.4 %attend_other.1 = bf16[4,528,128]{2,1,0:T(8,128)(2,1)} custom-call(s32[4]{0:T(128)S(1)} %copy-done.5, bf16[160,1024]{1,0:T(8,128)(2,1)S(1)} %copy-done.2, bf16[160,1024]{1,0:T(8,128)(2,1)S(1)} %collective-permute-done.zl_ref.refs_1_, bf16[160,1024]{1,0:T(8,128)(2,1)S(1)} %collective-permute-done.1.ylo_ref.refs_2_, ...), custom_call_target="tpu_custom_call" | custom-call | tf_op jit(solution)/shard_map/attend_other/pallas_call | solution.py:359
  62.2 3.5 %all-to-all-start.1 = ((bf16[4,528,128]{2,1,0:T(8,128)(2,1)}), bf16[4,528,128]{2,1,0:T(8,128)(2,1)S(1)}, u32[]{:S(2)}, u32[]{:S(2)}) async-start(bf16[4,528,128]{2,1,0:T(8,128)(2,1)} %attend_other.1), calls=%async_computation.1 | async-start | bytes 1081344 | tf_op jit(solution)/shard_map/all_to_all | solution.py:54
  65.7 1.9 collective-permute-start.5
  67.7 2.4 %collective-permute-start.6 = (bf16[160,1024]{1,0:T(8,128)(2,1)S(1)}, bf16[160,1024]{1,0:T(8,128)(2,1)S(1)}, u32[]{:S(2)}, u32[]{:S(2)}) collective-permute-start(bf16[160,1024]{1,0:T(8,128)(2,1)S(1)} %collective-permute-done.1.ylo_ref.refs_2_), channel_id=1, source_target_pairs={{0,16},{16,0},{1,17},{17,1},{2,18},{18,2},{3,19},{19,3},{4,20},{20... | collective-permute-start | bytes 983048 | tf_op jit(solution)/shard_map/ppermute | solution.py:50
  70.1 1.9 collective-permute-start.7
  73.6 1.9 all-to-all-done.1.came_ref
  75.5 2.0 project.1
  77.5 6.8 %all-to-all-start.2 = ((bf16[4,32,2048]{2,1,0:T(8,128)(2,1)}), bf16[4,32,2048]{2,1,0:T(8,128)(2,1)S(1)}, u32[]{:S(2)}, u32[]{:S(2)}) async-start(bf16[4,32,2048]{2,1,0:T(8,128)(2,1)} %bitcast.9), calls=%async_computation.2 | async-start | bytes 1048576 | tf_op jit(solution)/shard_map/all_to_all | solution.py:54
  90.2 6.1 %all-to-all-done.2 = bf16[4,32,2048]{2,1,0:T(8,128)(2,1)S(1)} async-done(((bf16[4,32,2048]{2,1,0:T(8,128)(2,1)}), bf16[4,32,2048]{2,1,0:T(8,128)(2,1)S(1)}, u32[]{:S(2)}, u32[]{:S(2)}) %all-to-all-start.2) | async-done | bytes 524320 | tf_op jit(solution)/shard_map/all_to_all | solution.py:54
  96.4 1.1 broadcast_in_dim.46
  97.5 8.5 %all-to-all-start.3 = ((bf16[8,32,2048]{2,1,0:T(8,128)(2,1)}), bf16[8,32,2048]{2,1,0:T(8,128)(2,1)S(1)}, u32[]{:S(2)}, u32[]{:S(2)}) async-start(bf16[8,32,2048]{2,1,0:T(8,128)(2,1)} %broadcast_in_dim.46), calls=%async_computation.3 | async-start | bytes 2097152 | tf_op jit(solution)/shard_map/all_to_all | solution.py:54
  106.2 29.1 %all-to-all-done.3 = bf16[8,32,2048]{2,1,0:T(8,128)(2,1)S(1)} async-done(((bf16[8,32,2048]{2,1,0:T(8,128)(2,1)}), bf16[8,32,2048]{2,1,0:T(8,128)(2,1)S(1)}, u32[]{:S(2)}, u32[]{:S(2)}) %all-to-all-start.3) | async-done | bytes 1048608 | tf_op jit(solution)/shard_map/all_to_all | solution.py:54
  135.3 2.2 %copy-done.1 = bf16[4096,512]{1,0:T(8,128)(2,1)S(1)} copy-done((bf16[4096,512]{1,0:T(8,128)(2,1)S(1)}, bf16[4096,512]{1,0:T(8,128)(2,1)}, u32[]{:S(2)}) %copy-start.1) | copy-done | bytes 4194328
  137.5 1.9 mix.1
  139.4 1.9 collective-permute-start.8
  141.4 8.6 %collective-permute-done.8 = bf16[256,640]{1,0:T(8,128)(2,1)S(1)} collective-permute-done((bf16[256,640]{1,0:T(8,128)(2,1)S(1)}, bf16[256,640]{1,0:T(8,128)(2,1)S(1)}, u32[]{:S(2)}, u32[]{:S(2)}) %collective-permute-start.8) | collective-permute-done | bytes 327712 | tf_op jit(solution)/shard_map/ppermute | solution.py:50
  152.8 7.7 %all-to-all-start.4 = ((bf16[32,32,128]{2,1,0:T(8,128)(2,1)}), bf16[32,32,128]{2,1,0:T(8,128)(2,1)S(1)}, u32[]{:S(2)}, u32[]{:S(2)}) async-start(bf16[32,32,128]{2,1,0:T(8,128)(2,1)} %maximum_maximum_fusion), calls=%async_computation.4 | async-start | bytes 524288 | tf_op jit(solution)/shard_map/all_to_all | solution.py:54
  161.3 12.3 %all-to-all-done.4.came_ref = bf16[32,32,128]{2,1,0:T(8,128)(2,1)S(1)} async-done(((bf16[32,32,128]{2,1,0:T(8,128)(2,1)}), bf16[32,32,128]{2,1,0:T(8,128)(2,1)S(1)}, u32[]{:S(2)}, u32[]{:S(2)}) %all-to-all-start.4) | async-done | bytes 262176 | tf_op jit(solution)/shard_map/all_to_all | solution.py:54
  174.2 1.7 scan.1
  176.0 4.6 %all-to-all-start.5 = ((bf16[32,16,128]{2,1,0:T(8,128)(2,1)}), bf16[32,16,128]{2,1,0:T(8,128)(2,1)S(1)}, u32[]{:S(2)}, u32[]{:S(2)}) async-start(bf16[32,16,128]{2,1,0:T(8,128)(2,1)} %scan.1), calls=%async_computation.5 | async-start | bytes 262144 | tf_op jit(solution)/shard_map/all_to_all | solution.py:54
  181.8 9.4 %all-to-all-done.5 = bf16[32,16,128]{2,1,0:T(8,128)(2,1)S(1)} async-done(((bf16[32,16,128]{2,1,0:T(8,128)(2,1)}), bf16[32,16,128]{2,1,0:T(8,128)(2,1)S(1)}, u32[]{:S(2)}, u32[]{:S(2)}) %all-to-all-start.5) | async-done | bytes 131104 | tf_op jit(solution)/shard_map/all_to_all | solution.py:54
  (104 shorter events, 18.1 us)
Async XLA Ops:
  7.2 28.6 %copy-start = (bf16[128,4,256]{2,1,0:T(4,128)(2,1)S(1)}, bf16[128,4,256]{2,1,0:T(4,128)(2,1)}, u32[]{:S(2)}) copy-start(bf16[128,4,256]{2,1,0:T(4,128)(2,1)} %param.19) | copy-start | bytes 786436
  7.2 28.8 %copy-start.11 = (bf16[128,4]{0,1:T(4,128)(2,1)S(1)}, bf16[128,4]{0,1:T(4,128)(2,1)}, u32[]{:S(2)}) copy-start(bf16[128,4]{0,1:T(4,128)(2,1)} %param.20) | copy-start | bytes 3076
  7.2 28.9 %copy-start.9 = (bf16[128,256]{1,0:T(8,128)(2,1)S(1)}, bf16[128,256]{1,0:T(8,128)(2,1)}, u32[]{:S(2)}) copy-start(bf16[128,256]{1,0:T(8,128)(2,1)} %param.18) | copy-start | bytes 196612
  10.2 40.6 %all-to-all-start = ((bf16[16,128,128]{2,1,0:T(8,128)(2,1)}), bf16[16,128,128]{2,1,0:T(8,128)(2,1)S(1)}, u32[]{:S(2)}, u32[]{:S(2)}) async-start(bf16[16,128,128]{2,1,0:T(8,128)(2,1)} %broadcast_in_dim.24), calls=%async_computation | async-start | bytes 1048576 | tf_op jit(solution)/shard_map/all_to_all | solution.py:54
  23.6 111.7 %all-gather.2.cloned.1.call-start = ((), (), s32[]{:S(2)}) async-start(), calls=%async_computation.6 | async-start | bytes 4325376 | tf_op jit(solution)/shard_map/all_gather | solution.py:345
  27.4 23.4 %collective-permute-start = (bf16[160,1024]{1,0:T(8,128)(2,1)}, bf16[160,1024]{1,0:T(8,128)(2,1)S(1)}, u32[]{:S(2)}, u32[]{:S(2)}) collective-permute-start(bf16[160,1024]{1,0:T(8,128)(2,1)} %get-tuple-element.15), channel_id=1, source_target_pairs={{0,1},{1,0},{2,3},{3,2},{4,5},{5,4},{6,7},{7,6},{8,9},{9,8},{10,11... | collective-permute-start | bytes 983048 | tf_op jit(solution)/shard_map/ppermute | solution.py:50
  30.5 20.3 %collective-permute-start.2 = (bf16[160,1024]{1,0:T(8,128)(2,1)}, bf16[160,1024]{1,0:T(8,128)(2,1)S(1)}, u32[]{:S(2)}, u32[]{:S(2)}) collective-permute-start(bf16[160,1024]{1,0:T(8,128)(2,1)} %get-tuple-element.15), channel_id=1, source_target_pairs={{0,3},{1,2},{2,1},{3,0},{4,7},{5,6},{6,5},{7,4},{8,11},{9,10},{10,... | collective-permute-start | bytes 983048 | tf_op jit(solution)/shard_map/ppermute | solution.py:341
  33.7 17.1 %collective-permute-start.1 = (bf16[160,1024]{1,0:T(8,128)(2,1)}, bf16[160,1024]{1,0:T(8,128)(2,1)S(1)}, u32[]{:S(2)}, u32[]{:S(2)}) collective-permute-start(bf16[160,1024]{1,0:T(8,128)(2,1)} %get-tuple-element.14.home_ref.refs_0_), channel_id=1, source_target_pairs={{0,2},{2,0},{1,3},{3,1},{4,6},{6,4},{5,7},{7,5},{8,10},{10,8},{9,1... | collective-permute-start | bytes 983048 | tf_op jit(solution)/shard_map/ppermute | solution.py:50
  36.2 0.7 collective-permute-start.3
  36.8 14.0 %copy-start.8 = (bf16[128,512]{1,0:T(8,128)(2,1)}, bf16[128,512]{1,0:T(8,128)(2,1)S(1)}, u32[]{:S(2)}) copy-start(bf16[128,512]{1,0:T(8,128)(2,1)S(1)} %collective-permute-done.3) | copy-start | bytes 393220
  50.9 8.0 %collective-permute-start.4 = (bf16[16,128,128]{2,1,0:T(8,128)(2,1)S(1)}, bf16[16,128,128]{2,1,0:T(8,128)(2,1)S(1)}, u32[]{:S(2)}, u32[]{:S(2)}) collective-permute-start(bf16[16,128,128]{2,1,0:T(8,128)(2,1)S(1)} %all-to-all-done.kv_ref), channel_id=1, source_target_pairs={{0,16},{16,0},{1,17},{17,1},{2,18},{18,2},{3,19},{19,3},{4,20},{20... | collective-permute-start | bytes 1572872 | tf_op jit(solution)/shard_map/ppermute | solution.py:50
  54.8 1.0 copy-start.2
  55.7 0.7 copy-start.5
  58.8 16.7 %copy-start.3 = (bf16[160,1024]{1,0:T(8,128)(2,1)S(1)}, bf16[160,1024]{1,0:T(8,128)(2,1)}, u32[]{:S(2)}) copy-start(bf16[160,1024]{1,0:T(8,128)(2,1)} %get-tuple-element.14.home_ref.refs_0_) | copy-start | bytes 983044
  58.9 16.7 %copy-start.4 = (bf16[128,1024]{1,0:T(8,128)(2,1)S(1)}, bf16[128,1024]{1,0:T(8,128)(2,1)}, u32[]{:S(2)}) copy-start(bf16[128,1024]{1,0:T(8,128)(2,1)} %get-tuple-element.22.refs_4_) | copy-start | bytes 786436
  58.9 16.7 %copy-start.6 = (s32[4]{0:T(128)S(1)}, s32[4]{0:T(128)}, u32[]{:S(2)}) copy-start(s32[4]{0:T(128)} %pad_add_fusion.spots) | copy-start | bytes 52
  62.2 13.3 %all-to-all-start.1 = ((bf16[4,528,128]{2,1,0:T(8,128)(2,1)}), bf16[4,528,128]{2,1,0:T(8,128)(2,1)S(1)}, u32[]{:S(2)}, u32[]{:S(2)}) async-start(bf16[4,528,128]{2,1,0:T(8,128)(2,1)} %attend_other.1), calls=%async_computation.1 | async-start | bytes 1081344 | tf_op jit(solution)/shard_map/all_to_all | solution.py:54
  65.7 7.2 %collective-permute-start.5 = (bf16[160,1024]{1,0:T(8,128)(2,1)S(1)}, bf16[160,1024]{1,0:T(8,128)(2,1)S(1)}, u32[]{:S(2)}, u32[]{:S(2)}) collective-permute-start(bf16[160,1024]{1,0:T(8,128)(2,1)S(1)} %collective-permute-done.zl_ref.refs_1_), channel_id=1, source_target_pairs={{0,16},{16,0},{1,17},{17,1},{2,18},{18,2},{3,19},{19,3},{4,20},{20... | collective-permute-start | bytes 983048 | tf_op jit(solution)/shard_map/ppermute | solution.py:50
  67.7 5.2 %collective-permute-start.6 = (bf16[160,1024]{1,0:T(8,128)(2,1)S(1)}, bf16[160,1024]{1,0:T(8,128)(2,1)S(1)}, u32[]{:S(2)}, u32[]{:S(2)}) collective-permute-start(bf16[160,1024]{1,0:T(8,128)(2,1)S(1)} %collective-permute-done.1.ylo_ref.refs_2_), channel_id=1, source_target_pairs={{0,16},{16,0},{1,17},{17,1},{2,18},{18,2},{3,19},{19,3},{4,20},{20... | collective-permute-start | bytes 983048 | tf_op jit(solution)/shard_map/ppermute | solution.py:50
  70.1 3.5 %collective-permute-start.7 = (bf16[160,1024]{1,0:T(8,128)(2,1)S(1)}, bf16[160,1024]{1,0:T(8,128)(2,1)S(1)}, u32[]{:S(2)}, u32[]{:S(2)}) collective-permute-start(bf16[160,1024]{1,0:T(8,128)(2,1)S(1)} %collective-permute-done.2.both_ref.refs_3_), channel_id=1, source_target_pairs={{0,16},{16,0},{1,17},{17,1},{2,18},{18,2},{3,19},{19,3},{4,20},{20... | collective-permute-start | bytes 983048 | tf_op jit(solution)/shard_map/ppermute | solution.py:50
  77.5 18.7 %all-to-all-start.2 = ((bf16[4,32,2048]{2,1,0:T(8,128)(2,1)}), bf16[4,32,2048]{2,1,0:T(8,128)(2,1)S(1)}, u32[]{:S(2)}, u32[]{:S(2)}) async-start(bf16[4,32,2048]{2,1,0:T(8,128)(2,1)} %bitcast.9), calls=%async_computation.2 | async-start | bytes 1048576 | tf_op jit(solution)/shard_map/all_to_all | solution.py:54
  96.3 9.7 %copy-start.10 = (f32[4096]{0:T(1024)S(1)}, f32[4096]{0:T(1024)}, u32[]{:S(2)}) copy-start(f32[4096]{0:T(1024)} %param.17) | copy-start | bytes 49156
  97.5 37.8 %all-to-all-start.3 = ((bf16[8,32,2048]{2,1,0:T(8,128)(2,1)}), bf16[8,32,2048]{2,1,0:T(8,128)(2,1)S(1)}, u32[]{:S(2)}, u32[]{:S(2)}) async-start(bf16[8,32,2048]{2,1,0:T(8,128)(2,1)} %broadcast_in_dim.46), calls=%async_computation.3 | async-start | bytes 2097152 | tf_op jit(solution)/shard_map/all_to_all | solution.py:54
  135.3 2.2 %copy-start.1 = (bf16[4096,512]{1,0:T(8,128)(2,1)S(1)}, bf16[4096,512]{1,0:T(8,128)(2,1)}, u32[]{:S(2)}) copy-start(bf16[4096,512]{1,0:T(8,128)(2,1)} %all-gather.2.cloned.1.call-done) | copy-start | bytes 12582916
  137.5 3.9 %copy-start.13 = (f32[4]{0:T(128)S(1)}, f32[4]{0:T(128)}, u32[]{:S(2)}) copy-start(f32[4]{0:T(128)} %param.22) | copy-start | bytes 52
  139.4 11.5 %copy-start.12 = (f32[4]{0:T(128)S(1)}, f32[4]{0:T(128)}, u32[]{:S(2)}) copy-start(f32[4]{0:T(128)} %param.21) | copy-start | bytes 52
  139.4 10.7 %collective-permute-start.8 = (bf16[256,640]{1,0:T(8,128)(2,1)S(1)}, bf16[256,640]{1,0:T(8,128)(2,1)S(1)}, u32[]{:S(2)}, u32[]{:S(2)}) collective-permute-start(bf16[256,640]{1,0:T(8,128)(2,1)S(1)} %get-tuple-element.25), channel_id=1, source_target_pairs={{0,1},{1,0},{2,3},{3,2},{4,5},{5,4},{6,7},{7,6},{8,9},{9,8},{10,11... | collective-permute-start | bytes 983048 | tf_op jit(solution)/shard_map/ppermute | solution.py:50
  152.8 20.7 %all-to-all-start.4 = ((bf16[32,32,128]{2,1,0:T(8,128)(2,1)}), bf16[32,32,128]{2,1,0:T(8,128)(2,1)S(1)}, u32[]{:S(2)}, u32[]{:S(2)}) async-start(bf16[32,32,128]{2,1,0:T(8,128)(2,1)} %maximum_maximum_fusion), calls=%async_computation.4 | async-start | bytes 524288 | tf_op jit(solution)/shard_map/all_to_all | solution.py:54
  173.5 0.7 copy-start.7
  176.0 15.5 %copy-start.14 = (f32[4]{0:T(128)S(1)}, f32[4]{0:T(128)}, u32[]{:S(2)}) copy-start(f32[4]{0:T(128)} %param.23) | copy-start | bytes 52
  176.0 15.3 %all-to-all-start.5 = ((bf16[32,16,128]{2,1,0:T(8,128)(2,1)}), bf16[32,16,128]{2,1,0:T(8,128)(2,1)S(1)}, u32[]{:S(2)}, u32[]{:S(2)}) async-start(bf16[32,16,128]{2,1,0:T(8,128)(2,1)} %scan.1), calls=%async_computation.5 | async-start | bytes 262144 | tf_op jit(solution)/shard_map/all_to_all | solution.py:54
Sparse Core Ops, SparseCore 0:
  51.0 69.0 all-gather.1

commit v7 on v6

--- a/solution.py
+++ b/solution.py
@@ -115,7 +115,9 @@
         q_ref = (home_ref, zl_ref, ylo_ref, both_ref)[head]
         query = jnp.concatenate(
             [
-                q_ref[128:, 128 * i : 128 * (i + 1)]
+                q_ref[32 * i : 32 * (i + 1)]
+                if head == 3
+                else q_ref[128:, 128 * i : 128 * (i + 1)]
                 for i in (0, 2, 1, 3, 4, 6, 5, 7)
             ]
         )
@@ -338,12 +340,12 @@
     near = [
         swap(away, "zl"),
         swap(home, "ylo"),
-        lax.ppermute(away, ("ylo", "zl"), [(0, 3), (1, 2), (2, 1), (3, 0)]),
+        lax.ppermute(queries, ("ylo", "zl"), [(0, 3), (1, 2), (2, 1), (3, 0)]),
     ]
     both, near, packed = lax.optimization_barrier((both, near, packed))
     both_co = swap(both, "co")
     weights = lax.all_gather(packed, CTX, axis=0, tiled=True).reshape(8, 2, 256, 512)
-    near_co = [swap(part, "co") for part in near]
+    passed = swap(near[0], "ylo")
 
     so_far = pl.pallas_call(
         functools.partial(attend, True),
@@ -364,6 +366,9 @@
         compiler_params=pltpu.CompilerParams(vmem_limit_bytes=32 << 20),
         name="attend_other",
     )(spots, home, *near, both_co, *so_far)
+    sent, passed = lax.optimization_barrier((sent, passed))
+    rows = [near[0], near[1], passed]
+    rows_co = [swap(part, "co") for part in rows]
     came = exchange(sent.reshape(4 * 528, 128), ("ylo", "zl")).reshape(4, 528, 128)
     head_part = pl.pallas_call(
         project,
@@ -373,7 +378,7 @@
         scratch_shapes=[pltpu.VMEM((4, 128, 128), BF)],
         compiler_params=pltpu.CompilerParams(vmem_limit_bytes=32 << 20),
         name="project",
-    )(spots, came, home, *near, rest, *near_co)
+    )(spots, came, home, *rows, rest, *rows_co)
 
     parts = exchange(head_part, "yhi").reshape(4, 32, 2048)
     attention_sum = jnp.sum(parts.astype(F32), axis=0)

time: 201 us -> 201 us (level)
  waiting for transfers between devices: 82 us -> 71 us
  starting transfers between devices: 65.7 us -> 76.1 us
    ppermute x7 -> x8, waiting for transfers between devices: 23.3 us -> 11.8 us  [swap(): return lax.ppermute(value, axis, [(0, 1), (1, 0)])]
    ppermute x7 -> x8, starting transfers between devices: 17.2 us -> 22.5 us  [swap(): return lax.ppermute(value, axis, [(0, 1), (1, 0)])]
    all_to_all x6, starting transfers between devices: 44.6 us -> 47.3 us  [exchange(): return lax.all_to_all(value, axes, split_axis=0, concat_axis=0, tiled=True)]
    ppermute x1, starting transfers between devices: 3.19 us -> 5.58 us  [body(): lax.ppermute(queries, ('ylo', 'zl'), [(0, 3), (1, 2), (2, 1), (3, 0)])]
    unnamed x50 -> x52, local copies, waits for them, and re-layouts: 13.7 us -> 13.7 us
  transfers between devices with their start and end apart: 16 -> 17, of which waited for: 8 -> 10; matrix products, arithmetic and copies ran while one was open for 6% -> 6% of each run, Pallas kernels for 5% -> 5%
where the time goes in v7:
time: 201 us; the launch traced here: 199 us
  starting transfers between devices  76.1 us (38%)
  waiting for transfers between devices  71 us (35%)
  local copies, waits for them, and re-layouts  18.9 us (9%)
  between operations  14.6 us (7%)
  Pallas kernels  14.5 us (7%)
  other arithmetic  2.43 us (1%)
    all_to_all x6, waiting for transfers between devices, exchange(): return lax.all_to_all(value, axes, split_axis=0, concat_axis=0, tiled=True)  57.4 us
    all_to_all x6, starting transfers between devices, exchange(): return lax.all_to_all(value, axes, split_axis=0, concat_axis=0, tiled=True)  47.3 us
    ppermute x8, starting transfers between devices, swap(): return lax.ppermute(value, axis, [(0, 1), (1, 0)])  22.5 us
    unnamed x52, local copies, waits for them, and re-layouts  13.7 us
    ppermute x8, waiting for transfers between devices, swap(): return lax.ppermute(value, axis, [(0, 1), (1, 0)])  11.8 us
    ppermute x1, starting transfers between devices, body(): lax.ppermute(queries, ('ylo', 'zl'), [(0, 3), (1, 2), (2, 1), (3, 0)])  5.58 us
  transfers between devices with their start and end apart: 17, of which 10 were waited for; matrix products, arithmetic and copies ran while one was open for 6% of the time, Pallas kernels for 5%

profile of v7, /device:TPU:1, one launch (start us, length us, event | category | flops | bytes accessed | tf_op | source)
XLA Modules:
  0.0 199.0 jit_solution(7678012176942146125)
XLA Ops:
  7.2 1.0 copy.50
  10.2 13.4 %all-to-all-start = ((bf16[16,128,128]{2,1,0:T(8,128)(2,1)}), bf16[16,128,128]{2,1,0:T(8,128)(2,1)S(1)}, u32[]{:S(2)}, u32[]{:S(2)}) async-start(bf16[16,128,128]{2,1,0:T(8,128)(2,1)} %broadcast_in_dim.24), calls=%async_computation | async-start | bytes 1048576 | tf_op jit(solution)/shard_map/all_to_all | solution.py:54
  24.3 3.1 %pick.1 = (bf16[160,1024]{1,0:T(8,128)(2,1)}, bf16[160,1024]{1,0:T(8,128)(2,1)}, bf16[128,1024]{1,0:T(8,128)(2,1)}) custom-call(s32[4]{0:T(128)} %pad_add_fusion.spots, bf16[256,128]{1,0:T(8,128)(2,1)} %q_ref.1, bf16[128,4096]{1,0:T(8,128)(2,1)} %w_hbm.1), custom_call_target="tpu_custom_call" | custom-call | tf_op jit(solution)/shard_map/pick/pallas_call | solution.py:319
  27.4 3.2 %collective-permute-start.1 = (bf16[160,1024]{1,0:T(8,128)(2,1)}, bf16[160,1024]{1,0:T(8,128)(2,1)S(1)}, u32[]{:S(2)}, u32[]{:S(2)}) collective-permute-start(bf16[160,1024]{1,0:T(8,128)(2,1)} %get-tuple-element.16.home_ref.refs_0_), channel_id=1, source_target_pairs={{0,2},{2,0},{1,3},{3,1},{4,6},{6,4},{5,7},{7,5},{8,10},{10,8},{9,1... | collective-permute-start | bytes 983048 | tf_op jit(solution)/shard_map/ppermute | solution.py:50
  30.6 3.1 %collective-permute-start = (bf16[160,1024]{1,0:T(8,128)(2,1)}, bf16[160,1024]{1,0:T(8,128)(2,1)S(1)}, u32[]{:S(2)}, u32[]{:S(2)}) collective-permute-start(bf16[160,1024]{1,0:T(8,128)(2,1)} %get-tuple-element.17), channel_id=1, source_target_pairs={{0,1},{1,0},{2,3},{3,2},{4,5},{5,4},{6,7},{7,6},{8,9},{9,8},{10,11... | collective-permute-start | bytes 983048 | tf_op jit(solution)/shard_map/ppermute | solution.py:50
  34.8 5.6 %collective-permute-start.2 = (bf16[256,128]{1,0:T(8,128)(2,1)S(1)}, bf16[256,128]{1,0:T(8,128)(2,1)S(1)}, u32[]{:S(2)}, u32[]{:S(2)}) collective-permute-start(bf16[256,128]{1,0:T(8,128)(2,1)S(1)} %copy-done.9), channel_id=1, source_target_pairs={{0,3},{1,2},{2,1},{3,0},{4,7},{5,6},{6,5},{7,4},{8,11},{9,10},{10,... | collective-permute-start | bytes 196616 | tf_op jit(solution)/shard_map/ppermute | solution.py:343
  40.3 1.7 collective-permute-done.2.both_ref
  42.1 2.7 %collective-permute-done.zl_ref.refs_1_ = bf16[160,1024]{1,0:T(8,128)(2,1)S(1)} collective-permute-done((bf16[160,1024]{1,0:T(8,128)(2,1)}, bf16[160,1024]{1,0:T(8,128)(2,1)S(1)}, u32[]{:S(2)}, u32[]{:S(2)}) %collective-permute-start) | collective-permute-done | bytes 327712 | tf_op jit(solution)/shard_map/ppermute | solution.py:50
  44.8 3.4 %collective-permute-start.4 = (bf16[16,128,128]{2,1,0:T(8,128)(2,1)S(1)}, bf16[16,128,128]{2,1,0:T(8,128)(2,1)S(1)}, u32[]{:S(2)}, u32[]{:S(2)}) collective-permute-start(bf16[16,128,128]{2,1,0:T(8,128)(2,1)S(1)} %all-to-all-done.kv_ref), channel_id=1, source_target_pairs={{0,16},{16,0},{1,17},{17,1},{2,18},{18,2},{3,19},{19,3},{4,20},{20... | collective-permute-start | bytes 1572872 | tf_op jit(solution)/shard_map/ppermute | solution.py:50
  48.3 3.2 %collective-permute-start.5 = (bf16[160,1024]{1,0:T(8,128)(2,1)S(1)}, bf16[160,1024]{1,0:T(8,128)(2,1)S(1)}, u32[]{:S(2)}, u32[]{:S(2)}) collective-permute-start(bf16[160,1024]{1,0:T(8,128)(2,1)S(1)} %collective-permute-done.zl_ref.refs_1_), channel_id=1, source_target_pairs={{0,2},{2,0},{1,3},{3,1},{4,6},{6,4},{5,7},{7,5},{8,10},{10,8},{9,1... | collective-permute-start | bytes 983048 | tf_op jit(solution)/shard_map/ppermute | solution.py:50
  53.0 2.4 %attend_own.1 = (f32[4,128,256]{2,1,0:T(8,128)S(1)}, f32[4,8,128]{2,1,0:T(8,128)S(1)}) custom-call(s32[4]{0:T(128)S(1)} %copy-done.5, bf16[160,1024]{1,0:T(8,128)(2,1)S(1)} %copy-done.2, bf16[160,1024]{1,0:T(8,128)(2,1)S(1)} %collective-permute-done.zl_ref.refs_1_, bf16[160,1024]{1,0:T(8,128)(2,1)S(1)} %collective-permute-done.1.ylo_ref.refs_2_, ...), custom_call_target="tpu_custom_call" | custom-call | tf_op jit(solution)/shard_map/attend_own/pallas_call | solution.py:350
  55.5 3.4 %attend_other.1 = bf16[4,528,128]{2,1,0:T(8,128)(2,1)} custom-call(s32[4]{0:T(128)S(1)} %copy-done.5, bf16[160,1024]{1,0:T(8,128)(2,1)S(1)} %copy-done.2, bf16[160,1024]{1,0:T(8,128)(2,1)S(1)} %collective-permute-done.zl_ref.refs_1_, bf16[160,1024]{1,0:T(8,128)(2,1)S(1)} %collective-permute-done.1.ylo_ref.refs_2_, ...), custom_call_target="tpu_custom_call" | custom-call | tf_op jit(solution)/shard_map/attend_other/pallas_call | solution.py:361
  59.5 3.5 %all-to-all-start.1 = ((bf16[4,528,128]{2,1,0:T(8,128)(2,1)}), bf16[4,528,128]{2,1,0:T(8,128)(2,1)S(1)}, u32[]{:S(2)}, u32[]{:S(2)}) async-start(bf16[4,528,128]{2,1,0:T(8,128)(2,1)} %attend_other.1), calls=%async_computation.1 | async-start | bytes 1081344 | tf_op jit(solution)/shard_map/all_to_all | solution.py:54
  63.0 2.9 %collective-permute-start.6 = (bf16[160,1024]{1,0:T(8,128)(2,1)S(1)}, bf16[160,1024]{1,0:T(8,128)(2,1)S(1)}, u32[]{:S(2)}, u32[]{:S(2)}) collective-permute-start(bf16[160,1024]{1,0:T(8,128)(2,1)S(1)} %collective-permute-done.zl_ref.refs_1_), channel_id=1, source_target_pairs={{0,16},{16,0},{1,17},{17,1},{2,18},{18,2},{3,19},{19,3},{4,20},{20... | collective-permute-start | bytes 983048 | tf_op jit(solution)/shard_map/ppermute | solution.py:50
  65.9 1.9 collective-permute-start.7
  67.8 2.4 %collective-permute-start.8 = (bf16[160,1024]{1,0:T(8,128)(2,1)S(1)}, bf16[160,1024]{1,0:T(8,128)(2,1)S(1)}, u32[]{:S(2)}, u32[]{:S(2)}) collective-permute-start(bf16[160,1024]{1,0:T(8,128)(2,1)S(1)} %collective-permute-done.5.refs_3_), channel_id=1, source_target_pairs={{0,16},{16,0},{1,17},{17,1},{2,18},{18,2},{3,19},{19,3},{4,20},{20... | collective-permute-start | bytes 983048 | tf_op jit(solution)/shard_map/ppermute | solution.py:50
  71.4 2.0 all-to-all-done.1.came_ref
  73.4 2.0 project.1
  75.4 5.2 %all-to-all-start.2 = ((bf16[4,32,2048]{2,1,0:T(8,128)(2,1)}), bf16[4,32,2048]{2,1,0:T(8,128)(2,1)S(1)}, u32[]{:S(2)}, u32[]{:S(2)}) async-start(bf16[4,32,2048]{2,1,0:T(8,128)(2,1)} %bitcast.9), calls=%async_computation.2 | async-start | bytes 1048576 | tf_op jit(solution)/shard_map/all_to_all | solution.py:54
  86.4 4.2 %all-to-all-done.2 = bf16[4,32,2048]{2,1,0:T(8,128)(2,1)S(1)} async-done(((bf16[4,32,2048]{2,1,0:T(8,128)(2,1)}), bf16[4,32,2048]{2,1,0:T(8,128)(2,1)S(1)}, u32[]{:S(2)}, u32[]{:S(2)}) %all-to-all-start.2) | async-done | bytes 524320 | tf_op jit(solution)/shard_map/all_to_all | solution.py:54
  90.7 1.1 broadcast_in_dim.46
  91.9 10.4 %all-to-all-start.3 = ((bf16[8,32,2048]{2,1,0:T(8,128)(2,1)}), bf16[8,32,2048]{2,1,0:T(8,128)(2,1)S(1)}, u32[]{:S(2)}, u32[]{:S(2)}) async-start(bf16[8,32,2048]{2,1,0:T(8,128)(2,1)} %broadcast_in_dim.46), calls=%async_computation.3 | async-start | bytes 2097152 | tf_op jit(solution)/shard_map/all_to_all | solution.py:54
  102.4 29.1 %all-to-all-done.3 = bf16[8,32,2048]{2,1,0:T(8,128)(2,1)S(1)} async-done(((bf16[8,32,2048]{2,1,0:T(8,128)(2,1)}), bf16[8,32,2048]{2,1,0:T(8,128)(2,1)S(1)}, u32[]{:S(2)}, u32[]{:S(2)}) %all-to-all-start.3) | async-done | bytes 1048608 | tf_op jit(solution)/shard_map/all_to_all | solution.py:54
  131.5 2.2 %copy-done.1 = bf16[4096,512]{1,0:T(8,128)(2,1)S(1)} copy-done((bf16[4096,512]{1,0:T(8,128)(2,1)S(1)}, bf16[4096,512]{1,0:T(8,128)(2,1)}, u32[]{:S(2)}) %copy-start.1) | copy-done | bytes 4194328
  133.7 1.9 mix.1
  135.6 2.4 %collective-permute-start.9 = (bf16[256,640]{1,0:T(8,128)(2,1)S(1)}, bf16[256,640]{1,0:T(8,128)(2,1)S(1)}, u32[]{:S(2)}, u32[]{:S(2)}) collective-permute-start(bf16[256,640]{1,0:T(8,128)(2,1)S(1)} %get-tuple-element.29), channel_id=1, source_target_pairs={{0,1},{1,0},{2,3},{3,2},{4,5},{5,4},{6,7},{7,6},{8,9},{9,8},{10,11... | collective-permute-start | bytes 983048 | tf_op jit(solution)/shard_map/ppermute | solution.py:50
  138.1 8.2 %collective-permute-done.9 = bf16[256,640]{1,0:T(8,128)(2,1)S(1)} collective-permute-done((bf16[256,640]{1,0:T(8,128)(2,1)S(1)}, bf16[256,640]{1,0:T(8,128)(2,1)S(1)}, u32[]{:S(2)}, u32[]{:S(2)}) %collective-permute-start.9) | collective-permute-done | bytes 327712 | tf_op jit(solution)/shard_map/ppermute | solution.py:50
  149.1 10.8 %all-to-all-start.4 = ((bf16[32,32,128]{2,1,0:T(8,128)(2,1)}), bf16[32,32,128]{2,1,0:T(8,128)(2,1)S(1)}, u32[]{:S(2)}, u32[]{:S(2)}) async-start(bf16[32,32,128]{2,1,0:T(8,128)(2,1)} %maximum_maximum_fusion), calls=%async_computation.4 | async-start | bytes 524288 | tf_op jit(solution)/shard_map/all_to_all | solution.py:54
  160.6 12.6 %all-to-all-done.4.came_ref = bf16[32,32,128]{2,1,0:T(8,128)(2,1)S(1)} async-done(((bf16[32,32,128]{2,1,0:T(8,128)(2,1)}), bf16[32,32,128]{2,1,0:T(8,128)(2,1)S(1)}, u32[]{:S(2)}, u32[]{:S(2)}) %all-to-all-start.4) | async-done | bytes 262176 | tf_op jit(solution)/shard_map/all_to_all | solution.py:54
  173.9 1.7 scan.1
  175.7 4.1 %all-to-all-start.5 = ((bf16[32,16,128]{2,1,0:T(8,128)(2,1)}), bf16[32,16,128]{2,1,0:T(8,128)(2,1)S(1)}, u32[]{:S(2)}, u32[]{:S(2)}) async-start(bf16[32,16,128]{2,1,0:T(8,128)(2,1)} %scan.1), calls=%async_computation.5 | async-start | bytes 262144 | tf_op jit(solution)/shard_map/all_to_all | solution.py:54
  181.0 9.5 %all-to-all-done.5 = bf16[32,16,128]{2,1,0:T(8,128)(2,1)S(1)} async-done(((bf16[32,16,128]{2,1,0:T(8,128)(2,1)}), bf16[32,16,128]{2,1,0:T(8,128)(2,1)S(1)}, u32[]{:S(2)}, u32[]{:S(2)}) %all-to-all-start.5) | async-done | bytes 131104 | tf_op jit(solution)/shard_map/all_to_all | solution.py:54
  (108 shorter events, 20.2 us)
Async XLA Ops:
  7.2 26.6 %copy-start = (bf16[128,4,256]{2,1,0:T(4,128)(2,1)S(1)}, bf16[128,4,256]{2,1,0:T(4,128)(2,1)}, u32[]{:S(2)}) copy-start(bf16[128,4,256]{2,1,0:T(4,128)(2,1)} %param.19) | copy-start | bytes 786436
  7.2 26.7 %copy-start.12 = (bf16[128,4]{0,1:T(4,128)(2,1)S(1)}, bf16[128,4]{0,1:T(4,128)(2,1)}, u32[]{:S(2)}) copy-start(bf16[128,4]{0,1:T(4,128)(2,1)} %param.20) | copy-start | bytes 3076
  7.2 26.9 %copy-start.10 = (bf16[128,256]{1,0:T(8,128)(2,1)S(1)}, bf16[128,256]{1,0:T(8,128)(2,1)}, u32[]{:S(2)}) copy-start(bf16[128,256]{1,0:T(8,128)(2,1)} %param.18) | copy-start | bytes 196612
  8.2 26.5 %copy-start.9 = (bf16[256,128]{1,0:T(8,128)(2,1)S(1)}, bf16[256,128]{1,0:T(8,128)(2,1)}, u32[]{:S(2)}) copy-start(bf16[256,128]{1,0:T(8,128)(2,1)} %q_ref.1) | copy-start | bytes 196612
  10.2 34.6 %all-to-all-start = ((bf16[16,128,128]{2,1,0:T(8,128)(2,1)}), bf16[16,128,128]{2,1,0:T(8,128)(2,1)S(1)}, u32[]{:S(2)}, u32[]{:S(2)}) async-start(bf16[16,128,128]{2,1,0:T(8,128)(2,1)} %broadcast_in_dim.24), calls=%async_computation | async-start | bytes 1048576 | tf_op jit(solution)/shard_map/all_to_all | solution.py:54
  23.6 107.8 %all-gather.2.cloned.1.call-start = ((), (), s32[]{:S(2)}) async-start(), calls=%async_computation.6 | async-start | bytes 4325376 | tf_op jit(solution)/shard_map/all_gather | solution.py:347
  27.4 14.7 %collective-permute-start.1 = (bf16[160,1024]{1,0:T(8,128)(2,1)}, bf16[160,1024]{1,0:T(8,128)(2,1)S(1)}, u32[]{:S(2)}, u32[]{:S(2)}) collective-permute-start(bf16[160,1024]{1,0:T(8,128)(2,1)} %get-tuple-element.16.home_ref.refs_0_), channel_id=1, source_target_pairs={{0,2},{2,0},{1,3},{3,1},{4,6},{6,4},{5,7},{7,5},{8,10},{10,8},{9,1... | collective-permute-start | bytes 983048 | tf_op jit(solution)/shard_map/ppermute | solution.py:50
  30.6 14.2 %collective-permute-start = (bf16[160,1024]{1,0:T(8,128)(2,1)}, bf16[160,1024]{1,0:T(8,128)(2,1)S(1)}, u32[]{:S(2)}, u32[]{:S(2)}) collective-permute-start(bf16[160,1024]{1,0:T(8,128)(2,1)} %get-tuple-element.17), channel_id=1, source_target_pairs={{0,1},{1,0},{2,3},{3,2},{4,5},{5,4},{6,7},{7,6},{8,9},{9,8},{10,11... | collective-permute-start | bytes 983048 | tf_op jit(solution)/shard_map/ppermute | solution.py:50
  34.1 8.0 %collective-permute-start.3 = (bf16[128,512]{1,0:T(8,128)(2,1)S(1)}, bf16[128,512]{1,0:T(8,128)(2,1)S(1)}, u32[]{:S(2)}, u32[]{:S(2)}) collective-permute-start(bf16[128,512]{1,0:T(8,128)(2,1)S(1)} %fusion.24), channel_id=1, source_target_pairs={{0,0},{1,32},{32,1},{33,33},{2,2},{3,34},{34,3},{35,35},{4,4},{5,3... | collective-permute-start | bytes 393224 | tf_op jit(solution)/shard_map/ppermute | solution.py:316
  34.8 7.3 %collective-permute-start.2 = (bf16[256,128]{1,0:T(8,128)(2,1)S(1)}, bf16[256,128]{1,0:T(8,128)(2,1)S(1)}, u32[]{:S(2)}, u32[]{:S(2)}) collective-permute-start(bf16[256,128]{1,0:T(8,128)(2,1)S(1)} %copy-done.9), channel_id=1, source_target_pairs={{0,3},{1,2},{2,1},{3,0},{4,7},{5,6},{6,5},{7,4},{8,11},{9,10},{10,... | collective-permute-start | bytes 196616 | tf_op jit(solution)/shard_map/ppermute | solution.py:343
  42.1 2.7 %copy-start.8 = (bf16[128,512]{1,0:T(8,128)(2,1)}, bf16[128,512]{1,0:T(8,128)(2,1)S(1)}, u32[]{:S(2)}) copy-start(bf16[128,512]{1,0:T(8,128)(2,1)S(1)} %collective-permute-done.3) | copy-start | bytes 393220
  44.8 10.7 %collective-permute-start.4 = (bf16[16,128,128]{2,1,0:T(8,128)(2,1)S(1)}, bf16[16,128,128]{2,1,0:T(8,128)(2,1)S(1)}, u32[]{:S(2)}, u32[]{:S(2)}) collective-permute-start(bf16[16,128,128]{2,1,0:T(8,128)(2,1)S(1)} %all-to-all-done.kv_ref), channel_id=1, source_target_pairs={{0,16},{16,0},{1,17},{17,1},{2,18},{18,2},{3,19},{19,3},{4,20},{20... | collective-permute-start | bytes 1572872 | tf_op jit(solution)/shard_map/ppermute | solution.py:50
  48.3 11.2 %collective-permute-start.5 = (bf16[160,1024]{1,0:T(8,128)(2,1)S(1)}, bf16[160,1024]{1,0:T(8,128)(2,1)S(1)}, u32[]{:S(2)}, u32[]{:S(2)}) collective-permute-start(bf16[160,1024]{1,0:T(8,128)(2,1)S(1)} %collective-permute-done.zl_ref.refs_1_), channel_id=1, source_target_pairs={{0,2},{2,0},{1,3},{3,1},{4,6},{6,4},{5,7},{7,5},{8,10},{10,8},{9,1... | collective-permute-start | bytes 983048 | tf_op jit(solution)/shard_map/ppermute | solution.py:50
  51.5 1.0 copy-start.2
  55.5 17.9 %copy-start.3 = (bf16[160,1024]{1,0:T(8,128)(2,1)S(1)}, bf16[160,1024]{1,0:T(8,128)(2,1)}, u32[]{:S(2)}) copy-start(bf16[160,1024]{1,0:T(8,128)(2,1)} %get-tuple-element.16.home_ref.refs_0_) | copy-start | bytes 983044
  55.5 17.9 %copy-start.4 = (bf16[128,1024]{1,0:T(8,128)(2,1)S(1)}, bf16[128,1024]{1,0:T(8,128)(2,1)}, u32[]{:S(2)}) copy-start(bf16[128,1024]{1,0:T(8,128)(2,1)} %get-tuple-element.26.refs_4_) | copy-start | bytes 786436
  55.5 17.9 %copy-start.6 = (s32[4]{0:T(128)S(1)}, s32[4]{0:T(128)}, u32[]{:S(2)}) copy-start(s32[4]{0:T(128)} %pad_add_fusion.spots) | copy-start | bytes 52
  59.5 13.9 %all-to-all-start.1 = ((bf16[4,528,128]{2,1,0:T(8,128)(2,1)}), bf16[4,528,128]{2,1,0:T(8,128)(2,1)S(1)}, u32[]{:S(2)}, u32[]{:S(2)}) async-start(bf16[4,528,128]{2,1,0:T(8,128)(2,1)} %attend_other.1), calls=%async_computation.1 | async-start | bytes 1081344 | tf_op jit(solution)/shard_map/all_to_all | solution.py:54
  63.0 8.1 %collective-permute-start.6 = (bf16[160,1024]{1,0:T(8,128)(2,1)S(1)}, bf16[160,1024]{1,0:T(8,128)(2,1)S(1)}, u32[]{:S(2)}, u32[]{:S(2)}) collective-permute-start(bf16[160,1024]{1,0:T(8,128)(2,1)S(1)} %collective-permute-done.zl_ref.refs_1_), channel_id=1, source_target_pairs={{0,16},{16,0},{1,17},{17,1},{2,18},{18,2},{3,19},{19,3},{4,20},{20... | collective-permute-start | bytes 983048 | tf_op jit(solution)/shard_map/ppermute | solution.py:50
  65.9 5.2 %collective-permute-start.7 = (bf16[160,1024]{1,0:T(8,128)(2,1)S(1)}, bf16[160,1024]{1,0:T(8,128)(2,1)S(1)}, u32[]{:S(2)}, u32[]{:S(2)}) collective-permute-start(bf16[160,1024]{1,0:T(8,128)(2,1)S(1)} %collective-permute-done.1.ylo_ref.refs_2_), channel_id=1, source_target_pairs={{0,16},{16,0},{1,17},{17,1},{2,18},{18,2},{3,19},{19,3},{4,20},{20... | collective-permute-start | bytes 983048 | tf_op jit(solution)/shard_map/ppermute | solution.py:50
  67.8 3.6 %collective-permute-start.8 = (bf16[160,1024]{1,0:T(8,128)(2,1)S(1)}, bf16[160,1024]{1,0:T(8,128)(2,1)S(1)}, u32[]{:S(2)}, u32[]{:S(2)}) collective-permute-start(bf16[160,1024]{1,0:T(8,128)(2,1)S(1)} %collective-permute-done.5.refs_3_), channel_id=1, source_target_pairs={{0,16},{16,0},{1,17},{17,1},{2,18},{18,2},{3,19},{19,3},{4,20},{20... | collective-permute-start | bytes 983048 | tf_op jit(solution)/shard_map/ppermute | solution.py:50
  75.4 15.2 %all-to-all-start.2 = ((bf16[4,32,2048]{2,1,0:T(8,128)(2,1)}), bf16[4,32,2048]{2,1,0:T(8,128)(2,1)S(1)}, u32[]{:S(2)}, u32[]{:S(2)}) async-start(bf16[4,32,2048]{2,1,0:T(8,128)(2,1)} %bitcast.9), calls=%async_computation.2 | async-start | bytes 1048576 | tf_op jit(solution)/shard_map/all_to_all | solution.py:54
  90.7 11.6 %copy-start.11 = (f32[4096]{0:T(1024)S(1)}, f32[4096]{0:T(1024)}, u32[]{:S(2)}) copy-start(f32[4096]{0:T(1024)} %param.17) | copy-start | bytes 49156
  91.9 39.6 %all-to-all-start.3 = ((bf16[8,32,2048]{2,1,0:T(8,128)(2,1)}), bf16[8,32,2048]{2,1,0:T(8,128)(2,1)S(1)}, u32[]{:S(2)}, u32[]{:S(2)}) async-start(bf16[8,32,2048]{2,1,0:T(8,128)(2,1)} %broadcast_in_dim.46), calls=%async_computation.3 | async-start | bytes 2097152 | tf_op jit(solution)/shard_map/all_to_all | solution.py:54
  131.5 2.2 %copy-start.1 = (bf16[4096,512]{1,0:T(8,128)(2,1)S(1)}, bf16[4096,512]{1,0:T(8,128)(2,1)}, u32[]{:S(2)}) copy-start(bf16[4096,512]{1,0:T(8,128)(2,1)} %all-gather.2.cloned.1.call-done) | copy-start | bytes 12582916
  133.7 4.4 %copy-start.14 = (f32[4]{0:T(128)S(1)}, f32[4]{0:T(128)}, u32[]{:S(2)}) copy-start(f32[4]{0:T(128)} %param.22) | copy-start | bytes 52
  135.6 11.5 %copy-start.13 = (f32[4]{0:T(128)S(1)}, f32[4]{0:T(128)}, u32[]{:S(2)}) copy-start(f32[4]{0:T(128)} %param.21) | copy-start | bytes 52
  135.6 10.7 %collective-permute-start.9 = (bf16[256,640]{1,0:T(8,128)(2,1)S(1)}, bf16[256,640]{1,0:T(8,128)(2,1)S(1)}, u32[]{:S(2)}, u32[]{:S(2)}) collective-permute-start(bf16[256,640]{1,0:T(8,128)(2,1)S(1)} %get-tuple-element.29), channel_id=1, source_target_pairs={{0,1},{1,0},{2,3},{3,2},{4,5},{5,4},{6,7},{7,6},{8,9},{9,8},{10,11... | collective-permute-start | bytes 983048 | tf_op jit(solution)/shard_map/ppermute | solution.py:50
  149.1 24.1 %all-to-all-start.4 = ((bf16[32,32,128]{2,1,0:T(8,128)(2,1)}), bf16[32,32,128]{2,1,0:T(8,128)(2,1)S(1)}, u32[]{:S(2)}, u32[]{:S(2)}) async-start(bf16[32,32,128]{2,1,0:T(8,128)(2,1)} %maximum_maximum_fusion), calls=%async_computation.4 | async-start | bytes 524288 | tf_op jit(solution)/shard_map/all_to_all | solution.py:54
  173.2 0.7 copy-start.7
  175.7 15.0 %copy-start.15 = (f32[4]{0:T(128)S(1)}, f32[4]{0:T(128)}, u32[]{:S(2)}) copy-start(f32[4]{0:T(128)} %param.23) | copy-start | bytes 52
  175.7 14.8 %all-to-all-start.5 = ((bf16[32,16,128]{2,1,0:T(8,128)(2,1)}), bf16[32,16,128]{2,1,0:T(8,128)(2,1)S(1)}, u32[]{:S(2)}, u32[]{:S(2)}) async-start(bf16[32,16,128]{2,1,0:T(8,128)(2,1)} %scan.1), calls=%async_computation.5 | async-start | bytes 262144 | tf_op jit(solution)/shard_map/all_to_all | solution.py:54
  (1 other events, 0.6 us)
Sparse Core Ops, SparseCore 0:
  44.9 71.4 all-gather.1

commit v8 on v7

--- a/solution.py
+++ b/solution.py
@@ -370,6 +370,7 @@
     rows = [near[0], near[1], passed]
     rows_co = [swap(part, "co") for part in rows]
     came = exchange(sent.reshape(4 * 528, 128), ("ylo", "zl")).reshape(4, 528, 128)
+    came, late_y = lax.optimization_barrier((came, y))
     head_part = pl.pallas_call(
         project,
         out_shape=jax.ShapeDtypeStruct((128, 2048), BF),
@@ -382,7 +383,7 @@
 
     parts = exchange(head_part, "yhi").reshape(4, 32, 2048)
     attention_sum = jnp.sum(parts.astype(F32), axis=0)
-    hidden_mine = features(lax.dynamic_slice(hidden, (32 * y, 0), (32, 4096)), zl)
+    hidden_mine = features(lax.dynamic_slice(hidden, (32 * late_y, 0), (32, 4096)), zl)
     residual = (hidden_mine.astype(F32) + attention_sum).astype(BF)
     spread = jnp.broadcast_to(residual[None], (8, 32, 2048)).reshape(256, 2048)
     residual = exchange(spread, Y)

time: 201 us -> 201 us (level)
  transfers between devices with their start and end apart: 17 -> 17, of which waited for: 10 -> 9; matrix products, arithmetic and copies ran while one was open for 6% -> 6% of each run, Pallas kernels for 5% -> 5%
where the time goes in v8:
time: 201 us; the launch traced here: 199 us
  starting transfers between devices  76.1 us (38%)
  waiting for transfers between devices  71 us (35%)
  local copies, waits for them, and re-layouts  18.9 us (9%)
  between operations  14.6 us (7%)
  Pallas kernels  14.5 us (7%)
  other arithmetic  2.43 us (1%)
    all_to_all x6, waiting for transfers between devices, exchange(): return lax.all_to_all(value, axes, split_axis=0, concat_axis=0, tiled=True)  57.7 us
    all_to_all x6, starting transfers between devices, exchange(): return lax.all_to_all(value, axes, split_axis=0, concat_axis=0, tiled=True)  47.3 us
    ppermute x8, starting transfers between devices, swap(): return lax.ppermute(value, axis, [(0, 1), (1, 0)])  22.6 us
    unnamed x52, local copies, waits for them, and re-layouts  13.7 us
    ppermute x8, waiting for transfers between devices, swap(): return lax.ppermute(value, axis, [(0, 1), (1, 0)])  11.5 us
    ppermute x1, starting transfers between devices, body(): lax.ppermute(queries, ('ylo', 'zl'), [(0, 3), (1, 2), (2, 1), (3, 0)])  5.58 us
  transfers between devices with their start and end apart: 17, of which 9 were waited for; matrix products, arithmetic and copies ran while one was open for 6% of the time, Pallas kernels for 5%

profile of v8, /device:TPU:1, one launch (start us, length us, event | category | flops | bytes accessed | tf_op | source)
XLA Modules:
  0.0 199.1 jit_solution(12431499091462824239)
XLA Ops:
  7.2 1.0 copy.50
  10.2 13.4 %all-to-all-start = ((bf16[16,128,128]{2,1,0:T(8,128)(2,1)}), bf16[16,128,128]{2,1,0:T(8,128)(2,1)S(1)}, u32[]{:S(2)}, u32[]{:S(2)}) async-start(bf16[16,128,128]{2,1,0:T(8,128)(2,1)} %broadcast_in_dim.24), calls=%async_computation | async-start | bytes 1048576 | tf_op jit(solution)/shard_map/all_to_all | solution.py:54
  24.3 3.1 %pick.1 = (bf16[160,1024]{1,0:T(8,128)(2,1)}, bf16[160,1024]{1,0:T(8,128)(2,1)}, bf16[128,1024]{1,0:T(8,128)(2,1)}) custom-call(s32[4]{0:T(128)} %pad_add_fusion.spots, bf16[256,128]{1,0:T(8,128)(2,1)} %q_ref.1, bf16[128,4096]{1,0:T(8,128)(2,1)} %w_hbm.1), custom_call_target="tpu_custom_call" | custom-call | tf_op jit(solution)/shard_map/pick/pallas_call | solution.py:319
  27.4 3.2 %collective-permute-start.1 = (bf16[160,1024]{1,0:T(8,128)(2,1)}, bf16[160,1024]{1,0:T(8,128)(2,1)S(1)}, u32[]{:S(2)}, u32[]{:S(2)}) collective-permute-start(bf16[160,1024]{1,0:T(8,128)(2,1)} %get-tuple-element.18.home_ref.refs_0_), channel_id=1, source_target_pairs={{0,2},{2,0},{1,3},{3,1},{4,6},{6,4},{5,7},{7,5},{8,10},{10,8},{9,1... | collective-permute-start | bytes 983048 | tf_op jit(solution)/shard_map/ppermute | solution.py:50
  30.6 3.1 %collective-permute-start = (bf16[160,1024]{1,0:T(8,128)(2,1)}, bf16[160,1024]{1,0:T(8,128)(2,1)S(1)}, u32[]{:S(2)}, u32[]{:S(2)}) collective-permute-start(bf16[160,1024]{1,0:T(8,128)(2,1)} %get-tuple-element.19), channel_id=1, source_target_pairs={{0,1},{1,0},{2,3},{3,2},{4,5},{5,4},{6,7},{7,6},{8,9},{9,8},{10,11... | collective-permute-start | bytes 983048 | tf_op jit(solution)/shard_map/ppermute | solution.py:50
  34.8 5.6 %collective-permute-start.2 = (bf16[256,128]{1,0:T(8,128)(2,1)S(1)}, bf16[256,128]{1,0:T(8,128)(2,1)S(1)}, u32[]{:S(2)}, u32[]{:S(2)}) collective-permute-start(bf16[256,128]{1,0:T(8,128)(2,1)S(1)} %copy-done.9), channel_id=1, source_target_pairs={{0,3},{1,2},{2,1},{3,0},{4,7},{5,6},{6,5},{7,4},{8,11},{9,10},{10,... | collective-permute-start | bytes 196616 | tf_op jit(solution)/shard_map/ppermute | solution.py:343
  40.3 1.7 collective-permute-done.2.both_ref
  42.1 2.7 %collective-permute-done.zl_ref.refs_1_ = bf16[160,1024]{1,0:T(8,128)(2,1)S(1)} collective-permute-done((bf16[160,1024]{1,0:T(8,128)(2,1)}, bf16[160,1024]{1,0:T(8,128)(2,1)S(1)}, u32[]{:S(2)}, u32[]{:S(2)}) %collective-permute-start) | collective-permute-done | bytes 327712 | tf_op jit(solution)/shard_map/ppermute | solution.py:50
  44.8 3.4 %collective-permute-start.4 = (bf16[16,128,128]{2,1,0:T(8,128)(2,1)S(1)}, bf16[16,128,128]{2,1,0:T(8,128)(2,1)S(1)}, u32[]{:S(2)}, u32[]{:S(2)}) collective-permute-start(bf16[16,128,128]{2,1,0:T(8,128)(2,1)S(1)} %all-to-all-done.kv_ref), channel_id=1, source_target_pairs={{0,16},{16,0},{1,17},{17,1},{2,18},{18,2},{3,19},{19,3},{4,20},{20... | collective-permute-start | bytes 1572872 | tf_op jit(solution)/shard_map/ppermute | solution.py:50
  48.3 3.2 %collective-permute-start.5 = (bf16[160,1024]{1,0:T(8,128)(2,1)S(1)}, bf16[160,1024]{1,0:T(8,128)(2,1)S(1)}, u32[]{:S(2)}, u32[]{:S(2)}) collective-permute-start(bf16[160,1024]{1,0:T(8,128)(2,1)S(1)} %collective-permute-done.zl_ref.refs_1_), channel_id=1, source_target_pairs={{0,2},{2,0},{1,3},{3,1},{4,6},{6,4},{5,7},{7,5},{8,10},{10,8},{9,1... | collective-permute-start | bytes 983048 | tf_op jit(solution)/shard_map/ppermute | solution.py:50
  53.0 2.4 %attend_own.1 = (f32[4,128,256]{2,1,0:T(8,128)S(1)}, f32[4,8,128]{2,1,0:T(8,128)S(1)}) custom-call(s32[4]{0:T(128)S(1)} %copy-done.5, bf16[160,1024]{1,0:T(8,128)(2,1)S(1)} %copy-done.2, bf16[160,1024]{1,0:T(8,128)(2,1)S(1)} %collective-permute-done.zl_ref.refs_1_, bf16[160,1024]{1,0:T(8,128)(2,1)S(1)} %collective-permute-done.1.ylo_ref.refs_2_, ...), custom_call_target="tpu_custom_call" | custom-call | tf_op jit(solution)/shard_map/attend_own/pallas_call | solution.py:350
  55.5 3.4 %attend_other.1 = bf16[4,528,128]{2,1,0:T(8,128)(2,1)} custom-call(s32[4]{0:T(128)S(1)} %copy-done.5, bf16[160,1024]{1,0:T(8,128)(2,1)S(1)} %copy-done.2, bf16[160,1024]{1,0:T(8,128)(2,1)S(1)} %collective-permute-done.zl_ref.refs_1_, bf16[160,1024]{1,0:T(8,128)(2,1)S(1)} %collective-permute-done.1.ylo_ref.refs_2_, ...), custom_call_target="tpu_custom_call" | custom-call | tf_op jit(solution)/shard_map/attend_other/pallas_call | solution.py:361
  59.5 3.5 %all-to-all-start.1 = ((bf16[4,528,128]{2,1,0:T(8,128)(2,1)}), bf16[4,528,128]{2,1,0:T(8,128)(2,1)S(1)}, u32[]{:S(2)}, u32[]{:S(2)}) async-start(bf16[4,528,128]{2,1,0:T(8,128)(2,1)} %attend_other.1), calls=%async_computation.1 | async-start | bytes 1081344 | tf_op jit(solution)/shard_map/all_to_all | solution.py:54
  63.0 2.9 %collective-permute-start.6 = (bf16[160,1024]{1,0:T(8,128)(2,1)S(1)}, bf16[160,1024]{1,0:T(8,128)(2,1)S(1)}, u32[]{:S(2)}, u32[]{:S(2)}) collective-permute-start(bf16[160,1024]{1,0:T(8,128)(2,1)S(1)} %collective-permute-done.zl_ref.refs_1_), channel_id=1, source_target_pairs={{0,16},{16,0},{1,17},{17,1},{2,18},{18,2},{3,19},{19,3},{4,20},{20... | collective-permute-start | bytes 983048 | tf_op jit(solution)/shard_map/ppermute | solution.py:50
  65.9 1.9 collective-permute-start.7
  67.8 2.4 %collective-permute-start.8 = (bf16[160,1024]{1,0:T(8,128)(2,1)S(1)}, bf16[160,1024]{1,0:T(8,128)(2,1)S(1)}, u32[]{:S(2)}, u32[]{:S(2)}) collective-permute-start(bf16[160,1024]{1,0:T(8,128)(2,1)S(1)} %collective-permute-done.5.refs_3_), channel_id=1, source_target_pairs={{0,16},{16,0},{1,17},{17,1},{2,18},{18,2},{3,19},{19,3},{4,20},{20... | collective-permute-start | bytes 983048 | tf_op jit(solution)/shard_map/ppermute | solution.py:50
  70.2 3.2 %all-to-all-done.1.came_ref = bf16[4,528,128]{2,1,0:T(8,128)(2,1)S(1)} async-done(((bf16[4,528,128]{2,1,0:T(8,128)(2,1)}), bf16[4,528,128]{2,1,0:T(8,128)(2,1)S(1)}, u32[]{:S(2)}, u32[]{:S(2)}) %all-to-all-start.1) | async-done | bytes 540704 | tf_op jit(solution)/shard_map/all_to_all | solution.py:54
  73.4 2.0 project.1
  75.4 5.2 %all-to-all-start.2 = ((bf16[4,32,2048]{2,1,0:T(8,128)(2,1)}), bf16[4,32,2048]{2,1,0:T(8,128)(2,1)S(1)}, u32[]{:S(2)}, u32[]{:S(2)}) async-start(bf16[4,32,2048]{2,1,0:T(8,128)(2,1)} %bitcast.9), calls=%async_computation.2 | async-start | bytes 1048576 | tf_op jit(solution)/shard_map/all_to_all | solution.py:54
  87.3 3.4 %all-to-all-done.2 = bf16[4,32,2048]{2,1,0:T(8,128)(2,1)S(1)} async-done(((bf16[4,32,2048]{2,1,0:T(8,128)(2,1)}), bf16[4,32,2048]{2,1,0:T(8,128)(2,1)S(1)}, u32[]{:S(2)}, u32[]{:S(2)}) %all-to-all-start.2) | async-done | bytes 524320 | tf_op jit(solution)/shard_map/all_to_all | solution.py:54
  90.8 1.1 broadcast_in_dim.46
  91.9 10.4 %all-to-all-start.3 = ((bf16[8,32,2048]{2,1,0:T(8,128)(2,1)}), bf16[8,32,2048]{2,1,0:T(8,128)(2,1)S(1)}, u32[]{:S(2)}, u32[]{:S(2)}) async-start(bf16[8,32,2048]{2,1,0:T(8,128)(2,1)} %broadcast_in_dim.46), calls=%async_computation.3 | async-start | bytes 2097152 | tf_op jit(solution)/shard_map/all_to_all | solution.py:54
  102.4 29.1 %all-to-all-done.3 = bf16[8,32,2048]{2,1,0:T(8,128)(2,1)S(1)} async-done(((bf16[8,32,2048]{2,1,0:T(8,128)(2,1)}), bf16[8,32,2048]{2,1,0:T(8,128)(2,1)S(1)}, u32[]{:S(2)}, u32[]{:S(2)}) %all-to-all-start.3) | async-done | bytes 1048608 | tf_op jit(solution)/shard_map/all_to_all | solution.py:54
  131.5 2.2 %copy-done.1 = bf16[4096,512]{1,0:T(8,128)(2,1)S(1)} copy-done((bf16[4096,512]{1,0:T(8,128)(2,1)S(1)}, bf16[4096,512]{1,0:T(8,128)(2,1)}, u32[]{:S(2)}) %copy-start.1) | copy-done | bytes 4194328
  133.7 1.9 mix.1
  135.6 2.4 %collective-permute-start.9 = (bf16[256,640]{1,0:T(8,128)(2,1)S(1)}, bf16[256,640]{1,0:T(8,128)(2,1)S(1)}, u32[]{:S(2)}, u32[]{:S(2)}) collective-permute-start(bf16[256,640]{1,0:T(8,128)(2,1)S(1)} %get-tuple-element.33), channel_id=1, source_target_pairs={{0,1},{1,0},{2,3},{3,2},{4,5},{5,4},{6,7},{7,6},{8,9},{9,8},{10,11... | collective-permute-start | bytes 983048 | tf_op jit(solution)/shard_map/ppermute | solution.py:50
  138.2 8.1 %collective-permute-done.9 = bf16[256,640]{1,0:T(8,128)(2,1)S(1)} collective-permute-done((bf16[256,640]{1,0:T(8,128)(2,1)S(1)}, bf16[256,640]{1,0:T(8,128)(2,1)S(1)}, u32[]{:S(2)}, u32[]{:S(2)}) %collective-permute-start.9) | collective-permute-done | bytes 327712 | tf_op jit(solution)/shard_map/ppermute | solution.py:50
  149.1 10.8 %all-to-all-start.4 = ((bf16[32,32,128]{2,1,0:T(8,128)(2,1)}), bf16[32,32,128]{2,1,0:T(8,128)(2,1)S(1)}, u32[]{:S(2)}, u32[]{:S(2)}) async-start(bf16[32,32,128]{2,1,0:T(8,128)(2,1)} %maximum_maximum_fusion), calls=%async_computation.4 | async-start | bytes 524288 | tf_op jit(solution)/shard_map/all_to_all | solution.py:54
  160.6 12.6 %all-to-all-done.4.came_ref = bf16[32,32,128]{2,1,0:T(8,128)(2,1)S(1)} async-done(((bf16[32,32,128]{2,1,0:T(8,128)(2,1)}), bf16[32,32,128]{2,1,0:T(8,128)(2,1)S(1)}, u32[]{:S(2)}, u32[]{:S(2)}) %all-to-all-start.4) | async-done | bytes 262176 | tf_op jit(solution)/shard_map/all_to_all | solution.py:54
  173.9 1.7 scan.1
  175.7 4.1 %all-to-all-start.5 = ((bf16[32,16,128]{2,1,0:T(8,128)(2,1)}), bf16[32,16,128]{2,1,0:T(8,128)(2,1)S(1)}, u32[]{:S(2)}, u32[]{:S(2)}) async-start(bf16[32,16,128]{2,1,0:T(8,128)(2,1)} %scan.1), calls=%async_computation.5 | async-start | bytes 262144 | tf_op jit(solution)/shard_map/all_to_all | solution.py:54
  181.0 9.5 %all-to-all-done.5 = bf16[32,16,128]{2,1,0:T(8,128)(2,1)S(1)} async-done(((bf16[32,16,128]{2,1,0:T(8,128)(2,1)}), bf16[32,16,128]{2,1,0:T(8,128)(2,1)S(1)}, u32[]{:S(2)}, u32[]{:S(2)}) %all-to-all-start.5) | async-done | bytes 131104 | tf_op jit(solution)/shard_map/all_to_all | solution.py:54
  (108 shorter events, 19.8 us)
Async XLA Ops:
  7.2 26.6 %copy-start = (bf16[128,4,256]{2,1,0:T(4,128)(2,1)S(1)}, bf16[128,4,256]{2,1,0:T(4,128)(2,1)}, u32[]{:S(2)}) copy-start(bf16[128,4,256]{2,1,0:T(4,128)(2,1)} %param.19) | copy-start | bytes 786436
  7.2 26.7 %copy-start.12 = (bf16[128,4]{0,1:T(4,128)(2,1)S(1)}, bf16[128,4]{0,1:T(4,128)(2,1)}, u32[]{:S(2)}) copy-start(bf16[128,4]{0,1:T(4,128)(2,1)} %param.20) | copy-start | bytes 3076
  7.2 26.9 %copy-start.10 = (bf16[128,256]{1,0:T(8,128)(2,1)S(1)}, bf16[128,256]{1,0:T(8,128)(2,1)}, u32[]{:S(2)}) copy-start(bf16[128,256]{1,0:T(8,128)(2,1)} %param.18) | copy-start | bytes 196612
  8.2 26.5 %copy-start.9 = (bf16[256,128]{1,0:T(8,128)(2,1)S(1)}, bf16[256,128]{1,0:T(8,128)(2,1)}, u32[]{:S(2)}) copy-start(bf16[256,128]{1,0:T(8,128)(2,1)} %q_ref.1) | copy-start | bytes 196612
  10.2 34.6 %all-to-all-start = ((bf16[16,128,128]{2,1,0:T(8,128)(2,1)}), bf16[16,128,128]{2,1,0:T(8,128)(2,1)S(1)}, u32[]{:S(2)}, u32[]{:S(2)}) async-start(bf16[16,128,128]{2,1,0:T(8,128)(2,1)} %broadcast_in_dim.24), calls=%async_computation | async-start | bytes 1048576 | tf_op jit(solution)/shard_map/all_to_all | solution.py:54
  23.6 107.9 %all-gather.2.cloned.1.call-start = ((), (), s32[]{:S(2)}) async-start(), calls=%async_computation.6 | async-start | bytes 4325376 | tf_op jit(solution)/shard_map/all_gather | solution.py:347
  27.4 14.7 %collective-permute-start.1 = (bf16[160,1024]{1,0:T(8,128)(2,1)}, bf16[160,1024]{1,0:T(8,128)(2,1)S(1)}, u32[]{:S(2)}, u32[]{:S(2)}) collective-permute-start(bf16[160,1024]{1,0:T(8,128)(2,1)} %get-tuple-element.18.home_ref.refs_0_), channel_id=1, source_target_pairs={{0,2},{2,0},{1,3},{3,1},{4,6},{6,4},{5,7},{7,5},{8,10},{10,8},{9,1... | collective-permute-start | bytes 983048 | tf_op jit(solution)/shard_map/ppermute | solution.py:50
  30.6 14.2 %collective-permute-start = (bf16[160,1024]{1,0:T(8,128)(2,1)}, bf16[160,1024]{1,0:T(8,128)(2,1)S(1)}, u32[]{:S(2)}, u32[]{:S(2)}) collective-permute-start(bf16[160,1024]{1,0:T(8,128)(2,1)} %get-tuple-element.19), channel_id=1, source_target_pairs={{0,1},{1,0},{2,3},{3,2},{4,5},{5,4},{6,7},{7,6},{8,9},{9,8},{10,11... | collective-permute-start | bytes 983048 | tf_op jit(solution)/shard_map/ppermute | solution.py:50
  34.1 8.0 %collective-permute-start.3 = (bf16[128,512]{1,0:T(8,128)(2,1)S(1)}, bf16[128,512]{1,0:T(8,128)(2,1)S(1)}, u32[]{:S(2)}, u32[]{:S(2)}) collective-permute-start(bf16[128,512]{1,0:T(8,128)(2,1)S(1)} %fusion.24), channel_id=1, source_target_pairs={{0,0},{1,32},{32,1},{33,33},{2,2},{3,34},{34,3},{35,35},{4,4},{5,3... | collective-permute-start | bytes 393224 | tf_op jit(solution)/shard_map/ppermute | solution.py:316
  34.8 7.3 %collective-permute-start.2 = (bf16[256,128]{1,0:T(8,128)(2,1)S(1)}, bf16[256,128]{1,0:T(8,128)(2,1)S(1)}, u32[]{:S(2)}, u32[]{:S(2)}) collective-permute-start(bf16[256,128]{1,0:T(8,128)(2,1)S(1)} %copy-done.9), channel_id=1, source_target_pairs={{0,3},{1,2},{2,1},{3,0},{4,7},{5,6},{6,5},{7,4},{8,11},{9,10},{10,... | collective-permute-start | bytes 196616 | tf_op jit(solution)/shard_map/ppermute | solution.py:343
  42.1 2.7 %copy-start.8 = (bf16[128,512]{1,0:T(8,128)(2,1)}, bf16[128,512]{1,0:T(8,128)(2,1)S(1)}, u32[]{:S(2)}) copy-start(bf16[128,512]{1,0:T(8,128)(2,1)S(1)} %collective-permute-done.3) | copy-start | bytes 393220
  44.8 10.7 %collective-permute-start.4 = (bf16[16,128,128]{2,1,0:T(8,128)(2,1)S(1)}, bf16[16,128,128]{2,1,0:T(8,128)(2,1)S(1)}, u32[]{:S(2)}, u32[]{:S(2)}) collective-permute-start(bf16[16,128,128]{2,1,0:T(8,128)(2,1)S(1)} %all-to-all-done.kv_ref), channel_id=1, source_target_pairs={{0,16},{16,0},{1,17},{17,1},{2,18},{18,2},{3,19},{19,3},{4,20},{20... | collective-permute-start | bytes 1572872 | tf_op jit(solution)/shard_map/ppermute | solution.py:50
  48.3 11.2 %collective-permute-start.5 = (bf16[160,1024]{1,0:T(8,128)(2,1)S(1)}, bf16[160,1024]{1,0:T(8,128)(2,1)S(1)}, u32[]{:S(2)}, u32[]{:S(2)}) collective-permute-start(bf16[160,1024]{1,0:T(8,128)(2,1)S(1)} %collective-permute-done.zl_ref.refs_1_), channel_id=1, source_target_pairs={{0,2},{2,0},{1,3},{3,1},{4,6},{6,4},{5,7},{7,5},{8,10},{10,8},{9,1... | collective-permute-start | bytes 983048 | tf_op jit(solution)/shard_map/ppermute | solution.py:50
  51.5 1.0 copy-start.2
  55.5 17.9 %copy-start.3 = (bf16[160,1024]{1,0:T(8,128)(2,1)S(1)}, bf16[160,1024]{1,0:T(8,128)(2,1)}, u32[]{:S(2)}) copy-start(bf16[160,1024]{1,0:T(8,128)(2,1)} %get-tuple-element.18.home_ref.refs_0_) | copy-start | bytes 983044
  55.5 17.9 %copy-start.4 = (bf16[128,1024]{1,0:T(8,128)(2,1)S(1)}, bf16[128,1024]{1,0:T(8,128)(2,1)}, u32[]{:S(2)}) copy-start(bf16[128,1024]{1,0:T(8,128)(2,1)} %get-tuple-element.30.refs_4_) | copy-start | bytes 786436
  55.5 17.9 %copy-start.6 = (s32[4]{0:T(128)S(1)}, s32[4]{0:T(128)}, u32[]{:S(2)}) copy-start(s32[4]{0:T(128)} %pad_add_fusion.spots) | copy-start | bytes 52
  59.5 13.9 %all-to-all-start.1 = ((bf16[4,528,128]{2,1,0:T(8,128)(2,1)}), bf16[4,528,128]{2,1,0:T(8,128)(2,1)S(1)}, u32[]{:S(2)}, u32[]{:S(2)}) async-start(bf16[4,528,128]{2,1,0:T(8,128)(2,1)} %attend_other.1), calls=%async_computation.1 | async-start | bytes 1081344 | tf_op jit(solution)/shard_map/all_to_all | solution.py:54
  63.0 10.4 %collective-permute-start.6 = (bf16[160,1024]{1,0:T(8,128)(2,1)S(1)}, bf16[160,1024]{1,0:T(8,128)(2,1)S(1)}, u32[]{:S(2)}, u32[]{:S(2)}) collective-permute-start(bf16[160,1024]{1,0:T(8,128)(2,1)S(1)} %collective-permute-done.zl_ref.refs_1_), channel_id=1, source_target_pairs={{0,16},{16,0},{1,17},{17,1},{2,18},{18,2},{3,19},{19,3},{4,20},{20... | collective-permute-start | bytes 983048 | tf_op jit(solution)/shard_map/ppermute | solution.py:50
  65.9 7.5 %collective-permute-start.7 = (bf16[160,1024]{1,0:T(8,128)(2,1)S(1)}, bf16[160,1024]{1,0:T(8,128)(2,1)S(1)}, u32[]{:S(2)}, u32[]{:S(2)}) collective-permute-start(bf16[160,1024]{1,0:T(8,128)(2,1)S(1)} %collective-permute-done.1.ylo_ref.refs_2_), channel_id=1, source_target_pairs={{0,16},{16,0},{1,17},{17,1},{2,18},{18,2},{3,19},{19,3},{4,20},{20... | collective-permute-start | bytes 983048 | tf_op jit(solution)/shard_map/ppermute | solution.py:50
  67.8 5.6 %collective-permute-start.8 = (bf16[160,1024]{1,0:T(8,128)(2,1)S(1)}, bf16[160,1024]{1,0:T(8,128)(2,1)S(1)}, u32[]{:S(2)}, u32[]{:S(2)}) collective-permute-start(bf16[160,1024]{1,0:T(8,128)(2,1)S(1)} %collective-permute-done.5.refs_3_), channel_id=1, source_target_pairs={{0,16},{16,0},{1,17},{17,1},{2,18},{18,2},{3,19},{19,3},{4,20},{20... | collective-permute-start | bytes 983048 | tf_op jit(solution)/shard_map/ppermute | solution.py:50
  75.4 15.2 %all-to-all-start.2 = ((bf16[4,32,2048]{2,1,0:T(8,128)(2,1)}), bf16[4,32,2048]{2,1,0:T(8,128)(2,1)S(1)}, u32[]{:S(2)}, u32[]{:S(2)}) async-start(bf16[4,32,2048]{2,1,0:T(8,128)(2,1)} %bitcast.9), calls=%async_computation.2 | async-start | bytes 1048576 | tf_op jit(solution)/shard_map/all_to_all | solution.py:54
  90.7 11.5 %copy-start.11 = (f32[4096]{0:T(1024)S(1)}, f32[4096]{0:T(1024)}, u32[]{:S(2)}) copy-start(f32[4096]{0:T(1024)} %param.17) | copy-start | bytes 49156
  91.9 39.6 %all-to-all-start.3 = ((bf16[8,32,2048]{2,1,0:T(8,128)(2,1)}), bf16[8,32,2048]{2,1,0:T(8,128)(2,1)S(1)}, u32[]{:S(2)}, u32[]{:S(2)}) async-start(bf16[8,32,2048]{2,1,0:T(8,128)(2,1)} %broadcast_in_dim.46), calls=%async_computation.3 | async-start | bytes 2097152 | tf_op jit(solution)/shard_map/all_to_all | solution.py:54
  131.5 2.2 %copy-start.1 = (bf16[4096,512]{1,0:T(8,128)(2,1)S(1)}, bf16[4096,512]{1,0:T(8,128)(2,1)}, u32[]{:S(2)}) copy-start(bf16[4096,512]{1,0:T(8,128)(2,1)} %all-gather.2.cloned.1.call-done) | copy-start | bytes 12582916
  133.7 4.5 %copy-start.14 = (f32[4]{0:T(128)S(1)}, f32[4]{0:T(128)}, u32[]{:S(2)}) copy-start(f32[4]{0:T(128)} %param.22) | copy-start | bytes 52
  135.6 11.5 %copy-start.13 = (f32[4]{0:T(128)S(1)}, f32[4]{0:T(128)}, u32[]{:S(2)}) copy-start(f32[4]{0:T(128)} %param.21) | copy-start | bytes 52
  135.6 10.7 %collective-permute-start.9 = (bf16[256,640]{1,0:T(8,128)(2,1)S(1)}, bf16[256,640]{1,0:T(8,128)(2,1)S(1)}, u32[]{:S(2)}, u32[]{:S(2)}) collective-permute-start(bf16[256,640]{1,0:T(8,128)(2,1)S(1)} %get-tuple-element.33), channel_id=1, source_target_pairs={{0,1},{1,0},{2,3},{3,2},{4,5},{5,4},{6,7},{7,6},{8,9},{9,8},{10,11... | collective-permute-start | bytes 983048 | tf_op jit(solution)/shard_map/ppermute | solution.py:50
  149.1 24.1 %all-to-all-start.4 = ((bf16[32,32,128]{2,1,0:T(8,128)(2,1)}), bf16[32,32,128]{2,1,0:T(8,128)(2,1)S(1)}, u32[]{:S(2)}, u32[]{:S(2)}) async-start(bf16[32,32,128]{2,1,0:T(8,128)(2,1)} %maximum_maximum_fusion), calls=%async_computation.4 | async-start | bytes 524288 | tf_op jit(solution)/shard_map/all_to_all | solution.py:54
  173.2 0.7 copy-start.7
  175.7 15.0 %copy-start.15 = (f32[4]{0:T(128)S(1)}, f32[4]{0:T(128)}, u32[]{:S(2)}) copy-start(f32[4]{0:T(128)} %param.23) | copy-start | bytes 52
  175.7 14.8 %all-to-all-start.5 = ((bf16[32,16,128]{2,1,0:T(8,128)(2,1)}), bf16[32,16,128]{2,1,0:T(8,128)(2,1)S(1)}, u32[]{:S(2)}, u32[]{:S(2)}) async-start(bf16[32,16,128]{2,1,0:T(8,128)(2,1)} %scan.1), calls=%async_computation.5 | async-start | bytes 262144 | tf_op jit(solution)/shard_map/all_to_all | solution.py:54
  (1 other events, 0.6 us)
Sparse Core Ops, SparseCore 0:
  44.9 71.4 all-gather.1
